TPU v7x, 32 devices: a whole 2x2x4 slice. The times are simulated.
32 devices in a mesh: groups: 2 (over y), row: 4 (over z), col: 2 (over x), chan: 2 (over core).
Axes of the slice: x: 2, y: 2, z: 4, core: 2. Of those that a mesh axis runs over, the one named last changes fastest.
Arguments:
- layer_input: bfloat16 [2, 64, 32, 512], P(None, None, ('groups', 'col'), 'row'), parts along dimension 2, may hold values from -6 to 6
- features: bfloat16 [2, 64, 32, 512], P(None, 'chan', ('groups', 'col'), 'row'), parts along dimension 2, may hold values from -6 to 6
- vol_target: bfloat16 [8, 40, 32, 512], P('chan', None, ('groups', 'col'), 'row'), parts along dimension 2, may hold values from -6 to 6
- offsets: int32 [4, 4], P('row', ('groups', 'col')), parts along dimension 1, may hold values from 0 to 2, as said below
- w_first: bfloat16 [64, 64, 3, 3], replicated, may hold values from -0.25 to 0.25
- w_second: bfloat16 [64, 64, 3, 3], replicated, may hold values from -0.25 to 0.25
Outputs:
- grad_features: bfloat16 [2, 64, 32, 512], P(None, 'chan', ('groups', 'col'), 'row'), parts along dimension 2
- grad_w_first: float32 [128, 64, 3, 3], P('groups'), parts along dimension 0
- grad_w_second: float32 [128, 64, 3, 3], P('groups'), parts along dimension 0
There are 2 independent parts, one for each index of `groups`. A program takes and returns all parts, laid end to end along the dimension named above; an argument that names none is the same for every part. Nothing has to cross between parts.
Inputs may be any that keep to these rules, and one draw needn't show every extreme that they name: `offsets`: each tile's entry is at most its own tile row index along the epipolar direction; tiles of the first row have 0, and some tile has exactly 2.
All inputs are finite; a program needn't handle non-finite values.
Results may differ from a plain program's by a relative error of at most 0.005.
Values may be sent and summed in bfloat16 or wider, within the bound.
No kernel may reach another device: no remote copies, remote signals or barrier semaphores. Data moves between devices by JAX's collectives and lax.ppermute only.
A program may use at most 64 MiB of HBM per device.

v0:
```python
import math

import jax
import jax.numpy as jnp
from jax import lax
from jax.sharding import PartitionSpec as P

DISP = 40
MAXOFF = 2


def passed_along(block, axis, distance):
    devices = range(lax.axis_size(axis))
    route = [(i - distance, i) for i in devices if i - distance in devices]
    return lax.ppermute(block, axis, route)


def extended(array, sides, width):
    for axis, dim in sides:
        peers, length = (lax.axis_size(axis), array.shape[dim])
        up = [(i, (i + 1) % peers) for i in range(peers - 1)]
        down = [(j, i) for i, j in up]
        last = lax.slice_in_dim(array, length - width, length, axis=dim)
        leading = lax.slice_in_dim(array, 0, width, axis=dim)
        before = lax.ppermute(last, axis, up)
        after = lax.ppermute(leading, axis, down)
        array = jnp.concatenate([before, array, after], axis=dim)
    return array


def recompute_hidden(input_halo, w_first, tile_w, block_rows):
    summed = None
    for a in range(3):
        for b in range(3):
            product = jnp.einsum(
                "oi,nixy->noxy",
                w_first[:, :, a, b],
                input_halo[:, :, a : a + tile_w, b : b + block_rows],
                preferred_element_type=jnp.float32,
            )
            summed = product if summed is None else summed + product
    return jnp.maximum(summed, 0.0).astype(jnp.bfloat16)


def make_hidden(input_halo, w_first, tile_w, block_rows, first_ch, local_ch):
    hidden = recompute_hidden(input_halo, w_first, tile_w, block_rows)
    hidden_own = lax.dynamic_slice_in_dim(hidden, first_ch, local_ch, 1)
    return (hidden, hidden_own)


def correlate(left_feat, window, vol_target, block_rows):
    local_ch = left_feat.shape[0]
    tile_w = left_feat.shape[1]
    local_groups = vol_target.shape[0]
    group_size = local_ch // local_groups
    inv_size = 1.0 / group_size
    left_f32 = left_feat.astype(jnp.float32)

    def one_turn(t, state_now):
        left_grad, window_grad = state_now
        for j in range(8):
            d = t * 8 + j
            first_row = DISP - 1 - d
            window_rows = lax.dynamic_slice_in_dim(window, first_row, block_rows, 2).astype(
                jnp.float32
            )
            volume = (left_f32 * window_rows).reshape(
                local_groups, group_size, tile_w, block_rows
            ).sum(axis=1) * inv_size
            target_plane = lax.dynamic_index_in_dim(vol_target, d, 1, keepdims=False).astype(
                jnp.float32
            )
            weighted = jnp.repeat(volume - target_plane, group_size, axis=0) * inv_size
            left_grad = left_grad + weighted * window_rows
            window_part = (
                lax.dynamic_slice_in_dim(window_grad, first_row, block_rows, 2)
                + weighted * left_f32
            )
            window_grad = lax.dynamic_update_slice_in_dim(window_grad, window_part, first_row, 2)
        return (left_grad, window_grad)

    initial = (
        jnp.zeros((local_ch, tile_w, block_rows), jnp.float32),
        jnp.zeros((local_ch, tile_w, block_rows + DISP - 1), jnp.float32),
    )
    return lax.fori_loop(0, DISP // 8, one_turn, initial)


def body(layer_input, features, vol_target, offsets, w_first, w_second):
    all_channels = layer_input.shape[1]
    tile_w = layer_input.shape[2]
    block_rows = layer_input.shape[3]
    local_ch = features.shape[1]
    offset_here = offsets[0, 0]
    left_feat = features[0]
    right_feat = features[1]
    first_ch = lax.axis_index("chan") * local_ch
    main_rows = right_feat
    spill_rows = jnp.zeros((local_ch, tile_w, DISP - 1), jnp.bfloat16)
    for k in range(1, MAXOFF + 2):
        arrived = passed_along(right_feat, "row", k)
        main_rows = jnp.where(offset_here == k, arrived, main_rows)
        spill_rows = jnp.where(
            offset_here + 1 == k, arrived[:, :, block_rows - DISP + 1 :], spill_rows
        )
    window = jnp.concatenate([spill_rows, main_rows], axis=2)
    left_grad, window_grad = correlate(left_feat, window, vol_target, block_rows)
    main_grad = window_grad[:, :, DISP - 1 :]
    spill_grad = jnp.pad(
        window_grad[:, :, : DISP - 1], ((0, 0), (0, 0), (block_rows - DISP + 1, 0))
    )
    right_grad = jnp.where(offset_here == 0, main_grad, 0.0)
    for k in range(1, MAXOFF + 2):
        outgoing = jnp.where(offset_here == k, main_grad, 0.0) + jnp.where(
            offset_here + 1 == k, spill_grad, 0.0
        )
        right_grad = right_grad + passed_along(outgoing, "row", -k)
    grad_features = jnp.stack([left_grad, right_grad]).astype(jnp.bfloat16)
    grad_maps = lax.all_gather(grad_features, "chan", axis=1, tiled=True)
    joined = extended(
        jnp.concatenate([layer_input, grad_maps], axis=1), (("row", 3), ("col", 2)), 1
    )
    input_halo = joined[:, :all_channels]
    grad_halo = joined[:, all_channels:]
    hidden, hidden_here = make_hidden(input_halo, w_first, tile_w, block_rows, first_ch, local_ch)
    own_halo = lax.dynamic_slice_in_dim(grad_halo, first_ch, local_ch, 1)
    second_pieces = []
    for a in range(3):
        for b in range(3):
            view = own_halo[:, :, 2 - a : 2 - a + tile_w, 2 - b : 2 - b + block_rows]
            second_pieces.append(
                jnp.einsum("noxy,nixy->oi", view, hidden, preferred_element_type=jnp.float32)
            )
    second_local = jnp.stack(second_pieces, axis=-1).reshape(local_ch, all_channels, 3, 3)
    w2_cols = lax.dynamic_slice_in_dim(w_second, first_ch, local_ch, 1)
    summed = None
    for a in range(3):
        for b in range(3):
            view = grad_halo[:, :, 2 - a : 2 - a + tile_w, 2 - b : 2 - b + block_rows]
            product = jnp.einsum(
                "oi,noxy->nixy", w2_cols[:, :, a, b], view, preferred_element_type=jnp.float32
            )
            summed = product if summed is None else summed + product
    hidden_grad = jnp.where(hidden_here > 0, summed, 0.0).astype(jnp.bfloat16)
    first_pieces = []
    for a in range(3):
        for b in range(3):
            view = input_halo[:, :, a : a + tile_w, b : b + block_rows]
            first_pieces.append(
                jnp.einsum("noxy,nixy->oi", hidden_grad, view, preferred_element_type=jnp.float32)
            )
    first_local = jnp.stack(first_pieces, axis=-1).reshape(local_ch, all_channels, 3, 3)
    empty_grad = jnp.zeros((all_channels, all_channels, 3, 3), jnp.float32)
    first_full = lax.dynamic_update_slice_in_dim(empty_grad, first_local, first_ch, 0)
    second_full = lax.dynamic_update_slice_in_dim(empty_grad, second_local, first_ch, 0)
    first_sum, second_sum = lax.psum((first_full, second_full), ("row", "col", "chan"))
    factor = 1.0 / math.sqrt(
        2.0 * tile_w * lax.axis_size("col") * block_rows * lax.axis_size("row")
    )
    return (grad_features, first_sum * factor, second_sum * factor)


def solution(mesh):
    return jax.shard_map(
        body,
        mesh=mesh,
        in_specs=(
            P(None, None, ("groups", "col"), "row"),
            P(None, "chan", ("groups", "col"), "row"),
            P("chan", None, ("groups", "col"), "row"),
            P("row", ("groups", "col")),
            P(),
            P(),
        ),
        out_specs=(
            P(None, "chan", ("groups", "col"), "row"),
            P("groups", None, None, None),
            P("groups", None, None, None),
        ),
        check_vma=False,
    )
```

profile of v0, /device:TPU:0, one launch (start us, length us, event | category | flops | bytes accessed | tf_op | source)
XLA Modules:
  0.0 375.4 jit_solution(15215072760396662357)
XLA Ops:
  8.2 7.0 %collective-permute-start = (bf16[32,8,128]{2,0,1:T(8,128)(2,1)S(1)}, bf16[32,8,128]{2,0,1:T(8,128)(2,1)S(1)}, u32[]{:S(2)}, u32[]{:S(2)}) collective-permute-start(bf16[32,8,128]{2,0,1:T(8,128)(2,1)S(1)} %bitcast.440), channel_id=1, source_target_pairs={{0,12},{1,13},{2,14},{3,15},{16,28},{17,29},{18,30},{19,31}} | collective-permute-start | bytes 196616 | tf_op jit(solution)/shard_map/ppermute | solution.py:15
  21.3 197.9 %while.19 = (s32[]{:T(128)}, f32[32,8,128]{2,1,0:T(8,128)S(1)}, f32[32,8,167]{2,1,0:T(8,128)S(1)}, bf16[32,8,167]{2,1,0:T(8,128)(2,1)S(1)}, f32[32,8,128]{2,1,0:...) while((s32[]{:T(128)}, f32[32,8,128]{2,1,0:T(8,128)S(1)}, ...), condition=%wide.region_9.10_spmd.clone, body=%wide.region_0.9_spmd.clone.sunk | while | flops 2228291 | bytes 7406695 | solution.py:86
  22.0 4.8 %dynamic_update_slice.114 = f32[32,8,167]{2,1,0:T(8,128)S(1)} dynamic-update-slice(f32[32,8,167]{2,1,0:T(8,128)S(1)} %get-tuple-element.376, f32[32,8,128]{2,1,0:T(8,128)S(1)} %fusion.177, s32[]{:T(128)} %constant.221.clone.1..sunk, s32[]{:T(128)} %constant.221.clone.1..sunk, s32[]{:T(128)S(6)} %select_n.377) | dynamic-update-slice | bytes 262148 | tf_op jit(solution)/shard_map/while/body/eval_jaxpr/dynamic_update_slice | solution.py:79
  26.9 4.8 %dynamic_update_slice.115 = f32[32,8,167]{2,1,0:T(8,128)S(1)} dynamic-update-slice(f32[32,8,167]{2,1,0:T(8,128)S(1)} %dynamic_update_slice.114, f32[32,8,128]{2,1,0:T(8,128)S(1)} %fusion.178, s32[]{:T(128)} %constant.221.clone.1..sunk, s32[]{:T(128)} %constant.221.clone.1..sunk, s32[]{:T(128)S(6)} %select_n.384) | dynamic-update-slice | bytes 262148 | tf_op jit(solution)/shard_map/while/body/eval_jaxpr/dynamic_update_slice | solution.py:79
  31.9 4.8 %dynamic_update_slice.116 = f32[32,8,167]{2,1,0:T(8,128)S(1)} dynamic-update-slice(f32[32,8,167]{2,1,0:T(8,128)S(1)} %dynamic_update_slice.115, f32[32,8,128]{2,1,0:T(8,128)S(1)} %fusion.179, s32[]{:T(128)} %constant.221.clone.1..sunk, s32[]{:T(128)} %constant.221.clone.1..sunk, s32[]{:T(128)S(6)} %select_n.383) | dynamic-update-slice | bytes 262148 | tf_op jit(solution)/shard_map/while/body/eval_jaxpr/dynamic_update_slice | solution.py:79
  36.8 4.8 %dynamic_update_slice.117 = f32[32,8,167]{2,1,0:T(8,128)S(1)} dynamic-update-slice(f32[32,8,167]{2,1,0:T(8,128)S(1)} %dynamic_update_slice.116, f32[32,8,128]{2,1,0:T(8,128)S(1)} %fusion.180, s32[]{:T(128)} %constant.221.clone.1..sunk, s32[]{:T(128)} %constant.221.clone.1..sunk, s32[]{:T(128)S(6)} %select_n.382) | dynamic-update-slice | bytes 262148 | tf_op jit(solution)/shard_map/while/body/eval_jaxpr/dynamic_update_slice | solution.py:79
  41.8 4.8 %dynamic_update_slice.118 = f32[32,8,167]{2,1,0:T(8,128)S(1)} dynamic-update-slice(f32[32,8,167]{2,1,0:T(8,128)S(1)} %dynamic_update_slice.117, f32[32,8,128]{2,1,0:T(8,128)S(1)} %fusion.181, s32[]{:T(128)} %constant.221.clone.1..sunk, s32[]{:T(128)} %constant.221.clone.1..sunk, s32[]{:T(128)S(6)} %select_n.381) | dynamic-update-slice | bytes 262148 | tf_op jit(solution)/shard_map/while/body/eval_jaxpr/dynamic_update_slice | solution.py:79
  46.7 4.8 %dynamic_update_slice.119 = f32[32,8,167]{2,1,0:T(8,128)S(1)} dynamic-update-slice(f32[32,8,167]{2,1,0:T(8,128)S(1)} %dynamic_update_slice.118, f32[32,8,128]{2,1,0:T(8,128)S(1)} %fusion.182, s32[]{:T(128)} %constant.221.clone.1..sunk, s32[]{:T(128)} %constant.221.clone.1..sunk, s32[]{:T(128)S(6)} %select_n.380) | dynamic-update-slice | bytes 262148 | tf_op jit(solution)/shard_map/while/body/eval_jaxpr/dynamic_update_slice | solution.py:79
  51.7 4.8 %dynamic_update_slice.120 = f32[32,8,167]{2,1,0:T(8,128)S(1)} dynamic-update-slice(f32[32,8,167]{2,1,0:T(8,128)S(1)} %dynamic_update_slice.119, f32[32,8,128]{2,1,0:T(8,128)S(1)} %fusion.183, s32[]{:T(128)} %constant.221.clone.1..sunk, s32[]{:T(128)} %constant.221.clone.1..sunk, s32[]{:T(128)S(6)} %select_n.379) | dynamic-update-slice | bytes 262148 | tf_op jit(solution)/shard_map/while/body/eval_jaxpr/dynamic_update_slice | solution.py:79
  56.7 4.8 %dynamic_update_slice.121 = f32[32,8,167]{2,1,0:T(8,128)S(1)} dynamic-update-slice(f32[32,8,167]{2,1,0:T(8,128)S(1)} %dynamic_update_slice.120, f32[32,8,128]{2,1,0:T(8,128)S(1)} %fusion.184, s32[]{:T(128)} %constant.221.clone.1..sunk, s32[]{:T(128)} %constant.221.clone.1..sunk, s32[]{:T(128)S(6)} %select_n.378) | dynamic-update-slice | bytes 262148 | tf_op jit(solution)/shard_map/while/body/eval_jaxpr/dynamic_update_slice | solution.py:79
  62.4 4.8 %dynamic_update_slice.114 = f32[32,8,167]{2,1,0:T(8,128)S(1)} dynamic-update-slice(f32[32,8,167]{2,1,0:T(8,128)S(1)} %get-tuple-element.376, f32[32,8,128]{2,1,0:T(8,128)S(1)} %fusion.177, s32[]{:T(128)} %constant.221.clone.1..sunk, s32[]{:T(128)} %constant.221.clone.1..sunk, s32[]{:T(128)S(6)} %select_n.377) | dynamic-update-slice | bytes 262148 | tf_op jit(solution)/shard_map/while/body/eval_jaxpr/dynamic_update_slice | solution.py:79
  67.4 4.8 %dynamic_update_slice.115 = f32[32,8,167]{2,1,0:T(8,128)S(1)} dynamic-update-slice(f32[32,8,167]{2,1,0:T(8,128)S(1)} %dynamic_update_slice.114, f32[32,8,128]{2,1,0:T(8,128)S(1)} %fusion.178, s32[]{:T(128)} %constant.221.clone.1..sunk, s32[]{:T(128)} %constant.221.clone.1..sunk, s32[]{:T(128)S(6)} %select_n.384) | dynamic-update-slice | bytes 262148 | tf_op jit(solution)/shard_map/while/body/eval_jaxpr/dynamic_update_slice | solution.py:79
  72.3 4.8 %dynamic_update_slice.116 = f32[32,8,167]{2,1,0:T(8,128)S(1)} dynamic-update-slice(f32[32,8,167]{2,1,0:T(8,128)S(1)} %dynamic_update_slice.115, f32[32,8,128]{2,1,0:T(8,128)S(1)} %fusion.179, s32[]{:T(128)} %constant.221.clone.1..sunk, s32[]{:T(128)} %constant.221.clone.1..sunk, s32[]{:T(128)S(6)} %select_n.383) | dynamic-update-slice | bytes 262148 | tf_op jit(solution)/shard_map/while/body/eval_jaxpr/dynamic_update_slice | solution.py:79
  77.3 4.8 %dynamic_update_slice.117 = f32[32,8,167]{2,1,0:T(8,128)S(1)} dynamic-update-slice(f32[32,8,167]{2,1,0:T(8,128)S(1)} %dynamic_update_slice.116, f32[32,8,128]{2,1,0:T(8,128)S(1)} %fusion.180, s32[]{:T(128)} %constant.221.clone.1..sunk, s32[]{:T(128)} %constant.221.clone.1..sunk, s32[]{:T(128)S(6)} %select_n.382) | dynamic-update-slice | bytes 262148 | tf_op jit(solution)/shard_map/while/body/eval_jaxpr/dynamic_update_slice | solution.py:79
  82.2 4.8 %dynamic_update_slice.118 = f32[32,8,167]{2,1,0:T(8,128)S(1)} dynamic-update-slice(f32[32,8,167]{2,1,0:T(8,128)S(1)} %dynamic_update_slice.117, f32[32,8,128]{2,1,0:T(8,128)S(1)} %fusion.181, s32[]{:T(128)} %constant.221.clone.1..sunk, s32[]{:T(128)} %constant.221.clone.1..sunk, s32[]{:T(128)S(6)} %select_n.381) | dynamic-update-slice | bytes 262148 | tf_op jit(solution)/shard_map/while/body/eval_jaxpr/dynamic_update_slice | solution.py:79
  87.2 4.8 %dynamic_update_slice.119 = f32[32,8,167]{2,1,0:T(8,128)S(1)} dynamic-update-slice(f32[32,8,167]{2,1,0:T(8,128)S(1)} %dynamic_update_slice.118, f32[32,8,128]{2,1,0:T(8,128)S(1)} %fusion.182, s32[]{:T(128)} %constant.221.clone.1..sunk, s32[]{:T(128)} %constant.221.clone.1..sunk, s32[]{:T(128)S(6)} %select_n.380) | dynamic-update-slice | bytes 262148 | tf_op jit(solution)/shard_map/while/body/eval_jaxpr/dynamic_update_slice | solution.py:79
  92.1 4.8 %dynamic_update_slice.120 = f32[32,8,167]{2,1,0:T(8,128)S(1)} dynamic-update-slice(f32[32,8,167]{2,1,0:T(8,128)S(1)} %dynamic_update_slice.119, f32[32,8,128]{2,1,0:T(8,128)S(1)} %fusion.183, s32[]{:T(128)} %constant.221.clone.1..sunk, s32[]{:T(128)} %constant.221.clone.1..sunk, s32[]{:T(128)S(6)} %select_n.379) | dynamic-update-slice | bytes 262148 | tf_op jit(solution)/shard_map/while/body/eval_jaxpr/dynamic_update_slice | solution.py:79
  102.8 4.8 %dynamic_update_slice.114 = f32[32,8,167]{2,1,0:T(8,128)S(1)} dynamic-update-slice(f32[32,8,167]{2,1,0:T(8,128)S(1)} %get-tuple-element.376, f32[32,8,128]{2,1,0:T(8,128)S(1)} %fusion.177, s32[]{:T(128)} %constant.221.clone.1..sunk, s32[]{:T(128)} %constant.221.clone.1..sunk, s32[]{:T(128)S(6)} %select_n.377) | dynamic-update-slice | bytes 262148 | tf_op jit(solution)/shard_map/while/body/eval_jaxpr/dynamic_update_slice | solution.py:79
  132.6 4.8 %dynamic_update_slice.120 = f32[32,8,167]{2,1,0:T(8,128)S(1)} dynamic-update-slice(f32[32,8,167]{2,1,0:T(8,128)S(1)} %dynamic_update_slice.119, f32[32,8,128]{2,1,0:T(8,128)S(1)} %fusion.183, s32[]{:T(128)} %constant.221.clone.1..sunk, s32[]{:T(128)} %constant.221.clone.1..sunk, s32[]{:T(128)S(6)} %select_n.379) | dynamic-update-slice | bytes 262148 | tf_op jit(solution)/shard_map/while/body/eval_jaxpr/dynamic_update_slice | solution.py:79
  163.1 4.8 %dynamic_update_slice.118 = f32[32,8,167]{2,1,0:T(8,128)S(1)} dynamic-update-slice(f32[32,8,167]{2,1,0:T(8,128)S(1)} %dynamic_update_slice.117, f32[32,8,128]{2,1,0:T(8,128)S(1)} %fusion.181, s32[]{:T(128)} %constant.221.clone.1..sunk, s32[]{:T(128)} %constant.221.clone.1..sunk, s32[]{:T(128)S(6)} %select_n.381) | dynamic-update-slice | bytes 262148 | tf_op jit(solution)/shard_map/while/body/eval_jaxpr/dynamic_update_slice | solution.py:79
  193.6 4.8 %dynamic_update_slice.116 = f32[32,8,167]{2,1,0:T(8,128)S(1)} dynamic-update-slice(f32[32,8,167]{2,1,0:T(8,128)S(1)} %dynamic_update_slice.115, f32[32,8,128]{2,1,0:T(8,128)S(1)} %fusion.179, s32[]{:T(128)} %constant.221.clone.1..sunk, s32[]{:T(128)} %constant.221.clone.1..sunk, s32[]{:T(128)S(6)} %select_n.383) | dynamic-update-slice | bytes 262148 | tf_op jit(solution)/shard_map/while/body/eval_jaxpr/dynamic_update_slice | solution.py:79
  226.9 9.5 %collective-permute-done.4 = f32[32,8,128]{2,0,1:T(8,128)S(1)} collective-permute-done((f32[32,8,128]{2,0,1:T(8,128)S(1)}, f32[32,8,128]{2,0,1:T(8,128)S(1)}, u32[]{:S(2)}, u32[]{:S(2)}) %collective-permute-start.4) | collective-permute-done | bytes 131104 | tf_op jit(solution)/shard_map/ppermute | solution.py:15
  241.7 10.1 %collective-permute-done.6 = bf16[2,128,8,1]{3,1,2,0:T(8,128)(2,1)S(1)} collective-permute-done((bf16[2,128,8,1]{3,1,2,0:T(8,128)(2,1)S(1)}, bf16[2,128,8,1]{3,1,2,0:T(8,128)(2,1)S(1)}, u32[]{:S(2)}, u32[]{:S(2)}) %collective-permute-start.6) | collective-permute-done | bytes 4128 | tf_op jit(solution)/shard_map/ppermute | solution.py:25
  277.8 88.8 %all-reduce.4.cloned.1.call-done = (f32[64,64,3,3]{1,0,3,2:T(8,128)}, f32[64,64,3,3]{1,0,3,2:T(8,128)}) async-done(((f32[64,64,3,3]{1,0,3,2:T(8,128)}, f32[64,64,3,3]{1,0,3,2:T(8,128)}), (f32[64,64,3,3]{1,0,3,2:T(8,128)}, f32[64,64,3,3]{1,0,3,2:T(8,128)})) %all-reduce.4.cloned.1.call-update) | async-done | bytes 294928 | tf_op jit(solution)/shard_map/psum | solution.py:156
  (172 shorter events, 151.7 us)
Async XLA Ops:
  7.2 234.3 %copy-start = (bf16[64,64,3,3]{1,0,3,2:T(8,128)(2,1)S(1)}, bf16[64,64,3,3]{1,0,3,2:T(8,128)(2,1)}, u32[]{:S(2)}) copy-start(bf16[64,64,3,3]{1,0,3,2:T(8,128)(2,1)} %param.13) | copy-start | bytes 221188
  7.2 13.7 %copy-start.4 = (bf16[4,40,8,128]{3,2,1,0:T(8,128)(2,1)S(1)}, bf16[4,40,8,128]{3,2,1,0:T(8,128)(2,1)}, u32[]{:S(2)}) copy-start(bf16[4,40,8,128]{3,2,1,0:T(8,128)(2,1)} %param.10) | copy-start | bytes 983044
  7.2 359.4 %all-reduce.4.cloned.1.call-start = ((), (), s32[]{:S(2)}) async-start(), calls=%async_computation | async-start | bytes 1179648 | tf_op jit(solution)/shard_map/psum | solution.py:156
  8.2 12.7 %collective-permute-start = (bf16[32,8,128]{2,0,1:T(8,128)(2,1)S(1)}, bf16[32,8,128]{2,0,1:T(8,128)(2,1)S(1)}, u32[]{:S(2)}, u32[]{:S(2)}) collective-permute-start(bf16[32,8,128]{2,0,1:T(8,128)(2,1)S(1)} %bitcast.440), channel_id=1, source_target_pairs={{0,12},{1,13},{2,14},{3,15},{16,28},{17,29},{18,30},{19,31}} | collective-permute-start | bytes 196616 | tf_op jit(solution)/shard_map/ppermute | solution.py:15
  15.2 5.7 %collective-permute-start.1 = (bf16[32,8,128]{2,0,1:T(8,128)(2,1)S(1)}, bf16[32,8,128]{2,0,1:T(8,128)(2,1)S(1)}, u32[]{:S(2)}, u32[]{:S(2)}) collective-permute-start(bf16[32,8,128]{2,0,1:T(8,128)(2,1)S(1)} %bitcast.441), channel_id=1, source_target_pairs={{0,8},{4,12},{1,9},{5,13},{2,10},{6,14},{3,11},{7,15},{16,24},{20,... | collective-permute-start | bytes 196616 | tf_op jit(solution)/shard_map/ppermute | solution.py:15
  16.5 4.5 %collective-permute-start.2 = (bf16[32,8,128]{2,0,1:T(8,128)(2,1)S(1)}, bf16[32,8,128]{2,0,1:T(8,128)(2,1)S(1)}, u32[]{:S(2)}, u32[]{:S(2)}) collective-permute-start(bf16[32,8,128]{2,0,1:T(8,128)(2,1)S(1)} %bitcast.442), channel_id=1, source_target_pairs={{0,4},{4,8},{8,12},{1,5},{5,9},{9,13},{2,6},{6,10},{10,14},{3,7},{... | collective-permute-start | bytes 196616 | tf_op jit(solution)/shard_map/ppermute | solution.py:15
  219.3 4.2 %copy-start.1 = (bf16[2,64,8,128]{3,2,1,0:T(8,128)(2,1)S(1)}, bf16[2,64,8,128]{3,2,1,0:T(8,128)(2,1)}, u32[]{:S(2)}) copy-start(bf16[2,64,8,128]{3,2,1,0:T(8,128)(2,1)} %param.8) | copy-start | bytes 786436
  219.5 7.4 %collective-permute-start.3 = (f32[32,8,128]{2,0,1:T(8,128)S(1)}, f32[32,8,128]{2,0,1:T(8,128)S(1)}, u32[]{:S(2)}, u32[]{:S(2)}) collective-permute-start(f32[32,8,128]{2,0,1:T(8,128)S(1)} %get-tuple-element.273), channel_id=1, source_target_pairs={{4,0},{8,4},{12,8},{5,1},{9,5},{13,9},{6,2},{10,6},{14,10},{7,3},{... | collective-permute-start | bytes 393224 | tf_op jit(solution)/shard_map/ppermute | solution.py:15
  220.8 15.5 %collective-permute-start.4 = (f32[32,8,128]{2,0,1:T(8,128)S(1)}, f32[32,8,128]{2,0,1:T(8,128)S(1)}, u32[]{:S(2)}, u32[]{:S(2)}) collective-permute-start(f32[32,8,128]{2,0,1:T(8,128)S(1)} %get-tuple-element.274), channel_id=1, source_target_pairs={{8,0},{12,4},{9,1},{13,5},{10,2},{14,6},{11,3},{15,7},{24,16},{28,... | collective-permute-start | bytes 393224 | tf_op jit(solution)/shard_map/ppermute | solution.py:15
  222.1 14.2 %collective-permute-start.5 = (f32[32,8,128]{2,0,1:T(8,128)S(1)}, f32[32,8,128]{2,0,1:T(8,128)S(1)}, u32[]{:S(2)}, u32[]{:S(2)}) collective-permute-start(f32[32,8,128]{2,0,1:T(8,128)S(1)} %get-tuple-element.275), channel_id=1, source_target_pairs={{12,0},{13,1},{14,2},{15,3},{28,16},{29,17},{30,18},{31,19}} | collective-permute-start | bytes 393224 | tf_op jit(solution)/shard_map/ppermute | solution.py:15
  238.8 13.1 %collective-permute-start.6 = (bf16[2,128,8,1]{3,1,2,0:T(8,128)(2,1)S(1)}, bf16[2,128,8,1]{3,1,2,0:T(8,128)(2,1)S(1)}, u32[]{:S(2)}, u32[]{:S(2)}) collective-permute-start(bf16[2,128,8,1]{3,1,2,0:T(8,128)(2,1)S(1)} %get-tuple-element.271), channel_id=1, source_target_pairs={{0,4},{4,8},{8,12},{1,5},{5,9},{9,13},{2,6},{6,10},{10,14},{3,7},{... | collective-permute-start | bytes 12296 | tf_op jit(solution)/shard_map/ppermute | solution.py:25
  240.1 15.9 %collective-permute-start.7 = (bf16[2,128,8,1]{3,1,2,0:T(8,128)(2,1)S(1)}, bf16[2,128,8,1]{3,1,2,0:T(8,128)(2,1)S(1)}, u32[]{:S(2)}, u32[]{:S(2)}) collective-permute-start(bf16[2,128,8,1]{3,1,2,0:T(8,128)(2,1)S(1)} %get-tuple-element.272), channel_id=1, source_target_pairs={{4,0},{8,4},{12,8},{5,1},{9,5},{13,9},{6,2},{10,6},{14,10},{7,3},{... | collective-permute-start | bytes 12296 | tf_op jit(solution)/shard_map/ppermute | solution.py:26
  256.2 5.4 %copy-start.5 = (bf16[64,64,3,3]{1,0,3,2:T(8,128)(2,1)S(1)}, bf16[64,64,3,3]{1,0,3,2:T(8,128)(2,1)}, u32[]{:S(2)}) copy-start(bf16[64,64,3,3]{1,0,3,2:T(8,128)(2,1)} %param.12) | copy-start | bytes 221188
  256.2 6.0 %collective-permute-start.8 = (bf16[2,128,1,130]{3,1,2,0:T(8,128)(2,1)S(1)}, bf16[2,128,1,130]{3,1,2,0:T(8,128)(2,1)S(1)}, u32[]{:S(2)}, u32[]{:S(2)}) collective-permute-start(bf16[2,128,1,130]{3,1,2,0:T(8,128)(2,1)S(1)} %get-tuple-element.267), channel_id=1, source_target_pairs={{0,2},{1,3},{4,6},{5,7},{8,10},{9,11},{12,14},{13,15},{16,18},{17,... | collective-permute-start | bytes 199688 | tf_op jit(solution)/shard_map/ppermute | solution.py:25
  259.7 6.9 %collective-permute-start.9 = (bf16[2,128,1,130]{3,1,2,0:T(8,128)(2,1)S(1)}, bf16[2,128,1,130]{3,1,2,0:T(8,128)(2,1)S(1)}, u32[]{:S(2)}, u32[]{:S(2)}) collective-permute-start(bf16[2,128,1,130]{3,1,2,0:T(8,128)(2,1)S(1)} %get-tuple-element.268), channel_id=1, source_target_pairs={{2,0},{3,1},{6,4},{7,5},{10,8},{11,9},{14,12},{15,13},{18,16},{19,... | collective-permute-start | bytes 199688 | tf_op jit(solution)/shard_map/ppermute | solution.py:26
  276.2 0.7 copy-start.3
  276.3 0.7 copy-start.2
Sparse Core Ops, SparseCore 0:
  277.2 89.3 all-reduce.3
where the time goes:
time: 376 us; the launch traced here: 375 us
  local copies, waits for them, and re-layouts  191 us (51%)
  waiting for transfers between devices  120 us (32%)
  starting transfers between devices  22.3 us (6%)
  between operations  15.2 us (4%)
  other arithmetic  12.7 us (3%)
  matrix products  10.3 us (3%)
    dynamic_update_slice x40, local copies, waits for them, and re-layouts, one_turn(): lax.dynamic_update_slice_in_dim(window_grad, window_part, first_row, 2)  189 us
    psum x1, waiting for transfers between devices, body(): lax.psum((first_full, second_full), ('row', 'col', 'chan'))  88.8 us
    ppermute x6, starting transfers between devices, passed_along(): return lax.ppermute(block, axis, route)  14.6 us
    ppermute x6, waiting for transfers between devices, passed_along(): return lax.ppermute(block, axis, route)  12.8 us
    ppermute x2, waiting for transfers between devices, extended(): before = lax.ppermute(last, axis, up)  10.2 us
    ppermute x2, waiting for transfers between devices, extended(): after = lax.ppermute(leading, axis, down)  8.51 us
  transfers between devices with their start and end apart: 11, of which 7 were waited for; matrix products, arithmetic and copies ran while one was open for 1% of the time, Pallas kernels for 0%

commit v1 on v0

v1 whole, which is shorter than its diff:
```python
import math

import jax
import jax.numpy as jnp
from jax import lax
from jax.experimental import pallas as pl
from jax.experimental.pallas import tpu as pltpu
from jax.sharding import PartitionSpec as P

DISP = 40
MAXOFF = 2


def passed_along(block, axis, distance):
    devices = range(lax.axis_size(axis))
    route = [(i - distance, i) for i in devices if i - distance in devices]
    return lax.ppermute(block, axis, route)


def extended(array, sides, width):
    for axis, dim in sides:
        peers, length = (lax.axis_size(axis), array.shape[dim])
        up = [(i, (i + 1) % peers) for i in range(peers - 1)]
        down = [(j, i) for i, j in up]
        last = lax.slice_in_dim(array, length - width, length, axis=dim)
        leading = lax.slice_in_dim(array, 0, width, axis=dim)
        before = lax.ppermute(last, axis, up)
        after = lax.ppermute(leading, axis, down)
        array = jnp.concatenate([before, array, after], axis=dim)
    return array


def correlation_kernel(offset_ref, left_ref, own_ref, one_ref, two_ref, three_ref, target_ref,
                       left_out, own_out, one_out, two_out, three_out):
    offset = offset_ref[0, 0]
    group_size, tile_w, block_rows = left_ref.shape
    inv_size = 1.0 / group_size
    shape = (tile_w, block_rows)
    lane = lax.broadcasted_iota(jnp.int32, shape, 1)
    left, main, spill = [], [], []
    for c in range(group_size):
        own, one, two, three = (r[c].astype(jnp.float32) for r in (own_ref, one_ref, two_ref, three_ref))
        left.append(left_ref[c].astype(jnp.float32))
        main.append(jnp.where(offset == 0, own, jnp.where(offset == 1, one, two)))
        spill.append(jnp.where(offset == 0, one, jnp.where(offset == 1, two, three)))
    zero = jnp.zeros(shape, jnp.float32)
    left_grad = [zero] * group_size
    whole_grad = [zero] * group_size
    spill_grad = [zero] * group_size
    for d in range(DISP):
        volume = None
        shifted = []
        for c in range(group_size):
            if d:
                moved = pltpu.roll(jnp.where(lane >= block_rows - d, spill[c], main[c]), d, 1)
            else:
                moved = main[c]
            shifted.append(moved)
            product = left[c] * moved
            volume = product if volume is None else volume + product
        weighted = (volume * inv_size - target_ref[0, d].astype(jnp.float32)) * inv_size
        for c in range(group_size):
            left_grad[c] = left_grad[c] + weighted * shifted[c]
            part = weighted * left[c]
            if d:
                part = pltpu.roll(part, block_rows - d, 1)
                spill_grad[c] = spill_grad[c] + jnp.where(lane >= block_rows - d, part, 0.0)
            whole_grad[c] = whole_grad[c] + part
    for c in range(group_size):
        main_grad = whole_grad[c] - spill_grad[c]
        left_out[c] = left_grad[c].astype(left_out.dtype)
        own_out[c] = jnp.where(offset == 0, main_grad, 0.0)
        one_out[c] = jnp.where(offset == 0, spill_grad[c], jnp.where(offset == 1, main_grad, 0.0)).astype(one_out.dtype)
        two_out[c] = jnp.where(offset == 1, spill_grad[c], jnp.where(offset == 2, main_grad, 0.0)).astype(two_out.dtype)
        three_out[c] = jnp.where(offset == 2, spill_grad[c], 0.0).astype(three_out.dtype)


def correlate(offset, left_feat, blocks, vol_target):
    local_ch, tile_w, block_rows = left_feat.shape
    groups = vol_target.shape[0]
    size = local_ch // groups
    tile = pl.BlockSpec((size, tile_w, block_rows), lambda g: (g, 0, 0))
    small = jax.ShapeDtypeStruct(left_feat.shape, jnp.bfloat16)
    return pl.pallas_call(
        correlation_kernel,
        grid=(groups,),
        in_specs=[pl.BlockSpec(memory_space=pltpu.SMEM)] + [tile] * 5
        + [pl.BlockSpec((1, DISP, tile_w, block_rows), lambda g: (g, 0, 0, 0))],
        out_specs=[tile] * 5,
        out_shape=[small, jax.ShapeDtypeStruct(left_feat.shape, jnp.float32), small, small, small],
        name="correlate",
    )(offset, left_feat, *blocks, vol_target)


def summed_over(partial, axis):
    peers = lax.axis_size(axis)
    step = 1
    while step < peers:
        rounded = partial.astype(jnp.bfloat16)
        arrived = lax.ppermute(rounded, axis, [(i, i ^ step) for i in range(peers)])
        partial = rounded.astype(jnp.float32) + arrived.astype(jnp.float32)
        step *= 2
    return partial


def body(layer_input, features, vol_target, offsets, w_first, w_second):
    all_channels = layer_input.shape[1]
    tile_w = layer_input.shape[2]
    block_rows = layer_input.shape[3]
    local_ch = features.shape[1]
    left_feat = features[0]
    right_feat = features[1]
    first_ch = lax.axis_index("chan") * local_ch
    blocks = [right_feat] + [passed_along(right_feat, "row", k) for k in range(1, MAXOFF + 2)]
    left_grad, own, *outgoing = correlate(offsets, left_feat, blocks, vol_target)
    right_grad = own
    for k, part in enumerate(outgoing, 1):
        right_grad = right_grad + passed_along(part, "row", -k).astype(jnp.float32)
    grad_features = jnp.stack([left_grad, right_grad.astype(jnp.bfloat16)])
    swap = [(i, i ^ 1) for i in range(2)]
    grad_maps = lax.all_gather(grad_features, "chan", axis=1, tiled=True)
    joined = extended(
        jnp.concatenate([layer_input, grad_maps], axis=1), (("row", 3), ("col", 2)), 1
    )
    input_halo = joined[:, :all_channels]
    grad_halo = joined[:, all_channels:]
    summed = None
    for a in range(3):
        for b in range(3):
            product = jnp.einsum(
                "oi,nixy->noxy",
                w_first[:, :, a, b],
                input_halo[:, :, a : a + tile_w, b : b + block_rows],
                preferred_element_type=jnp.float32,
            )
            summed = product if summed is None else summed + product
    hidden = jnp.maximum(summed, 0.0).astype(jnp.bfloat16)
    hidden_here = lax.dynamic_slice_in_dim(hidden, first_ch, local_ch, 1)
    own_halo = lax.dynamic_slice_in_dim(grad_halo, first_ch, local_ch, 1)
    second_pieces = []
    for a in range(3):
        for b in range(3):
            view = own_halo[:, :, 2 - a : 2 - a + tile_w, 2 - b : 2 - b + block_rows]
            second_pieces.append(
                jnp.einsum("noxy,nixy->oi", view, hidden, preferred_element_type=jnp.float32)
            )
    w2_cols = lax.dynamic_slice_in_dim(w_second, first_ch, local_ch, 1)
    summed = None
    for a in range(3):
        for b in range(3):
            view = grad_halo[:, :, 2 - a : 2 - a + tile_w, 2 - b : 2 - b + block_rows]
            product = jnp.einsum(
                "oi,noxy->nixy", w2_cols[:, :, a, b], view, preferred_element_type=jnp.float32
            )
            summed = product if summed is None else summed + product
    hidden_grad = jnp.where(hidden_here > 0, summed, 0.0).astype(jnp.bfloat16)
    first_pieces = []
    for a in range(3):
        for b in range(3):
            view = input_halo[:, :, a : a + tile_w, b : b + block_rows]
            first_pieces.append(
                jnp.einsum("noxy,nixy->oi", hidden_grad, view, preferred_element_type=jnp.float32)
            )
    partial = jnp.concatenate([jnp.stack(first_pieces), jnp.stack(second_pieces)], axis=2)
    for axis in ("col", "row"):
        partial = summed_over(partial, axis)
    factor = 1.0 / math.sqrt(
        2.0 * tile_w * lax.axis_size("col") * block_rows * lax.axis_size("row")
    )
    both = lax.all_gather(partial * factor, "chan", axis=1, tiled=True)
    both = both.reshape(3, 3, all_channels, 2 * all_channels).transpose(2, 3, 0, 1)
    return (grad_features, both[:, :all_channels], both[:, all_channels:])


def solution(mesh):
    return jax.shard_map(
        body,
        mesh=mesh,
        in_specs=(
            P(None, None, ("groups", "col"), "row"),
            P(None, "chan", ("groups", "col"), "row"),
            P("chan", None, ("groups", "col"), "row"),
            P("row", ("groups", "col")),
            P(),
            P(),
        ),
        out_specs=(
            P(None, "chan", ("groups", "col"), "row"),
            P("groups", None, None, None),
            P("groups", None, None, None),
        ),
        check_vma=False,
    )
```

time: 376 us -> 107 us (0.28)
  local copies, waits for them, and re-layouts: 191 us -> 4.55 us
  waiting for transfers between devices: 120 us -> 36.5 us
  between operations: 15.2 us -> 1.8 us
  Pallas kernels: 0 us -> 12.9 us
  starting transfers between devices: 22.3 us -> 30.2 us
  other arithmetic: 12.7 us -> 7.12 us
    dynamic_update_slice x42 -> x0, local copies, waits for them, and re-layouts: 189 us -> none  [the longest x40 189 us: one_turn(): lax.dynamic_update_slice_in_dim(window_grad, window_part, first_row, 2)]
    psum x1 -> x0, waiting for transfers between devices: 88.8 us -> none  [body(): lax.psum((first_full, second_full), ('row', 'col', 'chan'))]
    pallas_call x0 -> x1, Pallas kernels: none -> 12.9 us  [correlate(): pl.pallas_call(correlation_kernel, grid=(groups,), in_specs=[pl.BlockSpec...]
    ppermute x0 -> x3, waiting for transfers between devices: none -> 10.7 us  [summed_over(): arrived = lax.ppermute(rounded, axis, [(i, i ^ step) for i in range(peers)])]
    ppermute x2, waiting for transfers between devices: 10.2 us -> 1.18 us  [extended(): before = lax.ppermute(last, axis, up)]
    ppermute x2, waiting for transfers between devices: 8.51 us -> 16.4 us  [extended(): after = lax.ppermute(leading, axis, down)]
    add x46 -> x0, other arithmetic: 5.92 us -> none  [the longest x40 4.36 us: one_turn(): lax.dynamic_slice_in_dim(window_grad, first_row, block_rows, 2)]
    ppermute x0 -> x3, starting transfers between devices: none -> 4.65 us  [summed_over(): arrived = lax.ppermute(rounded, axis, [(i, i ^ step) for i in range(peers)])]
  transfers between devices with their start and end apart: 11 -> 13, of which waited for: 7 -> 10; matrix products, arithmetic and copies ran while one was open for 1% -> 4% of each run, Pallas kernels for 0% -> 0%
where the time goes in v1:
time: 107 us; the launch traced here: 106 us
  waiting for transfers between devices  36.5 us (34%)
  starting transfers between devices  30.2 us (28%)
  Pallas kernels  12.9 us (12%)
  matrix products  9.04 us (8%)
  other arithmetic  7.12 us (7%)
  local copies, waits for them, and re-layouts  4.55 us (4%)
  blocking collectives  4.01 us (4%)
  between operations  1.8 us (2%)
    ppermute x2, waiting for transfers between devices, extended(): after = lax.ppermute(leading, axis, down)  16.4 us
    ppermute x6, starting transfers between devices, passed_along(): return lax.ppermute(block, axis, route)  14.7 us
    pallas_call x1, Pallas kernels, correlate(): pl.pallas_call(correlation_kernel, grid=(groups,), in_specs=[pl.BlockSpec...  12.9 us
    ppermute x3, waiting for transfers between devices, summed_over(): arrived = lax.ppermute(rounded, axis, [(i, i ^ step) for i in range(peers)])  10.7 us
    ppermute x6, waiting for transfers between devices, passed_along(): return lax.ppermute(block, axis, route)  8.27 us
    ppermute x2, starting transfers between devices, extended(): before = lax.ppermute(last, axis, up)  7.99 us
    ppermute x3, starting transfers between devices, summed_over(): arrived = lax.ppermute(rounded, axis, [(i, i ^ step) for i in range(peers)])  4.65 us
    slice x2, other arithmetic, body(): view = grad_halo[:, :, 2 - a:2 - a + tile_w, 2 - b:2 - b + block_rows]  3.56 us
  transfers between devices with their start and end apart: 13, of which 10 were waited for; matrix products, arithmetic and copies ran while one was open for 4% of the time, Pallas kernels for 0%

profile of v1, /device:TPU:0, one launch (start us, length us, event | category | flops | bytes accessed | tf_op | source)
XLA Modules:
  0.0 106.1 jit_solution(1508001566311946375)
XLA Ops:
  0.7 1.6 %slice_bitcast_fusion = (bf16[32,8,128]{2,1,0:T(8,128)(2,1)S(1)}, bf16[32,8,128]{2,1,0:T(8,128)(2,1)}) fusion(bf16[2,32,8,128]{3,2,1,0:T(8,128)(2,1)} %param.7), kind=kLoop, calls=%fused_computation.191 | loop fusion | bytes 262144 | tf_op jit(solution)/shard_map/squeeze | solution.py:112
  2.2 4.9 %collective-permute-start = (bf16[32,8,128]{2,1,0:T(8,128)(2,1)S(1)}, bf16[32,8,128]{2,1,0:T(8,128)(2,1)S(1)}, u32[]{:S(2)}, u32[]{:S(2)}) collective-permute-start(bf16[32,8,128]{2,1,0:T(8,128)(2,1)S(1)} %get-tuple-element.46.own_ref), channel_id=1, source_target_pairs={{0,4},{4,8},{8,12},{1,5},{5,9},{9,13},{2,6},{6,10},{10,14},{3,7},{... | collective-permute-start | bytes 196616 | tf_op jit(solution)/shard_map/ppermute | solution.py:17
  7.2 4.5 %collective-permute-start.1 = (bf16[32,8,128]{2,1,0:T(8,128)(2,1)S(1)}, bf16[32,8,128]{2,1,0:T(8,128)(2,1)S(1)}, u32[]{:S(2)}, u32[]{:S(2)}) collective-permute-start(bf16[32,8,128]{2,1,0:T(8,128)(2,1)S(1)} %get-tuple-element.46.own_ref), channel_id=1, source_target_pairs={{0,8},{4,12},{1,9},{5,13},{2,10},{6,14},{3,11},{7,15},{16,24},{20,... | collective-permute-start | bytes 196616 | tf_op jit(solution)/shard_map/ppermute | solution.py:17
  11.7 1.3 %collective-permute-start.2 = (bf16[32,8,128]{2,1,0:T(8,128)(2,1)S(1)}, bf16[32,8,128]{2,1,0:T(8,128)(2,1)S(1)}, u32[]{:S(2)}, u32[]{:S(2)}) collective-permute-start(bf16[32,8,128]{2,1,0:T(8,128)(2,1)S(1)} %get-tuple-element.46.own_ref), channel_id=1, source_target_pairs={{0,12},{1,13},{2,14},{3,15},{16,28},{17,29},{18,30},{19,31}} | collective-permute-start | bytes 196616 | tf_op jit(solution)/shard_map/ppermute | solution.py:17
  15.5 12.9 %correlate.1 = (bf16[32,8,128]{2,1,0:T(8,128)(2,1)}, f32[32,8,128]{2,1,0:T(8,128)}, bf16[32,8,128]{2,1,0:T(8,128)(2,1)}, bf16[32,8,128]{2,1,0:T(8,128)(2,1)}, bf16[32,8,128]{2,1,0:T(8,128)(2,1)}) custom-call(s32[1,1]{1,0:T(1,128)S(6)} %copy.248.offset_ref, bf16[32,8,128]{2,1,0:T(8,128)(2,1)} %get-tuple-element.47.left_ref, bf16[32,8,128]{2,1,0:T(8,128)(2,1)} %copy-done.3, ...), custom_call_target="tpu_custom_call" | custom-call | tf_op jit(solution)/shard_map/correlate/pallas_call | solution.py:84
  31.0 1.4 %collective-permute-start.5 = (bf16[32,8,128]{2,1,0:T(8,128)(2,1)}, bf16[32,8,128]{2,1,0:T(8,128)(2,1)S(1)}, u32[]{:S(2)}, u32[]{:S(2)}) collective-permute-start(bf16[32,8,128]{2,1,0:T(8,128)(2,1)} %get-tuple-element.12), channel_id=1, source_target_pairs={{12,0},{13,1},{14,2},{15,3},{28,16},{29,17},{30,18},{31,19}} | collective-permute-start | bytes 196616 | tf_op jit(solution)/shard_map/ppermute | solution.py:17
  32.5 2.8 %collective-permute-done.3 = bf16[32,8,128]{2,1,0:T(8,128)(2,1)S(1)} collective-permute-done((bf16[32,8,128]{2,1,0:T(8,128)(2,1)}, bf16[32,8,128]{2,1,0:T(8,128)(2,1)S(1)}, u32[]{:S(2)}, u32[]{:S(2)}) %collective-permute-start.3) | collective-permute-done | bytes 65568 | tf_op jit(solution)/shard_map/ppermute | solution.py:17
  35.2 2.4 %collective-permute-done.4 = bf16[32,8,128]{2,1,0:T(8,128)(2,1)S(1)} collective-permute-done((bf16[32,8,128]{2,1,0:T(8,128)(2,1)}, bf16[32,8,128]{2,1,0:T(8,128)(2,1)S(1)}, u32[]{:S(2)}, u32[]{:S(2)}) %collective-permute-start.4) | collective-permute-done | bytes 65568 | tf_op jit(solution)/shard_map/ppermute | solution.py:17
  37.6 2.8 %collective-permute-done.5 = bf16[32,8,128]{2,1,0:T(8,128)(2,1)S(1)} collective-permute-done((bf16[32,8,128]{2,1,0:T(8,128)(2,1)}, bf16[32,8,128]{2,1,0:T(8,128)(2,1)S(1)}, u32[]{:S(2)}, u32[]{:S(2)}) %collective-permute-start.5) | collective-permute-done | bytes 65568 | tf_op jit(solution)/shard_map/ppermute | solution.py:17
  41.3 2.0 %all_gather.6 = bf16[2,64,8,128]{3,2,1,0:T(8,128)(2,1)S(1)} all-gather(bf16[2,32,8,128]{3,2,1,0:T(8,128)(2,1)S(1)} %pad_maximum_fusion.23), channel_id=1, replica_groups=mesh['groups'=2,'row'=4,'col'=2,'chan'=2] {'chan'}, dimensions={1}, use_global_device_ids=true | all-gather | bytes 393216 | tf_op jit(solution)/shard_map/all_gather | solution.py:121
  44.9 4.6 %collective-permute-start.6 = (bf16[2,128,8,1]{3,2,1,0:T(8,128)(2,1)S(1)}, bf16[2,128,8,1]{3,2,1,0:T(8,128)(2,1)S(1)}, u32[]{:S(2)}, u32[]{:S(2)}) collective-permute-start(bf16[2,128,8,1]{3,2,1,0:T(8,128)(2,1)S(1)} %get-tuple-element.42), channel_id=1, source_target_pairs={{0,4},{4,8},{8,12},{1,5},{5,9},{9,13},{2,6},{6,10},{10,14},{3,7},{... | collective-permute-start | bytes 12296 | tf_op jit(solution)/shard_map/ppermute | solution.py:27
  49.8 9.7 %collective-permute-done.7 = bf16[2,128,8,1]{3,2,1,0:T(8,128)(2,1)S(1)} collective-permute-done((bf16[2,128,8,1]{3,2,1,0:T(8,128)(2,1)S(1)}, bf16[2,128,8,1]{3,2,1,0:T(8,128)(2,1)S(1)}, u32[]{:S(2)}, u32[]{:S(2)}) %collective-permute-start.7) | collective-permute-done | bytes 4128 | tf_op jit(solution)/shard_map/ppermute | solution.py:28
  60.6 1.3 %pad_maximum_fusion.22 = (bf16[2,128,1,130]{3,2,1,0:T(2,128)(2,1)S(1)}, bf16[2,128,1,130]{3,2,1,0:T(2,128)(2,1)S(1)}) fusion(bf16[2,128,8,1]{3,2,1,0:T(8,128)(2,1)S(1)} %collective-permute-done.7, bf16[2,128,8,128]{3,2,1,0:T(8,128)(2,1)S(1)} %constant_dynamic-update-slice_fusion, bf16[2,128,8,1]{3,2,1,0:T(8,128)(2,1)S(1)} %collective-permute-done.6), kind=kLoop, calls=%fused_computation.124 | loop fusion | flops 399360 | bytes 665600 | tf_op jit(solution)/shard_map/slice | solution.py:25
  62.0 3.4 %collective-permute-start.8 = (bf16[2,128,1,130]{3,2,1,0:T(2,128)(2,1)S(1)}, bf16[2,128,1,130]{3,2,1,0:T(2,128)(2,1)S(1)}, u32[]{:S(2)}, u32[]{:S(2)}) collective-permute-start(bf16[2,128,1,130]{3,2,1,0:T(2,128)(2,1)S(1)} %get-tuple-element.27), channel_id=1, source_target_pairs={{0,2},{1,3},{4,6},{5,7},{8,10},{9,11},{12,14},{13,15},{16,18},{17,... | collective-permute-start | bytes 199688 | tf_op jit(solution)/shard_map/ppermute | solution.py:27
  65.4 1.5 %collective-permute-start.9 = (bf16[2,128,1,130]{3,2,1,0:T(2,128)(2,1)S(1)}, bf16[2,128,1,130]{3,2,1,0:T(2,128)(2,1)S(1)}, u32[]{:S(2)}, u32[]{:S(2)}) collective-permute-start(bf16[2,128,1,130]{3,2,1,0:T(2,128)(2,1)S(1)} %get-tuple-element.28), channel_id=1, source_target_pairs={{2,0},{3,1},{6,4},{7,5},{10,8},{11,9},{14,12},{15,13},{18,16},{19,... | collective-permute-start | bytes 199688 | tf_op jit(solution)/shard_map/ppermute | solution.py:28
  67.5 6.7 %collective-permute-done.9 = bf16[2,128,1,130]{3,2,1,0:T(2,128)(2,1)S(1)} collective-permute-done((bf16[2,128,1,130]{3,2,1,0:T(2,128)(2,1)S(1)}, bf16[2,128,1,130]{3,2,1,0:T(2,128)(2,1)S(1)}, u32[]{:S(2)}, u32[]{:S(2)}) %collective-permute-start.9) | collective-permute-done | bytes 66592 | tf_op jit(solution)/shard_map/ppermute | solution.py:28
  74.2 2.0 %pad_maximum_fusion.11 = (bf16[2,64,8,128]{3,2,1,0:T(8,128)(2,1)S(1)}, bf16[2,64,8,128]{3,2,1,0:T(8,128)(2,1)S(1)}, bf16[2,64,8,128]{3,2,1,0:T(8,128)(2,1)S(1)},...) fusion(bf16[2,128,1,130]{3,2,1,0:T(2,128)(2,1)S(1)} %collective-permute-done.9, ...), kind=kLoop, calls=%fused_computation.113 | loop fusion | flops 4718592 | bytes 1909760 | tf_op jit(solution)/shard_map/slice | solution.py:151
  76.5 1.6 %pad_maximum_fusion.4 = (bf16[2,64,8,128]{3,2,1,0:T(8,128)(2,1)S(1)}, bf16[2,64,8,128]{3,2,1,0:T(8,128)(2,1)S(1)}, bf16[2,64,8,128]{3,2,1,0:T(8,128)(2,1)S(1)}, bf16[2,64,8,128]{3,2,1,0:T(8,128)(2,1)S(1)}) fusion(bf16[2,128,1,130]{3,2,1,0:T(2,128)(2,1)S(1)} %collective-permute-done.8, bf16[2,128,8,1]{3,2,1,0:T(8,128)(2,1)S(1)} %collective-permute-done.7, ...), kind=kLoop, calls=%fused_computation.106 | loop fusion | flops 4194304 | bytes 1647616 | tf_op jit(solution)/shard_map/slice | solution.py:151
  87.7 4.3 %collective-permute-done.10 = bf16[9,32,128]{2,1,0:T(8,128)(2,1)S(1)} collective-permute-done((bf16[9,32,128]{2,1,0:T(8,128)(2,1)S(1)}, bf16[9,32,128]{2,1,0:T(8,128)(2,1)S(1)}, u32[]{:S(2)}, u32[]{:S(2)}) %collective-permute-start.10) | collective-permute-done | bytes 73760 | tf_op jit(solution)/shard_map/ppermute | solution.py:100
  92.2 2.5 %collective-permute-start.11 = (bf16[9,32,128]{2,1,0:T(8,128)(2,1)S(1)}, bf16[9,32,128]{2,1,0:T(8,128)(2,1)S(1)}, u32[]{:S(2)}, u32[]{:S(2)}) collective-permute-start(bf16[9,32,128]{2,1,0:T(8,128)(2,1)S(1)} %add_convert_fusion.1), channel_id=1, source_target_pairs={{0,4},{4,0},{8,12},{12,8},{1,5},{5,1},{9,13},{13,9},{2,6},{6,2},{1... | collective-permute-start | bytes 221192 | tf_op jit(solution)/shard_map/ppermute | solution.py:100
  94.7 3.1 %collective-permute-done.11 = bf16[9,32,128]{2,1,0:T(8,128)(2,1)S(1)} collective-permute-done((bf16[9,32,128]{2,1,0:T(8,128)(2,1)S(1)}, bf16[9,32,128]{2,1,0:T(8,128)(2,1)S(1)}, u32[]{:S(2)}, u32[]{:S(2)}) %collective-permute-start.11) | collective-permute-done | bytes 73760 | tf_op jit(solution)/shard_map/ppermute | solution.py:100
  97.8 2.1 %collective-permute-start.12 = (bf16[9,32,128]{2,1,0:T(8,128)(2,1)S(1)}, bf16[9,32,128]{2,1,0:T(8,128)(2,1)S(1)}, u32[]{:S(2)}, u32[]{:S(2)}) collective-permute-start(bf16[9,32,128]{2,1,0:T(8,128)(2,1)S(1)} %add_convert_fusion), channel_id=1, source_target_pairs={{0,8},{4,12},{8,0},{12,4},{1,9},{5,13},{9,1},{13,5},{2,10},{6,14},... | collective-permute-start | bytes 221192 | tf_op jit(solution)/shard_map/ppermute | solution.py:100
  99.9 3.3 %collective-permute-done.12 = bf16[9,32,128]{2,1,0:T(8,128)(2,1)S(1)} collective-permute-done((bf16[9,32,128]{2,1,0:T(8,128)(2,1)S(1)}, bf16[9,32,128]{2,1,0:T(8,128)(2,1)S(1)}, u32[]{:S(2)}, u32[]{:S(2)}) %collective-permute-start.12) | collective-permute-done | bytes 73760 | tf_op jit(solution)/shard_map/ppermute | solution.py:100
  103.2 2.0 %all_gather.7 = f32[9,64,128]{2,1,0:T(8,128)S(1)} all-gather(f32[9,32,128]{2,1,0:T(8,128)S(1)} %add_multiply_fusion), channel_id=1, replica_groups=mesh['groups'=2,'row'=4,'col'=2,'chan'=2] {'chan'}, dimensions={1}, use_global_device_ids=true | all-gather | bytes 442368 | tf_op jit(solution)/shard_map/all_gather | solution.py:170
  (79 shorter events, 19.7 us)
Async XLA Ops:
  0.6 48.9 %copy-start = (bf16[64,64,3,3]{1,0,3,2:T(8,128)(2,1)S(1)}, bf16[64,64,3,3]{1,0,3,2:T(8,128)(2,1)}, u32[]{:S(2)}) copy-start(bf16[64,64,3,3]{1,0,3,2:T(8,128)(2,1)} %param.11) | copy-start | bytes 221188
  0.6 12.3 %copy-start.1 = (bf16[2,64,8,128]{3,2,1,0:T(8,128)(2,1)S(1)}, bf16[2,64,8,128]{3,2,1,0:T(8,128)(2,1)}, u32[]{:S(2)}) copy-start(bf16[2,64,8,128]{3,2,1,0:T(8,128)(2,1)} %param.6) | copy-start | bytes 786436
  2.2 11.7 %copy-start.3 = (bf16[32,8,128]{2,1,0:T(8,128)(2,1)}, bf16[32,8,128]{2,1,0:T(8,128)(2,1)S(1)}, u32[]{:S(2)}) copy-start(bf16[32,8,128]{2,1,0:T(8,128)(2,1)S(1)} %get-tuple-element.46.own_ref) | copy-start | bytes 196612
  2.2 12.4 %collective-permute-start = (bf16[32,8,128]{2,1,0:T(8,128)(2,1)S(1)}, bf16[32,8,128]{2,1,0:T(8,128)(2,1)S(1)}, u32[]{:S(2)}, u32[]{:S(2)}) collective-permute-start(bf16[32,8,128]{2,1,0:T(8,128)(2,1)S(1)} %get-tuple-element.46.own_ref), channel_id=1, source_target_pairs={{0,4},{4,8},{8,12},{1,5},{5,9},{9,13},{2,6},{6,10},{10,14},{3,7},{... | collective-permute-start | bytes 196616 | tf_op jit(solution)/shard_map/ppermute | solution.py:17
  7.2 7.4 %collective-permute-start.1 = (bf16[32,8,128]{2,1,0:T(8,128)(2,1)S(1)}, bf16[32,8,128]{2,1,0:T(8,128)(2,1)S(1)}, u32[]{:S(2)}, u32[]{:S(2)}) collective-permute-start(bf16[32,8,128]{2,1,0:T(8,128)(2,1)S(1)} %get-tuple-element.46.own_ref), channel_id=1, source_target_pairs={{0,8},{4,12},{1,9},{5,13},{2,10},{6,14},{3,11},{7,15},{16,24},{20,... | collective-permute-start | bytes 196616 | tf_op jit(solution)/shard_map/ppermute | solution.py:17
  11.7 3.2 %collective-permute-start.2 = (bf16[32,8,128]{2,1,0:T(8,128)(2,1)S(1)}, bf16[32,8,128]{2,1,0:T(8,128)(2,1)S(1)}, u32[]{:S(2)}, u32[]{:S(2)}) collective-permute-start(bf16[32,8,128]{2,1,0:T(8,128)(2,1)S(1)} %get-tuple-element.46.own_ref), channel_id=1, source_target_pairs={{0,12},{1,13},{2,14},{3,15},{16,28},{17,29},{18,30},{19,31}} | collective-permute-start | bytes 196616 | tf_op jit(solution)/shard_map/ppermute | solution.py:17
  14.6 0.6 copy-start.6
  14.6 0.6 copy-start.7
  14.9 0.6 copy-start.8
  28.4 6.8 %collective-permute-start.3 = (bf16[32,8,128]{2,1,0:T(8,128)(2,1)}, bf16[32,8,128]{2,1,0:T(8,128)(2,1)S(1)}, u32[]{:S(2)}, u32[]{:S(2)}) collective-permute-start(bf16[32,8,128]{2,1,0:T(8,128)(2,1)} %get-tuple-element.10), channel_id=1, source_target_pairs={{4,0},{8,4},{12,8},{5,1},{9,5},{13,9},{6,2},{10,6},{14,10},{7,3},{... | collective-permute-start | bytes 196616 | tf_op jit(solution)/shard_map/ppermute | solution.py:17
  29.7 8.0 %collective-permute-start.4 = (bf16[32,8,128]{2,1,0:T(8,128)(2,1)}, bf16[32,8,128]{2,1,0:T(8,128)(2,1)S(1)}, u32[]{:S(2)}, u32[]{:S(2)}) collective-permute-start(bf16[32,8,128]{2,1,0:T(8,128)(2,1)} %get-tuple-element.11), channel_id=1, source_target_pairs={{8,0},{12,4},{9,1},{13,5},{10,2},{14,6},{11,3},{15,7},{24,16},{28,... | collective-permute-start | bytes 196616 | tf_op jit(solution)/shard_map/ppermute | solution.py:17
  31.0 9.5 %copy-start.5 = (f32[32,8,128]{2,1,0:T(8,128)S(1)}, f32[32,8,128]{2,1,0:T(8,128)}, u32[]{:S(2)}) copy-start(f32[32,8,128]{2,1,0:T(8,128)} %get-tuple-element.9) | copy-start | bytes 393220
  31.0 9.5 %collective-permute-start.5 = (bf16[32,8,128]{2,1,0:T(8,128)(2,1)}, bf16[32,8,128]{2,1,0:T(8,128)(2,1)S(1)}, u32[]{:S(2)}, u32[]{:S(2)}) collective-permute-start(bf16[32,8,128]{2,1,0:T(8,128)(2,1)} %get-tuple-element.12), channel_id=1, source_target_pairs={{12,0},{13,1},{14,2},{15,3},{28,16},{29,17},{30,18},{31,19}} | collective-permute-start | bytes 196616 | tf_op jit(solution)/shard_map/ppermute | solution.py:17
  40.5 0.8 copy-start.9
  41.3 2.0 %copy-start.2 = (bf16[2,32,8,128]{3,2,1,0:T(8,128)(2,1)}, bf16[2,32,8,128]{3,2,1,0:T(8,128)(2,1)S(1)}, u32[]{:S(2)}) copy-start(bf16[2,32,8,128]{3,2,1,0:T(8,128)(2,1)S(1)} %pad_maximum_fusion.23) | copy-start | bytes 393220
  43.6 15.9 %collective-permute-start.7 = (bf16[2,128,8,1]{3,2,1,0:T(8,128)(2,1)S(1)}, bf16[2,128,8,1]{3,2,1,0:T(8,128)(2,1)S(1)}, u32[]{:S(2)}, u32[]{:S(2)}) collective-permute-start(bf16[2,128,8,1]{3,2,1,0:T(8,128)(2,1)S(1)} %get-tuple-element.43), channel_id=1, source_target_pairs={{4,0},{8,4},{12,8},{5,1},{9,5},{13,9},{6,2},{10,6},{14,10},{7,3},{... | collective-permute-start | bytes 12296 | tf_op jit(solution)/shard_map/ppermute | solution.py:28
  44.9 15.7 %collective-permute-start.6 = (bf16[2,128,8,1]{3,2,1,0:T(8,128)(2,1)S(1)}, bf16[2,128,8,1]{3,2,1,0:T(8,128)(2,1)S(1)}, u32[]{:S(2)}, u32[]{:S(2)}) collective-permute-start(bf16[2,128,8,1]{3,2,1,0:T(8,128)(2,1)S(1)} %get-tuple-element.42), channel_id=1, source_target_pairs={{0,4},{4,8},{8,12},{1,5},{5,9},{9,13},{2,6},{6,10},{10,14},{3,7},{... | collective-permute-start | bytes 12296 | tf_op jit(solution)/shard_map/ppermute | solution.py:27
  62.0 14.5 %collective-permute-start.8 = (bf16[2,128,1,130]{3,2,1,0:T(2,128)(2,1)S(1)}, bf16[2,128,1,130]{3,2,1,0:T(2,128)(2,1)S(1)}, u32[]{:S(2)}, u32[]{:S(2)}) collective-permute-start(bf16[2,128,1,130]{3,2,1,0:T(2,128)(2,1)S(1)} %get-tuple-element.27), channel_id=1, source_target_pairs={{0,2},{1,3},{4,6},{5,7},{8,10},{9,11},{12,14},{13,15},{16,18},{17,... | collective-permute-start | bytes 199688 | tf_op jit(solution)/shard_map/ppermute | solution.py:27
  65.4 8.8 %collective-permute-start.9 = (bf16[2,128,1,130]{3,2,1,0:T(2,128)(2,1)S(1)}, bf16[2,128,1,130]{3,2,1,0:T(2,128)(2,1)S(1)}, u32[]{:S(2)}, u32[]{:S(2)}) collective-permute-start(bf16[2,128,1,130]{3,2,1,0:T(2,128)(2,1)S(1)} %get-tuple-element.28), channel_id=1, source_target_pairs={{2,0},{3,1},{6,4},{7,5},{10,8},{11,9},{14,12},{15,13},{18,16},{19,... | collective-permute-start | bytes 199688 | tf_op jit(solution)/shard_map/ppermute | solution.py:28
  76.5 1.6 %copy-start.4 = (bf16[64,64,3,3]{1,0,3,2:T(8,128)(2,1)S(1)}, bf16[64,64,3,3]{1,0,3,2:T(8,128)(2,1)}, u32[]{:S(2)}) copy-start(bf16[64,64,3,3]{1,0,3,2:T(8,128)(2,1)} %param.10) | copy-start | bytes 221188
  87.6 4.4 %collective-permute-start.10 = (bf16[9,32,128]{2,1,0:T(8,128)(2,1)S(1)}, bf16[9,32,128]{2,1,0:T(8,128)(2,1)S(1)}, u32[]{:S(2)}, u32[]{:S(2)}) collective-permute-start(bf16[9,32,128]{2,1,0:T(8,128)(2,1)S(1)} %pad_maximum_fusion.24), channel_id=1, source_target_pairs={{0,2},{2,0},{1,3},{3,1},{4,6},{6,4},{5,7},{7,5},{8,10},{10,8},{9,1... | collective-permute-start | bytes 221192 | tf_op jit(solution)/shard_map/ppermute | solution.py:100
  92.2 5.6 %collective-permute-start.11 = (bf16[9,32,128]{2,1,0:T(8,128)(2,1)S(1)}, bf16[9,32,128]{2,1,0:T(8,128)(2,1)S(1)}, u32[]{:S(2)}, u32[]{:S(2)}) collective-permute-start(bf16[9,32,128]{2,1,0:T(8,128)(2,1)S(1)} %add_convert_fusion.1), channel_id=1, source_target_pairs={{0,4},{4,0},{8,12},{12,8},{1,5},{5,1},{9,13},{13,9},{2,6},{6,2},{1... | collective-permute-start | bytes 221192 | tf_op jit(solution)/shard_map/ppermute | solution.py:100
  97.8 5.3 %collective-permute-start.12 = (bf16[9,32,128]{2,1,0:T(8,128)(2,1)S(1)}, bf16[9,32,128]{2,1,0:T(8,128)(2,1)S(1)}, u32[]{:S(2)}, u32[]{:S(2)}) collective-permute-start(bf16[9,32,128]{2,1,0:T(8,128)(2,1)S(1)} %add_convert_fusion), channel_id=1, source_target_pairs={{0,8},{4,12},{8,0},{12,4},{1,9},{5,13},{9,1},{13,5},{2,10},{6,14},... | collective-permute-start | bytes 221192 | tf_op jit(solution)/shard_map/ppermute | solution.py:100

commit v2 on v1

v2 whole, which is shorter than its diff:
```python
import functools
import math

import jax
import jax.numpy as jnp
from jax import lax
from jax.experimental import pallas as pl
from jax.experimental.pallas import tpu as pltpu
from jax.sharding import PartitionSpec as P

DISP = 40
MAXOFF = 2
F32 = jnp.float32
BF16 = jnp.bfloat16
SPACE = 12 << 20


def call(kernel, outs, *args, smem=0, scratch=(), flops=1 << 20, name=None):
    whole = pl.BlockSpec(memory_space=pltpu.VMEM)
    return pl.pallas_call(
        kernel,
        in_specs=[pl.BlockSpec(memory_space=pltpu.SMEM)] * smem + [whole] * (len(args) - smem),
        out_specs=[whole] * len(outs),
        out_shape=[jax.ShapeDtypeStruct(s, t) for s, t in outs],
        scratch_shapes=list(scratch),
        compiler_params=pltpu.CompilerParams(vmem_limit_bytes=SPACE),
        cost_estimate=pl.CostEstimate(flops=flops, bytes_accessed=1 << 20, transcendentals=0),
        name=name,
    )(*args)


def moved(block, axis, *distances):
    peers = lax.axis_size(axis)
    route = [(i - d, i) for d in distances for i in range(peers) if 0 <= i - d < peers]
    return lax.ppermute(block, axis, route)


def tap(rows, b, before, after):
    if b == 1:
        return rows
    lane = lax.broadcasted_iota(jnp.int32, rows.shape, 1)
    last = rows.shape[1] - 1
    if b == 0:
        return jnp.where(lane == 0, jnp.broadcast_to(before, rows.shape), pltpu.roll(rows, 1, 1))
    return jnp.where(lane == last, jnp.broadcast_to(after, rows.shape), pltpu.roll(rows, last, 1))


def nt(a, b):
    return lax.dot_general(a, b, (((1,), (1,)), ((), ())), preferred_element_type=F32)


def pack_kernel(layer_ref, features_ref, up_ref, down_ref):
    images, channels, tile_w, block_rows = layer_ref.shape
    local_ch = features_ref.shape[1]
    shape = (tile_w, block_rows)
    lane = lax.broadcasted_iota(jnp.int32, shape, 1)
    first = jnp.zeros(shape, F32)
    last = jnp.zeros(shape, F32)
    for n in range(images):
        for c in range(channels):
            tile = layer_ref[n, c].astype(F32)
            here = lane == n * channels + c
            first = jnp.where(here, jnp.broadcast_to(tile[:, :1], shape), first)
            last = jnp.where(here, jnp.broadcast_to(tile[:, block_rows - 1 :], shape), last)
    right = features_ref[1]
    up_ref[:local_ch] = right
    up_ref[local_ch] = last.astype(BF16)
    down_ref[:local_ch] = right
    down_ref[local_ch] = first.astype(BF16)


def correlation_kernel(merged, offset_ref, features_ref, one_ref, two_ref, three_ref, target_ref,
                       left_out, own_out, one_out, two_out, three_out, minus_out, moved_ref, residual_ref):
    offset = offset_ref[0, 0]
    row = lax.axis_index("row")
    local_ch, tile_w, block_rows = features_ref.shape[1:]
    groups = target_ref.shape[0]
    size = local_ch // groups
    inv_size = 1.0 / size
    shape = (tile_w, block_rows)
    lane = lax.broadcasted_iota(jnp.int32, shape, 1)
    zero = jnp.zeros(shape, F32)
    low_three = row <= MAXOFF

    def column(tile, at, kind, c, into):
        picked = jnp.broadcast_to(tile[:, at : at + 1], shape)
        return jnp.where(lane == kind * local_ch + c, picked, into)

    def one_group(g, edges):
        end_main, end_spill, start_main, end_left, start_left = edges
        base = g * size

        def scaled_left(c):
            return features_ref[0, base + c].astype(F32) * inv_size

        left, main, spill = [], [], []
        for c in range(size):
            own = features_ref[1, base + c].astype(F32)
            one, two, three = (r[base + c].astype(F32) for r in (one_ref, two_ref, three_ref))
            if merged:
                three = jnp.where(low_three, 0.0, three)
            left.append(scaled_left(c))
            main.append(jnp.where(offset == 0, own, jnp.where(offset == 1, one, two)))
            spill.append(jnp.where(offset == 0, one, jnp.where(offset == 1, two, three)))
        for d in range(DISP):
            products = []
            for c in range(size):
                moved = main[c]
                if d:
                    moved = pltpu.roll(jnp.where(lane >= block_rows - d, spill[c], moved), d, 1)
                moved_ref[d, c] = moved
                products.append(left[c] * moved)
            while len(products) > 1:
                products = [sum(products[i : i + 2]) for i in range(0, len(products), 2)]
            residual_ref[d] = products[0] - target_ref[g, d].astype(F32)
        for first in range(0, size, 2):
            channels = range(first, min(first + 2, size))
            left_grad = {c: zero for c in channels}
            whole_grad = {c: zero for c in channels}
            spill_grad = {c: zero for c in channels}
            scaled = {c: scaled_left(c) for c in channels}
            for d in range(DISP):
                residual = residual_ref[d]
                for c in channels:
                    left_grad[c] = left_grad[c] + residual * moved_ref[d, c]
                    part = residual * scaled[c]
                    if d:
                        part = pltpu.roll(part, block_rows - d, 1)
                        spill_grad[c] = spill_grad[c] + jnp.where(lane >= block_rows - d, part, 0.0)
                    whole_grad[c] = whole_grad[c] + part
            for c in channels:
                ch = base + c
                main_grad = whole_grad[c] - spill_grad[c]
                final = (left_grad[c] * inv_size).astype(BF16)
                left_out[ch] = final
                final = final.astype(F32)
                own_out[ch] = jnp.where(offset == 0, main_grad, 0.0)
                one_out[ch] = jnp.where(
                    offset == 0, spill_grad[c], jnp.where(offset == 1, main_grad, 0.0)
                ).astype(BF16)
                two_out[ch] = jnp.where(
                    offset == 1, spill_grad[c], jnp.where(offset == 2, main_grad, 0.0)
                ).astype(BF16)
                far = offset == 2
                if merged:
                    far = jnp.logical_and(far, jnp.logical_not(low_three))
                three_out[ch] = jnp.where(far, spill_grad[c], 0.0).astype(BF16)
                end_main = column(main_grad, block_rows - 1, 0, ch, end_main)
                end_spill = column(spill_grad[c], block_rows - 1, 0, ch, end_spill)
                start_main = column(main_grad, 0, 1, ch, start_main)
                end_left = column(final, block_rows - 1, 2, ch, end_left)
                start_left = column(final, 0, 3, ch, start_left)
        return end_main, end_spill, start_main, end_left, start_left

    end_main, end_spill, start_main, end_left, start_left = lax.fori_loop(
        0, groups, one_group, (zero,) * 5
    )

    def edges(k):
        tile = jnp.where(offset == k + 1, end_main, 0.0) + jnp.where(offset == k, end_spill, 0.0)
        tile = tile + jnp.where(offset == k - 1, start_main, 0.0)
        return tile + (end_left if k == -1 else start_left if k == 1 else 0.0)

    own_out[local_ch] = edges(0)
    one_out[local_ch] = edges(1).astype(BF16)
    two_out[local_ch] = edges(2).astype(BF16)
    if merged:
        three_out[local_ch] = jnp.where(low_three, edges(-1), edges(3)).astype(BF16)
    else:
        three_out[local_ch] = edges(3).astype(BF16)
    minus_out[0] = edges(-1).astype(BF16)


def hidden_kernel(layer_ref, before_ref, after_ref, weight_ref, slab_ref, hidden_ref, wide_ref):
    images, channels, tile_w, block_rows = layer_ref.shape
    wide_ref[...] = layer_ref[...].astype(F32).reshape(wide_ref.shape)
    last_row = lax.axis_index("row") == lax.axis_size("row") - 1
    local_ch = before_ref.shape[0] - 1
    before = before_ref[local_ch].astype(F32).T
    after = jnp.where(last_row, 0.0, after_ref[local_ch].astype(F32)).T
    for x in range(tile_w):
        for n in range(images):
            rows = wide_ref[pl.ds(n * channels * tile_w + x, channels, stride=tile_w), :]
            part = slice(n * channels, (n + 1) * channels)
            for b in range(3):
                slab_ref[x, b * channels : (b + 1) * channels, n * block_rows : (n + 1) * block_rows] = tap(
                    rows, b, before[part, x : x + 1], after[part, x : x + 1]
                ).astype(BF16)
    weights = first_weights(weight_ref)
    for x in range(1, tile_w - 1):
        hidden_ref[x] = hidden_row(weights, [slab_ref[x + a - 1] for a in range(3)])


def first_weights(weight_ref):
    return [jnp.concatenate([weight_ref[a, b] for b in range(3)], axis=1) for a in range(3)]


def hidden_row(weights, slabs):
    total = None
    for w, s in zip(weights, slabs):
        product = jnp.dot(w, s, preferred_element_type=F32)
        total = product if total is None else total + product
    return jnp.maximum(total, 0.0).astype(BF16)


def combine_kernel(swap, left_ref, own_ref, one_ref, two_ref, three_ref, minus_ref, layer_ref, before_ref, after_ref,
                   grad_ref, edge_ref, *rest):
    sends, (wide_ref, layer_wide, small_ref) = rest[:-3], rest[-3:]
    images, channels, tile_w, block_rows = layer_ref.shape
    local_ch = left_ref.shape[0]
    rows = local_ch * tile_w
    shape = (rows, block_rows)
    left = left_ref[...]
    right = own_ref[...] + one_ref[...].astype(F32) + two_ref[...].astype(F32) + three_ref[...].astype(F32)
    edge = right[local_ch] + minus_ref[0].astype(F32)
    outside = lax.broadcasted_iota(jnp.int32, edge.shape, 1) < jnp.where(lax.axis_index("row") == 0, local_ch, 0)
    edge = jnp.where(outside, 0.0, edge)
    right = right[:local_ch].astype(BF16)
    grad_ref[0] = left
    grad_ref[1] = right
    edge_ref[...] = edge
    wide_ref[:rows] = left.astype(F32).reshape(shape)
    wide_ref[rows:] = right.astype(F32).reshape(shape)
    layer_wide[...] = layer_ref[...].astype(F32).reshape(layer_wide.shape)
    last_row = lax.axis_index("row") == lax.axis_size("row") - 1
    small_ref[0] = before_ref[local_ch].astype(F32)
    small_ref[1] = jnp.where(last_row, 0.0, after_ref[local_ch].astype(F32))
    small_ref[2] = edge
    col = lax.axis_index("col")
    picks = [jnp.where(col == 0, tile_w - 1, 0)] if swap else [tile_w - 1, 0]
    all_in, all_grad = (images * channels, images * local_ch)
    spare = sends[0].shape[0] - all_in - all_grad
    sub = lax.broadcasted_iota(jnp.int32, (spare, block_rows), 0)
    for x, send_ref in zip(picks, sends):
        send_ref[:all_in] = layer_wide[pl.ds(x, all_in, stride=tile_w), :].astype(BF16)
        send_ref[all_in : all_in + all_grad] = wide_ref[pl.ds(x, all_grad, stride=tile_w), :].astype(BF16)
        corners = jnp.zeros((spare, block_rows), F32)
        for j in range(3):
            line = small_ref[j, pl.ds(x, 1), :]
            corners = jnp.where(sub == j, jnp.broadcast_to(line, corners.shape), corners)
        send_ref[all_in + all_grad :] = corners.astype(BF16)


def second_weights(weight_ref, chan, local_ch):
    first = pl.multiple_of(chan * local_ch, local_ch)
    result = []
    for a in range(3):
        parts = []
        for b in range(3):
            w = weight_ref[2 - a, 2 - b, pl.ds(first, local_ch), :].astype(F32)
            half = w.shape[1] // 2
            parts.append(jnp.where(chan == 0, w, jnp.concatenate([w[:, half:], w[:, :half]], axis=1)))
        result.append(jnp.concatenate(parts, axis=0).T.astype(BF16))
    return result


def edge_columns(edge, local_ch, n):
    at = (2, 3) if n == 0 else (0, 1)
    return tuple(edge[k * local_ch : (k + 1) * local_ch] for k in at)


def inner_kernel(grad_ref, edge_ref, hidden_ref, weight_ref, slab_ref, mine_ref, other_ref, second_ref, wide_ref):
    images, local_ch, tile_w, block_rows = grad_ref.shape
    wide_ref[...] = grad_ref[...].astype(F32).reshape(wide_ref.shape)
    edge = edge_ref[...].T
    for x in range(tile_w):
        for n in range(images):
            rows = wide_ref[pl.ds(n * local_ch * tile_w + x, local_ch, stride=tile_w), :]
            before, after = edge_columns(edge, local_ch, n)
            for b in range(3):
                slab_ref[x, b * local_ch : (b + 1) * local_ch, n * block_rows : (n + 1) * block_rows] = tap(
                    rows, b, before[:, x : x + 1], after[:, x : x + 1]
                ).astype(BF16)
    weights = second_weights(weight_ref, lax.axis_index("chan"), local_ch)
    sums = [None] * 3
    for x in range(1, tile_w - 1):
        total = None
        for a in range(3):
            slab = slab_ref[x + a - 1]
            product = jnp.dot(weights[a], slab, preferred_element_type=F32)
            total = product if total is None else total + product
            product = nt(slab, hidden_ref[x])
            sums[a] = product if sums[a] is None else sums[a] + product
        mine_ref[x] = total[:local_ch]
        other_ref[x] = total[local_ch:].astype(BF16)
    for a in range(3):
        second_ref[a] = sums[a]


def outer_kernel(before_ref, after_ref, layer_slab, grad_slab, hidden_ref, w_first_ref, w_second_ref,
                 inner_mine, inner_other, inner_second,
                 layer_edge, hidden_edge, mine_ref, other_ref, second_ref, grad_edge):
    tile_w, triple, lanes = layer_slab.shape
    channels = triple // 3
    local_ch = grad_slab.shape[1] // 3
    images = 2
    block_rows = lanes // images
    all_in, all_grad = (images * channels, images * local_ch)
    col = lax.axis_index("col")
    present = (col > 0, col < lax.axis_size("col") - 1)
    for side, (ref, ok) in enumerate(zip((before_ref, after_ref), present)):
        block = jnp.where(ok, ref[...].astype(F32), 0.0)
        corners = block[all_in + all_grad : all_in + all_grad + 8].T
        edge = corners[:, 2:3]
        for n in range(images):
            lanes_here = slice(n * block_rows, (n + 1) * block_rows)
            part = slice(n * channels, (n + 1) * channels)
            for b in range(3):
                layer_edge[side, b * channels : (b + 1) * channels, lanes_here] = tap(
                    block[part], b, corners[part, 0:1], corners[part, 1:2]
                ).astype(BF16)
            rows = block[all_in + n * local_ch : all_in + (n + 1) * local_ch]
            before, after = edge_columns(edge, local_ch, n)
            for b in range(3):
                grad_edge[side, b * local_ch : (b + 1) * local_ch, lanes_here] = tap(
                    rows, b, before, after
                ).astype(BF16)

    def at(own, halo, p):
        return halo[0] if p < 0 else halo[1] if p >= tile_w else own[p]

    first = first_weights(w_first_ref)
    second = second_weights(w_second_ref, lax.axis_index("chan"), local_ch)
    sums = [inner_second[a] for a in range(3)]
    mine_ref[...] = inner_mine[...]
    other_ref[...] = inner_other[...]
    for side, x in enumerate((0, tile_w - 1)):
        hidden = hidden_row(first, [at(layer_slab, layer_edge, x + a - 1) for a in range(3)])
        hidden_edge[side] = hidden
        total = None
        for a in range(3):
            slab = at(grad_slab, grad_edge, x + a - 1)
            product = jnp.dot(second[a], slab, preferred_element_type=F32)
            total = product if total is None else total + product
            sums[a] = sums[a] + nt(slab, hidden)
        mine_ref[x] = total[:local_ch]
        other_ref[x] = total[local_ch:].astype(BF16)
    for a in range(3):
        second_ref[a] = sums[a]


def first_kernel(mine_ref, arrived_ref, hidden_ref, hidden_edge, layer_slab, layer_edge, second_ref, out_ref):
    tile_w, local_ch, lanes = mine_ref.shape
    channels = layer_slab.shape[1] // 3
    first = pl.multiple_of(lax.axis_index("chan") * local_ch, local_ch)
    sums = [None] * 3
    for x in range(tile_w):
        if x == 0 or x == tile_w - 1:
            hidden = hidden_edge[0 if x == 0 else 1, pl.ds(first, local_ch), :]
        else:
            hidden = hidden_ref[x, pl.ds(first, local_ch), :]
        total = mine_ref[x] + arrived_ref[x].astype(F32)
        grad = jnp.where(hidden.astype(F32) > 0, total, 0.0).astype(BF16)
        for a in range(3):
            p = x + a - 1
            slab = layer_edge[0] if p < 0 else layer_edge[1] if p >= tile_w else layer_slab[p]
            product = nt(grad, slab)
            sums[a] = product if sums[a] is None else sums[a] + product
    for a in range(3):
        for b in range(3):
            one = sums[a][:, b * channels : (b + 1) * channels]
            two = second_ref[2 - a, (2 - b) * local_ch : (3 - b) * local_ch, :]
            out_ref[3 * a + b] = jnp.concatenate([one, two], axis=1).astype(out_ref.dtype)


def swapped(block, axis, step=1):
    return lax.ppermute(block, axis, [(i, i ^ step) for i in range(lax.axis_size(axis))])


def summed_over(partial, axis):
    peers = lax.axis_size(axis)
    step = 1
    while step < peers:
        rounded = lax.reduce_precision(partial, 8, 7)
        partial = rounded + swapped(rounded.astype(BF16), axis, step).astype(F32)
        step *= 2
    return partial


def body(layer_input, features, vol_target, offsets, w_first, w_second):
    images, channels, tile_w, block_rows = layer_input.shape
    local_ch = features.shape[1]
    groups = vol_target.shape[0]
    lanes = images * block_rows
    tile = (tile_w, block_rows)
    plain, framed = ((local_ch + k, *tile) for k in (0, 1))
    merged = lax.axis_size("row") == MAXOFF + 2
    swap = lax.axis_size("col") == 2
    w_first = w_first.transpose(2, 3, 0, 1)
    w_second = w_second.transpose(2, 3, 0, 1)

    up, down = call(pack_kernel, [(framed, BF16)] * 2, layer_input, features, name="pack")
    two = moved(features[1], "row", 2)
    if merged:
        three = below = moved(down, "row", MAXOFF + 1, -1)
    else:
        three = moved(features[1], "row", MAXOFF + 1)
        below = moved(down, "row", -1)
    one = moved(up, "row", 1)

    size = local_ch // groups
    left_grad, own, out_one, out_two, out_three, out_minus = call(
        functools.partial(correlation_kernel, merged),
        [(plain, BF16), (framed, F32)] + [(framed, BF16)] * 3 + [((1, *tile), BF16)],
        offsets, features, one, two, three, vol_target, smem=1, name="correlate", flops=1 << 26,
        scratch=[pltpu.VMEM((DISP, size, *tile), F32), pltpu.VMEM((DISP, *tile), F32)],
    )
    if merged:
        back_three = moved(out_three, "row", -MAXOFF - 1, 1)
        back_minus = jnp.zeros((1, *tile), BF16)
    else:
        back_three = moved(out_three, "row", -MAXOFF - 1)
        back_minus = moved(out_minus, "row", 1)
    back_one = moved(out_one, "row", -1)
    back_two = moved(out_two, "row", -2)

    slab_shape, hidden_shape = ((3 * channels, lanes), (channels, lanes))
    layer_slab, hidden = call(
        hidden_kernel, [((tile_w, *slab_shape), BF16), ((tile_w, *hidden_shape), BF16)],
        layer_input, one, below, w_first, name="hidden", flops=1 << 28,
        scratch=[pltpu.VMEM((images * channels * tile_w, block_rows), F32)],
    )
    message = ((images * (channels + local_ch) + 16, block_rows), BF16)
    grad_features, edge, *sends = call(
        functools.partial(combine_kernel, swap),
        [((images, *plain), BF16), (tile, F32)] + [message] * (1 if swap else 2),
        left_grad, own, back_one, back_two, back_three, back_minus, layer_input, one, below, name="combine",
        scratch=[pltpu.VMEM((images * local_ch * tile_w, block_rows), F32),
                 pltpu.VMEM((images * channels * tile_w, block_rows), F32),
                 pltpu.VMEM((3, *tile), F32)],
    )
    if swap:
        before = after = swapped(sends[0], "col")
    else:
        before, after = (moved(sends[0], "col", 1), moved(sends[1], "col", -1))
    half = (tile_w, local_ch, lanes)
    sums = (3, 3 * local_ch, channels)
    grad_slab, mine, other, second = call(
        inner_kernel, [((tile_w, 3 * local_ch, lanes), BF16), (half, F32), (half, BF16), (sums, F32)],
        grad_features, edge, hidden, w_second, name="inner", flops=1 << 28,
        scratch=[pltpu.VMEM((images * local_ch * tile_w, block_rows), F32)],
    )
    layer_edge, hidden_edge, mine, other, second = call(
        outer_kernel,
        [((2, *slab_shape), BF16), ((2, *hidden_shape), BF16), (half, F32), (half, BF16), (sums, F32)],
        before, after, layer_slab, grad_slab, hidden, w_first, w_second, mine, other, second, name="outer",
        flops=1 << 27, scratch=[pltpu.VMEM((2, 3 * local_ch, lanes), BF16)],
    )
    arrived = swapped(other, "chan")
    partial, = call(
        first_kernel, [((9, local_ch, 2 * channels), F32)],
        mine, arrived, hidden, hidden_edge, layer_slab, layer_edge, second, name="first", flops=1 << 27,
    )
    for axis in ("col", "row"):
        partial = summed_over(partial, axis)
    factor = 1.0 / math.sqrt(
        2.0 * tile_w * lax.axis_size("col") * block_rows * lax.axis_size("row")
    )
    both = lax.all_gather(partial * factor, "chan", axis=1, tiled=True)
    both = both.reshape(3, 3, channels, 2 * channels).transpose(2, 3, 0, 1)
    return (grad_features, both[:, :channels], both[:, channels:])


def solution(mesh):
    return jax.shard_map(
        body,
        mesh=mesh,
        in_specs=(
            P(None, None, ("groups", "col"), "row"),
            P(None, "chan", ("groups", "col"), "row"),
            P("chan", None, ("groups", "col"), "row"),
            P("row", ("groups", "col")),
            P(),
            P(),
        ),
        out_specs=(
            P(None, "chan", ("groups", "col"), "row"),
            P("groups", None, None, None),
            P("groups", None, None, None),
        ),
        check_vma=False,
    )
```

time: 107 us -> 56 us (0.52)
  waiting for transfers between devices: 36.5 us -> 22.1 us
  starting transfers between devices: 30.2 us -> 18.6 us
  matrix products: 9.04 us -> 0 us
  other arithmetic: 7.12 us -> 0.14 us
  Pallas kernels: 12.9 us -> 8.43 us
  blocking collectives: 4.01 us -> 2.02 us
  local copies, waits for them, and re-layouts: 4.55 us -> 2.96 us
    ppermute x13 -> x11, waiting for transfers between devices: 36.5 us -> 22.1 us  [the longest x5 14.9 us: swapped(): lax.ppermute(block, axis, [(i, i ^ step) for i in range(lax.axis_size(axi...]
    ppermute x13 -> x11, starting transfers between devices: 30.2 us -> 18.6 us  [the longest x6 15.4 us: moved(): return lax.ppermute(block, axis, route)]
    dot_general x36 -> x0, matrix products: 9.04 us -> none  [the longest x9 2.72 us: body(): jnp.einsum('oi,nixy->noxy', w_first[:, :, a, b], input_halo[:, :, a:a + t...]
    slice x3 -> x0, other arithmetic: 4.87 us -> none  [the longest x2 3.56 us: body(): view = grad_halo[:, :, 2 - a:2 - a + tile_w, 2 - b:2 - b + block_rows]]
    pallas_call x1 -> x7, Pallas kernels: 12.9 us -> 8.43 us  [call(): pl.pallas_call(kernel, in_specs=[pl.BlockSpec(memory_space=pltpu.SMEM)] *...]
    concatenate x4 -> x0, other arithmetic: 2.05 us -> none  [the longest x3 1.95 us: extended(): array = jnp.concatenate([before, array, after], axis=dim)]
    all_gather x1 -> x0, blocking collectives: 1.99 us -> none  [body(): grad_maps = lax.all_gather(grad_features, 'chan', axis=1, tiled=True)]
    squeeze x1, local copies, waits for them, and re-layouts: 1.56 us -> 0.01 us  [body(): two = moved(features[1], 'row', 2)]
  transfers between devices with their start and end apart: 13 -> 11, of which waited for: 10 -> 9; matrix products, arithmetic and copies ran while one was open for 4% -> 0% of each run, Pallas kernels for 0% -> 3%
where the time goes in v2:
time: 56 us; the launch traced here: 55.7 us
  waiting for transfers between devices  22.1 us (39%)
  starting transfers between devices  18.6 us (33%)
  Pallas kernels  8.43 us (15%)
  local copies, waits for them, and re-layouts  2.96 us (5%)
  blocking collectives  2.02 us (4%)
  between operations  1.44 us (3%)
    ppermute x6, starting transfers between devices, moved(): return lax.ppermute(block, axis, route)  15.4 us
    ppermute x5, waiting for transfers between devices, swapped(): lax.ppermute(block, axis, [(i, i ^ step) for i in range(lax.axis_size(axi...  14.9 us
    pallas_call x7, Pallas kernels, call(): pl.pallas_call(kernel, in_specs=[pl.BlockSpec(memory_space=pltpu.SMEM)] *...  8.43 us
    ppermute x6, waiting for transfers between devices, moved(): return lax.ppermute(block, axis, route)  7.19 us
    ppermute x5, starting transfers between devices, swapped(): lax.ppermute(block, axis, [(i, i ^ step) for i in range(lax.axis_size(axi...  3.26 us
    unnamed x16, local copies, waits for them, and re-layouts  2.06 us
    all_gather x1, blocking collectives, body(): both = lax.all_gather(partial * factor, 'chan', axis=1, tiled=True)  2.02 us
  transfers between devices with their start and end apart: 11, of which 9 were waited for; matrix products, arithmetic and copies ran while one was open for 0% of the time, Pallas kernels for 3%

profile of v2, /device:TPU:0, one launch (start us, length us, event | category | flops | bytes accessed | tf_op | source)
XLA Modules:
  0.0 55.7 jit_solution(2949456649298364290)
XLA Ops:
  0.6 0.9 %copy-done = bf16[2,64,8,128]{3,2,1,0:T(8,128)(2,1)S(1)} copy-done((bf16[2,64,8,128]{3,2,1,0:T(8,128)(2,1)S(1)}, bf16[2,64,8,128]{3,2,1,0:T(8,128)(2,1)}, u32[]{:S(2)}) %copy-start) | copy-done | bytes 262168
  1.6 0.9 %copy-done.2 = bf16[2,32,8,128]{3,2,1,0:T(8,128)(2,1)S(1)} copy-done((bf16[2,32,8,128]{3,2,1,0:T(8,128)(2,1)S(1)}, bf16[2,32,8,128]{3,2,1,0:T(8,128)(2,1)}, u32[]{:S(2)}) %copy-start.2) | copy-done | bytes 131096
  2.7 5.1 %collective-permute-start = (bf16[33,8,128]{2,1,0:T(8,128)(2,1)S(1)}, bf16[33,8,128]{2,1,0:T(8,128)(2,1)S(1)}, u32[]{:S(2)}, u32[]{:S(2)}) collective-permute-start(bf16[33,8,128]{2,1,0:T(8,128)(2,1)S(1)} %get-tuple-element.24), channel_id=1, source_target_pairs={{0,4},{4,8},{8,12},{1,5},{5,9},{9,13},{2,6},{6,10},{10,14},{3,7},{... | collective-permute-start | bytes 202760 | tf_op jit(solution)/shard_map/ppermute | solution.py:35
  7.8 1.5 %collective-permute-start.2 = (bf16[33,8,128]{2,1,0:T(8,128)(2,1)S(1)}, bf16[33,8,128]{2,1,0:T(8,128)(2,1)S(1)}, u32[]{:S(2)}, u32[]{:S(2)}) collective-permute-start(bf16[33,8,128]{2,1,0:T(8,128)(2,1)S(1)} %get-tuple-element.25), channel_id=1, source_target_pairs={{0,12},{4,0},{8,4},{12,8},{1,13},{5,1},{9,5},{13,9},{2,14},{6,2},{... | collective-permute-start | bytes 202760 | tf_op jit(solution)/shard_map/ppermute | solution.py:35
  9.3 3.5 %collective-permute-start.1 = (bf16[32,8,128]{2,1,0:T(8,128)(2,1)S(1)}, bf16[32,8,128]{2,1,0:T(8,128)(2,1)S(1)}, u32[]{:S(2)}, u32[]{:S(2)}) collective-permute-start(bf16[32,8,128]{2,1,0:T(8,128)(2,1)S(1)} %slice_bitcast_fusion), channel_id=1, source_target_pairs={{0,8},{4,12},{1,9},{5,13},{2,10},{6,14},{3,11},{7,15},{16,24},{20,... | collective-permute-start | bytes 196616 | tf_op jit(solution)/shard_map/ppermute | solution.py:35
  13.5 1.2 %collective-permute-done.1.two_ref = bf16[32,8,128]{2,1,0:T(8,128)(2,1)S(1)} collective-permute-done((bf16[32,8,128]{2,1,0:T(8,128)(2,1)S(1)}, bf16[32,8,128]{2,1,0:T(8,128)(2,1)S(1)}, u32[]{:S(2)}, u32[]{:S(2)}) %collective-permute-start.1) | collective-permute-done | bytes 65568 | tf_op jit(solution)/shard_map/ppermute | solution.py:35
  14.7 4.2 %correlate.1 = (bf16[32,8,128]{2,1,0:T(8,128)(2,1)S(1)}, f32[33,8,128]{2,1,0:T(8,128)S(1)}, bf16[33,8,128]{2,1,0:T(8,128)(2,1)S(1)}, bf16[33,8,128]{2,1,0:T(8,12...) custom-call(s32[1,1]{1,0:T(1,128)S(6)} %copy.9.offset_ref, ...), custom_call_target="tpu_custom_call" | custom-call | flops 67108864 | bytes 1048576 | tf_op jit(solution)/shard_map/correlate/pallas_call | solution.py:20
  18.9 1.3 %collective-permute-start.3 = (bf16[33,8,128]{2,1,0:T(8,128)(2,1)S(1)}, bf16[33,8,128]{2,1,0:T(8,128)(2,1)S(1)}, u32[]{:S(2)}, u32[]{:S(2)}) collective-permute-start(bf16[33,8,128]{2,1,0:T(8,128)(2,1)S(1)} %get-tuple-element.28), channel_id=1, source_target_pairs={{4,0},{8,4},{12,8},{5,1},{9,5},{13,9},{6,2},{10,6},{14,10},{7,3},{... | collective-permute-start | bytes 202760 | tf_op jit(solution)/shard_map/ppermute | solution.py:35
  20.2 1.3 %collective-permute-start.4 = (bf16[33,8,128]{2,1,0:T(8,128)(2,1)S(1)}, bf16[33,8,128]{2,1,0:T(8,128)(2,1)S(1)}, u32[]{:S(2)}, u32[]{:S(2)}) collective-permute-start(bf16[33,8,128]{2,1,0:T(8,128)(2,1)S(1)} %get-tuple-element.29), channel_id=1, source_target_pairs={{8,0},{12,4},{9,1},{13,5},{10,2},{14,6},{11,3},{15,7},{24,16},{28,... | collective-permute-start | bytes 202760 | tf_op jit(solution)/shard_map/ppermute | solution.py:35
  21.5 2.7 %collective-permute-start.5 = (bf16[33,8,128]{2,1,0:T(8,128)(2,1)S(1)}, bf16[33,8,128]{2,1,0:T(8,128)(2,1)S(1)}, u32[]{:S(2)}, u32[]{:S(2)}) collective-permute-start(bf16[33,8,128]{2,1,0:T(8,128)(2,1)S(1)} %get-tuple-element.30), channel_id=1, source_target_pairs={{12,0},{0,4},{4,8},{8,12},{13,1},{1,5},{5,9},{9,13},{14,2},{2,6},{... | collective-permute-start | bytes 202760 | tf_op jit(solution)/shard_map/ppermute | solution.py:35
  24.2 1.6 %collective-permute-done.3.one_ref = bf16[33,8,128]{2,1,0:T(8,128)(2,1)S(1)} collective-permute-done((bf16[33,8,128]{2,1,0:T(8,128)(2,1)S(1)}, bf16[33,8,128]{2,1,0:T(8,128)(2,1)S(1)}, u32[]{:S(2)}, u32[]{:S(2)}) %collective-permute-start.3) | collective-permute-done | bytes 67616 | tf_op jit(solution)/shard_map/ppermute | solution.py:35
  25.8 2.9 %collective-permute-done.4.two_ref = bf16[33,8,128]{2,1,0:T(8,128)(2,1)S(1)} collective-permute-done((bf16[33,8,128]{2,1,0:T(8,128)(2,1)S(1)}, bf16[33,8,128]{2,1,0:T(8,128)(2,1)S(1)}, u32[]{:S(2)}, u32[]{:S(2)}) %collective-permute-start.4) | collective-permute-done | bytes 67616 | tf_op jit(solution)/shard_map/ppermute | solution.py:35
  28.7 1.4 %collective-permute-done.5.three_ref = bf16[33,8,128]{2,1,0:T(8,128)(2,1)S(1)} collective-permute-done((bf16[33,8,128]{2,1,0:T(8,128)(2,1)S(1)}, bf16[33,8,128]{2,1,0:T(8,128)(2,1)S(1)}, u32[]{:S(2)}, u32[]{:S(2)}) %collective-permute-start.5) | collective-permute-done | bytes 67616 | tf_op jit(solution)/shard_map/ppermute | solution.py:35
  30.9 1.5 %collective-permute-start.6 = (bf16[208,128]{1,0:T(8,128)(2,1)S(1)}, bf16[208,128]{1,0:T(8,128)(2,1)S(1)}, u32[]{:S(2)}, u32[]{:S(2)}) collective-permute-start(bf16[208,128]{1,0:T(8,128)(2,1)S(1)} %get-tuple-element.32), channel_id=1, source_target_pairs={{0,2},{2,0},{1,3},{3,1},{4,6},{6,4},{5,7},{7,5},{8,10},{10,8},{9,1... | collective-permute-start | bytes 159752 | tf_op jit(solution)/shard_map/ppermute | solution.py:367
  34.1 0.9 %collective-permute-done.6.before_ref.after_ref = bf16[208,128]{1,0:T(8,128)(2,1)S(1)} collective-permute-done((bf16[208,128]{1,0:T(8,128)(2,1)S(1)}, bf16[208,128]{1,0:T(8,128)(2,1)S(1)}, u32[]{:S(2)}, u32[]{:S(2)}) %collective-permute-start.6) | collective-permute-done | bytes 53280 | tf_op jit(solution)/shard_map/ppermute | solution.py:367
  35.0 0.9 %outer.1 = (bf16[2,192,256]{2,1,0:T(8,128)(2,1)S(1)}, bf16[2,64,256]{2,1,0:T(8,128)(2,1)S(1)}, f32[8,32,256]{2,1,0:T(8,128)S(1)}, bf16[8,32,256]{2,1,0:T(8,128)(2,1)S(1)}, f32[3,96,64]{2,1,0:T(8,128)S(1)}) custom-call(bf16[208,128]{1,0:T(8,128)(2,1)S(1)} %collective-permute-done.6.before_ref.after_ref, ...), custom_call_target="tpu_custom_call" | custom-call | flops 134217728 | bytes 1048576 | tf_op jit(solution)/shard_map/outer/pallas_call | solution.py:20
  36.0 1.3 %collective-permute-done.7.arrived_ref = bf16[8,32,256]{2,1,0:T(8,128)(2,1)S(1)} collective-permute-done((bf16[8,32,256]{2,1,0:T(8,128)(2,1)S(1)}, bf16[8,32,256]{2,1,0:T(8,128)(2,1)S(1)}, u32[]{:S(2)}, u32[]{:S(2)}) %collective-permute-start.7) | collective-permute-done | bytes 131104 | tf_op jit(solution)/shard_map/ppermute | solution.py:367
  37.3 0.9 %first.1 = f32[9,32,128]{2,1,0:T(8,128)S(1)} custom-call(f32[8,32,256]{2,1,0:T(8,128)S(1)} %get-tuple-element.40.mine_ref, bf16[8,32,256]{2,1,0:T(8,128)(2,1)S(1)} %collective-permute-done.7.arrived_ref, bf16[8,64,256]{2,1,0:T(8,128)(2,1)S(1)} %get-tuple-element.35.hidden_ref, bf16[2,64,256]{2,1,0:T(8,128)(2,1)S(1)} %get-tuple-element.42.hidden_edge, ...), custom_call_target="tpu_custom_call" | custom-call | flops 134217728 | bytes 1048576 | tf_op jit(solution)/shard_map/first/pallas_call | solution.py:20
  38.3 1.6 %collective-permute-start.8 = (bf16[9,32,128]{2,1,0:T(8,128)(2,1)S(1)}, bf16[9,32,128]{2,1,0:T(8,128)(2,1)S(1)}, u32[]{:S(2)}, u32[]{:S(2)}) collective-permute-start(bf16[9,32,128]{2,1,0:T(8,128)(2,1)S(1)} %reduce-precision_convert_fusion), channel_id=1, source_target_pairs={{0,2},{2,0},{1,3},{3,1},{4,6},{6,4},{5,7},{7,5},{8,10},{10,8},{9,1... | collective-permute-start | bytes 221192 | tf_op jit(solution)/shard_map/ppermute | solution.py:367
  39.8 2.9 %collective-permute-done.8 = bf16[9,32,128]{2,1,0:T(8,128)(2,1)S(1)} collective-permute-done((bf16[9,32,128]{2,1,0:T(8,128)(2,1)S(1)}, bf16[9,32,128]{2,1,0:T(8,128)(2,1)S(1)}, u32[]{:S(2)}, u32[]{:S(2)}) %collective-permute-start.8) | collective-permute-done | bytes 73760 | tf_op jit(solution)/shard_map/ppermute | solution.py:367
  42.8 4.3 %collective-permute-done.9 = bf16[9,32,128]{2,1,0:T(8,128)(2,1)S(1)} collective-permute-done((bf16[9,32,128]{2,1,0:T(8,128)(2,1)S(1)}, bf16[9,32,128]{2,1,0:T(8,128)(2,1)S(1)}, u32[]{:S(2)}, u32[]{:S(2)}) %collective-permute-start.9) | collective-permute-done | bytes 73760 | tf_op jit(solution)/shard_map/ppermute | solution.py:367
  47.3 5.5 %collective-permute-done.10 = bf16[9,32,128]{2,1,0:T(8,128)(2,1)S(1)} collective-permute-done((bf16[9,32,128]{2,1,0:T(8,128)(2,1)S(1)}, bf16[9,32,128]{2,1,0:T(8,128)(2,1)S(1)}, u32[]{:S(2)}, u32[]{:S(2)}) %collective-permute-start.10) | collective-permute-done | bytes 73760 | tf_op jit(solution)/shard_map/ppermute | solution.py:367
  52.8 2.0 %all_gather.3 = f32[9,64,128]{2,1,0:T(8,128)S(1)} all-gather(f32[9,32,128]{2,1,0:T(8,128)S(1)} %add_multiply_fusion), channel_id=1, replica_groups=mesh['groups'=2,'row'=4,'col'=2,'chan'=2] {'chan'}, dimensions={1}, use_global_device_ids=true | all-gather | bytes 442368 | tf_op jit(solution)/shard_map/all_gather | solution.py:459
  54.8 0.9 %fusion.2 = (f32[64,64,3,3]{1,0,3,2:T(8,128)}, f32[64,64,3,3]{1,0,3,2:T(8,128)}) fusion(f32[64,128,3,3]{1,0,3,2:T(8,128)S(1)} %bitcast.11), kind=kLoop, calls=%fused_computation.7 | loop fusion | bytes 589824 | tf_op jit(solution)/shard_map/slice | solution.py:461
  (29 shorter events, 3.0 us)
Async XLA Ops:
  0.6 1.0 %copy-start = (bf16[2,64,8,128]{3,2,1,0:T(8,128)(2,1)S(1)}, bf16[2,64,8,128]{3,2,1,0:T(8,128)(2,1)}, u32[]{:S(2)}) copy-start(bf16[2,64,8,128]{3,2,1,0:T(8,128)(2,1)} %layer_ref.5) | copy-start | bytes 786436
  1.6 0.9 %copy-start.2 = (bf16[2,32,8,128]{3,2,1,0:T(8,128)(2,1)S(1)}, bf16[2,32,8,128]{3,2,1,0:T(8,128)(2,1)}, u32[]{:S(2)}) copy-start(bf16[2,32,8,128]{3,2,1,0:T(8,128)(2,1)} %features_ref.3) | copy-start | bytes 393220
  2.5 12.2 %copy-start.4 = (bf16[4,40,8,128]{3,2,1,0:T(8,128)(2,1)S(1)}, bf16[4,40,8,128]{3,2,1,0:T(8,128)(2,1)}, u32[]{:S(2)}) copy-start(bf16[4,40,8,128]{3,2,1,0:T(8,128)(2,1)} %target_ref.1) | copy-start | bytes 983044
  2.7 12.0 %copy-start.3 = (bf16[2,32,8,128]{3,2,1,0:T(8,128)(2,1)S(1)}, bf16[2,32,8,128]{3,2,1,0:T(8,128)(2,1)}, u32[]{:S(2)}) copy-start(bf16[2,32,8,128]{3,2,1,0:T(8,128)(2,1)} %features_ref.3) | copy-start | bytes 393220
  2.7 12.0 %collective-permute-start = (bf16[33,8,128]{2,1,0:T(8,128)(2,1)S(1)}, bf16[33,8,128]{2,1,0:T(8,128)(2,1)S(1)}, u32[]{:S(2)}, u32[]{:S(2)}) collective-permute-start(bf16[33,8,128]{2,1,0:T(8,128)(2,1)S(1)} %get-tuple-element.24), channel_id=1, source_target_pairs={{0,4},{4,8},{8,12},{1,5},{5,9},{9,13},{2,6},{6,10},{10,14},{3,7},{... | collective-permute-start | bytes 202760 | tf_op jit(solution)/shard_map/ppermute | solution.py:35
  7.8 6.9 %collective-permute-start.2 = (bf16[33,8,128]{2,1,0:T(8,128)(2,1)S(1)}, bf16[33,8,128]{2,1,0:T(8,128)(2,1)S(1)}, u32[]{:S(2)}, u32[]{:S(2)}) collective-permute-start(bf16[33,8,128]{2,1,0:T(8,128)(2,1)S(1)} %get-tuple-element.25), channel_id=1, source_target_pairs={{0,12},{4,0},{8,4},{12,8},{1,13},{5,1},{9,5},{13,9},{2,14},{6,2},{... | collective-permute-start | bytes 202760 | tf_op jit(solution)/shard_map/ppermute | solution.py:35
  9.3 5.4 %collective-permute-start.1 = (bf16[32,8,128]{2,1,0:T(8,128)(2,1)S(1)}, bf16[32,8,128]{2,1,0:T(8,128)(2,1)S(1)}, u32[]{:S(2)}, u32[]{:S(2)}) collective-permute-start(bf16[32,8,128]{2,1,0:T(8,128)(2,1)S(1)} %slice_bitcast_fusion), channel_id=1, source_target_pairs={{0,8},{4,12},{1,9},{5,13},{2,10},{6,14},{3,11},{7,15},{16,24},{20,... | collective-permute-start | bytes 196616 | tf_op jit(solution)/shard_map/ppermute | solution.py:35
  13.5 16.7 %copy-start.1 = (bf16[2,64,8,128]{3,2,1,0:T(8,128)(2,1)S(1)}, bf16[2,64,8,128]{3,2,1,0:T(8,128)(2,1)}, u32[]{:S(2)}) copy-start(bf16[2,64,8,128]{3,2,1,0:T(8,128)(2,1)} %layer_ref.5) | copy-start | bytes 786436
  18.9 6.9 %collective-permute-start.3 = (bf16[33,8,128]{2,1,0:T(8,128)(2,1)S(1)}, bf16[33,8,128]{2,1,0:T(8,128)(2,1)S(1)}, u32[]{:S(2)}, u32[]{:S(2)}) collective-permute-start(bf16[33,8,128]{2,1,0:T(8,128)(2,1)S(1)} %get-tuple-element.28), channel_id=1, source_target_pairs={{4,0},{8,4},{12,8},{5,1},{9,5},{13,9},{6,2},{10,6},{14,10},{7,3},{... | collective-permute-start | bytes 202760 | tf_op jit(solution)/shard_map/ppermute | solution.py:35
  20.2 8.5 %collective-permute-start.4 = (bf16[33,8,128]{2,1,0:T(8,128)(2,1)S(1)}, bf16[33,8,128]{2,1,0:T(8,128)(2,1)S(1)}, u32[]{:S(2)}, u32[]{:S(2)}) collective-permute-start(bf16[33,8,128]{2,1,0:T(8,128)(2,1)S(1)} %get-tuple-element.29), channel_id=1, source_target_pairs={{8,0},{12,4},{9,1},{13,5},{10,2},{14,6},{11,3},{15,7},{24,16},{28,... | collective-permute-start | bytes 202760 | tf_op jit(solution)/shard_map/ppermute | solution.py:35
  21.5 8.7 %collective-permute-start.5 = (bf16[33,8,128]{2,1,0:T(8,128)(2,1)S(1)}, bf16[33,8,128]{2,1,0:T(8,128)(2,1)S(1)}, u32[]{:S(2)}, u32[]{:S(2)}) collective-permute-start(bf16[33,8,128]{2,1,0:T(8,128)(2,1)S(1)} %get-tuple-element.30), channel_id=1, source_target_pairs={{12,0},{0,4},{4,8},{8,12},{13,1},{1,5},{5,9},{9,13},{14,2},{2,6},{... | collective-permute-start | bytes 202760 | tf_op jit(solution)/shard_map/ppermute | solution.py:35
  30.2 2.2 %copy-start.5 = (bf16[64,64,3,3]{1,0,3,2:T(8,128)(2,1)S(1)}, bf16[64,64,3,3]{1,0,3,2:T(8,128)(2,1)}, u32[]{:S(2)}) copy-start(bf16[64,64,3,3]{1,0,3,2:T(8,128)(2,1)} %param.10) | copy-start | bytes 221188
  30.9 4.1 %collective-permute-start.6 = (bf16[208,128]{1,0:T(8,128)(2,1)S(1)}, bf16[208,128]{1,0:T(8,128)(2,1)S(1)}, u32[]{:S(2)}, u32[]{:S(2)}) collective-permute-start(bf16[208,128]{1,0:T(8,128)(2,1)S(1)} %get-tuple-element.32), channel_id=1, source_target_pairs={{0,2},{2,0},{1,3},{3,1},{4,6},{6,4},{5,7},{7,5},{8,10},{10,8},{9,1... | collective-permute-start | bytes 159752 | tf_op jit(solution)/shard_map/ppermute | solution.py:367
  32.4 0.9 %copy-start.6 = (bf16[64,64,3,3]{1,0,3,2:T(8,128)(2,1)S(1)}, bf16[64,64,3,3]{1,0,3,2:T(8,128)(2,1)}, u32[]{:S(2)}) copy-start(bf16[64,64,3,3]{1,0,3,2:T(8,128)(2,1)} %param.11) | copy-start | bytes 221188
  32.4 1.0 %copy-start.7 = (bf16[2,32,8,128]{3,2,1,0:T(8,128)(2,1)S(1)}, bf16[2,32,8,128]{3,2,1,0:T(8,128)(2,1)}, u32[]{:S(2)}) copy-start(bf16[2,32,8,128]{3,2,1,0:T(8,128)(2,1)} %get-tuple-element.21.grad_ref) | copy-start | bytes 393220
  35.9 1.4 %collective-permute-start.7 = (bf16[8,32,256]{2,1,0:T(8,128)(2,1)S(1)}, bf16[8,32,256]{2,1,0:T(8,128)(2,1)S(1)}, u32[]{:S(2)}, u32[]{:S(2)}) collective-permute-start(bf16[8,32,256]{2,1,0:T(8,128)(2,1)S(1)} %get-tuple-element.41), channel_id=1, source_target_pairs={{0,1},{1,0},{2,3},{3,2},{4,5},{5,4},{6,7},{7,6},{8,9},{9,8},{10,11... | collective-permute-start | bytes 393224 | tf_op jit(solution)/shard_map/ppermute | solution.py:367
  38.3 4.4 %collective-permute-start.8 = (bf16[9,32,128]{2,1,0:T(8,128)(2,1)S(1)}, bf16[9,32,128]{2,1,0:T(8,128)(2,1)S(1)}, u32[]{:S(2)}, u32[]{:S(2)}) collective-permute-start(bf16[9,32,128]{2,1,0:T(8,128)(2,1)S(1)} %reduce-precision_convert_fusion), channel_id=1, source_target_pairs={{0,2},{2,0},{1,3},{3,1},{4,6},{6,4},{5,7},{7,5},{8,10},{10,8},{9,1... | collective-permute-start | bytes 221192 | tf_op jit(solution)/shard_map/ppermute | solution.py:367
  42.7 4.4 %collective-permute-start.9 = (bf16[9,32,128]{2,1,0:T(8,128)(2,1)S(1)}, bf16[9,32,128]{2,1,0:T(8,128)(2,1)S(1)}, u32[]{:S(2)}, u32[]{:S(2)}) collective-permute-start(bf16[9,32,128]{2,1,0:T(8,128)(2,1)S(1)} %fusion.1), channel_id=1, source_target_pairs={{0,4},{4,0},{8,12},{12,8},{1,5},{5,1},{9,13},{13,9},{2,6},{6,2},{1... | collective-permute-start | bytes 221192 | tf_op jit(solution)/shard_map/ppermute | solution.py:367
  47.2 5.5 %collective-permute-start.10 = (bf16[9,32,128]{2,1,0:T(8,128)(2,1)S(1)}, bf16[9,32,128]{2,1,0:T(8,128)(2,1)S(1)}, u32[]{:S(2)}, u32[]{:S(2)}) collective-permute-start(bf16[9,32,128]{2,1,0:T(8,128)(2,1)S(1)} %fusion), channel_id=1, source_target_pairs={{0,8},{4,12},{8,0},{12,4},{1,9},{5,13},{9,1},{13,5},{2,10},{6,14},... | collective-permute-start | bytes 221192 | tf_op jit(solution)/shard_map/ppermute | solution.py:367

commit v3 on v2

v3 whole, which is shorter than its diff:
```python
import functools
import math

import jax
import jax.numpy as jnp
from jax import lax
from jax.experimental import pallas as pl
from jax.experimental.pallas import tpu as pltpu
from jax.sharding import PartitionSpec as P


DISP = 40
MAXOFF = 2
F32 = jnp.float32
BF16 = jnp.bfloat16
SPACE = 12 << 20


def call(kernel, outs, *args, smem=0, far=False, scratch=(), flops=1 << 20):
    whole = pl.BlockSpec(memory_space=pltpu.VMEM)
    given = pl.BlockSpec(memory_space=pltpu.HBM) if far else whole
    return pl.pallas_call(
        kernel,
        in_specs=[pl.BlockSpec(memory_space=pltpu.SMEM)] * smem + [given] * (len(args) - smem),
        out_specs=[whole] * len(outs),
        out_shape=[jax.ShapeDtypeStruct(s, t) for s, t in outs],
        scratch_shapes=list(scratch),
        compiler_params=pltpu.CompilerParams(vmem_limit_bytes=SPACE),
        cost_estimate=pl.CostEstimate(flops=flops, bytes_accessed=1 << 20, transcendentals=0),
    )(*args)


def routes():
    peers = lax.axis_size("row")
    if peers == MAXOFF + 2 and peers & (peers - 1) == 0:
        return [("swap", mask) for mask in range(1, peers)]
    return [("line", k) for k in (*range(1, MAXOFF + 2), -1)]


def distance(route):
    kind, value = route
    if kind == "line":
        return value
    row = lax.axis_index("row")
    return row - (row ^ value)


def delivered(block, route, sign):
    kind, value = route
    if kind == "swap":
        return swapped(block, "row", value)
    return moved(block, "row", sign * value)


def moved(block, axis, distance):
    peers = lax.axis_size(axis)
    return lax.ppermute(block, axis, [(i - distance, i) for i in range(peers) if 0 <= i - distance < peers])


def tap(rows, b, before, after):
    if b == 1:
        return rows
    lane = lax.broadcasted_iota(jnp.int32, rows.shape, 1)
    last = rows.shape[1] - 1
    if b == 0:
        return jnp.where(lane == 0, jnp.broadcast_to(before, rows.shape), pltpu.roll(rows, 1, 1))
    return jnp.where(lane == last, jnp.broadcast_to(after, rows.shape), pltpu.roll(rows, last, 1))


def nt(a, b):
    return lax.dot_general(a, b, (((1,), (1,)), ((), ())), preferred_element_type=F32)


def fetch_kernel(*refs):
    count = len(refs) // 2
    sources, targets, sems = refs[:count], refs[count:-1], refs[-1]
    copies = [pltpu.make_async_copy(s, t, sems.at[i]) for i, (s, t) in enumerate(zip(sources, targets))]
    for copy in copies:
        copy.start()
    for copy in copies:
        copy.wait()


def pack_kernel(routing, layer_hbm, features_hbm, *rest):
    out_refs, (layer_ref, features_ref, sems) = rest[:-3], rest[-3:]
    images, channels, tile_w, block_rows = layer_ref.shape
    local_ch = features_ref.shape[0]
    copies = [pltpu.make_async_copy(features_hbm.at[1], features_ref, sems.at[images])]
    for n in range(images):
        copies.append(pltpu.make_async_copy(layer_hbm.at[n], layer_ref.at[n], sems.at[n]))
    for copy in copies:
        copy.start()
    for copy in copies:
        copy.wait()
    shape = (tile_w, block_rows)
    lane = lax.broadcasted_iota(jnp.int32, shape, 1)
    first = jnp.zeros(shape, F32)
    last = jnp.zeros(shape, F32)
    for n in range(images):
        for c in range(channels):
            tile = layer_ref[n, c].astype(F32)
            here = lane == n * channels + c
            first = jnp.where(here, jnp.broadcast_to(tile[:, :1], shape), first)
            last = jnp.where(here, jnp.broadcast_to(tile[:, block_rows - 1 :], shape), last)
    for route, out_ref in zip(routing, out_refs):
        ahead = distance(route) if route[0] == "line" else -distance(route)
        out_ref[:local_ch] = features_ref[...]
        out_ref[local_ch] = jnp.where(ahead == 1, last, jnp.where(ahead == -1, first, 0.0)).astype(BF16)


def correlation_kernel(routing, offset_ref, features_ref, target_ref, *rest):
    count = len(routing)
    block_refs, (left_out, own_out) = rest[:count], rest[count : count + 2]
    out_refs, (moved_ref, residual_ref) = rest[count + 2 : -2], rest[-2:]
    ahead = [distance(route) for route in routing]
    offset = offset_ref[0, 0]
    local_ch, tile_w, block_rows = features_ref.shape[1:]
    groups = target_ref.shape[0]
    size = local_ch // groups
    inv_size = 1.0 / size
    shape = (tile_w, block_rows)
    lane = lax.broadcasted_iota(jnp.int32, shape, 1)
    zero = jnp.zeros(shape, F32)

    def column(tile, at, kind, c, into):
        picked = jnp.broadcast_to(tile[:, at : at + 1], shape)
        return jnp.where(lane == kind * local_ch + c, picked, into)

    def one_group(g, edges):
        end_main, end_spill, start_main, end_left, start_left = edges
        base = g * size

        def scaled_left(c):
            return features_ref[0, base + c].astype(F32) * inv_size

        left, main, spill = [], [], []
        for c in range(size):
            here = features_ref[1, base + c].astype(F32)
            before = zero
            for k, block_ref in zip(ahead, block_refs):
                block = block_ref[base + c].astype(F32)
                here = jnp.where(k == offset, block, here)
                before = jnp.where(k == offset + 1, block, before)
            left.append(scaled_left(c))
            main.append(here)
            spill.append(before)
        for d in range(DISP):
            products = []
            for c in range(size):
                moved = main[c]
                if d:
                    moved = pltpu.roll(jnp.where(lane >= block_rows - d, spill[c], moved), d, 1)
                moved_ref[d, c] = moved
                products.append(left[c] * moved)
            while len(products) > 1:
                products = [sum(products[i : i + 2]) for i in range(0, len(products), 2)]
            residual_ref[d] = products[0] - target_ref[g, d].astype(F32)
        for first in range(0, size, 2):
            channels = range(first, min(first + 2, size))
            left_grad = {c: zero for c in channels}
            whole_grad = {c: zero for c in channels}
            spill_grad = {c: zero for c in channels}
            scaled = {c: scaled_left(c) for c in channels}
            for d in range(DISP):
                residual = residual_ref[d]
                for c in channels:
                    left_grad[c] = left_grad[c] + residual * moved_ref[d, c]
                    part = residual * scaled[c]
                    if d:
                        part = pltpu.roll(part, block_rows - d, 1)
                        spill_grad[c] = spill_grad[c] + jnp.where(lane >= block_rows - d, part, 0.0)
                    whole_grad[c] = whole_grad[c] + part
            for c in channels:
                ch = base + c
                main_grad = whole_grad[c] - spill_grad[c]
                final = (left_grad[c] * inv_size).astype(BF16)
                left_out[ch] = final
                final = final.astype(F32)
                own_out[ch] = jnp.where(offset == 0, main_grad, 0.0)
                for k, out_ref in zip(ahead, out_refs):
                    out_ref[ch] = jnp.where(
                        offset + 1 == k, spill_grad[c], jnp.where(offset == k, main_grad, 0.0)
                    ).astype(BF16)
                end_main = column(main_grad, block_rows - 1, 0, ch, end_main)
                end_spill = column(spill_grad[c], block_rows - 1, 0, ch, end_spill)
                start_main = column(main_grad, 0, 1, ch, start_main)
                end_left = column(final, block_rows - 1, 2, ch, end_left)
                start_left = column(final, 0, 3, ch, start_left)
        return end_main, end_spill, start_main, end_left, start_left

    end_main, end_spill, start_main, end_left, start_left = lax.fori_loop(
        0, groups, one_group, (zero,) * 5
    )

    def edges(k):
        tile = jnp.where(offset == k + 1, end_main, 0.0) + jnp.where(offset == k, end_spill, 0.0)
        tile = tile + jnp.where(offset == k - 1, start_main, 0.0)
        return tile + jnp.where(k == -1, end_left, jnp.where(k == 1, start_left, 0.0))

    own_out[local_ch] = edges(0)
    for k, out_ref in zip(ahead, out_refs):
        out_ref[local_ch] = edges(k).astype(BF16)


def hidden_kernel(routing, layer_ref, first_ref, second_ref, *rest):
    block_refs, (slab_ref, hidden_ref, first_out, second_out) = rest[: len(routing)], rest[len(routing) :][:4]
    rest = rest[len(routing) + 4 :]
    rows_refs, corner_refs, (wide_ref, small_ref) = rest[: len(rest) // 2 - 1], rest[len(rest) // 2 - 1 : -2], rest[-2:]
    images, channels, tile_w, block_rows = layer_ref.shape
    wide_ref[...] = layer_ref[...].astype(F32).reshape(wide_ref.shape)
    before = after = jnp.zeros((tile_w, block_rows), F32)
    for route, block_ref in zip(routing, block_refs):
        k = distance(route)
        tile = block_ref[block_ref.shape[0] - 1].astype(F32)
        before = jnp.where(k == 1, tile, before)
        after = jnp.where(k == -1, tile, after)
    small_ref[0] = before
    small_ref[1] = after
    before, after = before.T, after.T
    for x in range(tile_w):
        for n in range(images):
            rows = wide_ref[pl.ds(n * channels * tile_w + x, channels, stride=tile_w), :]
            part = slice(n * channels, (n + 1) * channels)
            for b in range(3):
                slab_ref[x, b * channels : (b + 1) * channels, n * block_rows : (n + 1) * block_rows] = tap(
                    rows, b, before[part, x : x + 1], after[part, x : x + 1]
                ).astype(BF16)
    weights = first_weights(first_ref)
    local_ch = channels // lax.axis_size("chan")
    for a, (w, v) in enumerate(zip(weights, second_weights(second_ref, lax.axis_index("chan"), local_ch))):
        first_out[a] = w
        second_out[a] = v
    for x in range(1, tile_w - 1):
        hidden_ref[x] = hidden_row(weights, [slab_ref[x + a - 1] for a in range(3)])
    for x, rows_ref, corner_ref in zip(border_rows(len(rows_refs), tile_w), rows_refs, corner_refs):
        rows_ref[...] = wide_ref[pl.ds(x, images * channels, stride=tile_w), :].astype(BF16)
        corner_ref[...] = stacked_lines([small_ref[j, pl.ds(x, 1), :] for j in range(2)], tile_w)


def border_rows(messages, tile_w):
    if messages == 1:
        return [jnp.where(lax.axis_index("col") == 0, tile_w - 1, 0)]
    return [tile_w - 1, 0]


def stacked_lines(lines, height):
    shape = (height, lines[0].shape[1])
    sub = lax.broadcasted_iota(jnp.int32, shape, 0)
    tile = jnp.zeros(shape, F32)
    for j, line in enumerate(lines):
        tile = jnp.where(sub == j, jnp.broadcast_to(line, shape), tile)
    return tile


def first_weights(weight_ref):
    return [jnp.concatenate([weight_ref[a, b] for b in range(3)], axis=1) for a in range(3)]


def hidden_row(weights, slabs):
    total = None
    for w, s in zip(weights, slabs):
        product = jnp.dot(w, s, preferred_element_type=F32)
        total = product if total is None else total + product
    return jnp.maximum(total, 0.0).astype(BF16)


def combine_kernel(arrivals, left_ref, own_ref, *rest):
    block_refs, rest = rest[:arrivals], rest[arrivals:]
    count = (len(rest) - 3) // 3
    rows_refs, corner_refs = rest[:count], rest[count : 2 * count]
    wide_ref, edge_ref = rest[2 * count : 2 * count + 2]
    sends, small_ref = rest[2 * count + 2 : -1], rest[-1]
    local_ch, tile_w, block_rows = left_ref.shape
    images = wide_ref.shape[0] // (local_ch * tile_w)
    rows = local_ch * tile_w
    shape = (rows, block_rows)
    lane = lax.broadcasted_iota(jnp.int32, (tile_w, block_rows), 1)
    left = left_ref[...]
    total = own_ref[...]
    for block_ref in block_refs:
        total = total + block_ref[...].astype(F32)
    right, edge = total[:local_ch].astype(BF16), total[local_ch]
    wide_ref[:rows] = left.astype(F32).reshape(shape)
    wide_ref[rows:] = right.astype(F32).reshape(shape)
    outside = lane < jnp.where(lax.axis_index("row") == 0, local_ch, 0)
    edge = jnp.where(outside, 0.0, edge)
    edge_ref[...] = edge
    small_ref[...] = edge
    all_in, all_grad = (rows_refs[0].shape[0], images * local_ch)
    for x, rows_ref, corner_ref, send_ref in zip(border_rows(count, tile_w), rows_refs, corner_refs, sends):
        send_ref[:all_in] = rows_ref[...]
        send_ref[all_in : all_in + all_grad] = wide_ref[pl.ds(x, all_grad, stride=tile_w), :].astype(BF16)
        lines = [corner_ref[0:1, :], corner_ref[1:2, :], small_ref[pl.ds(x, 1), :]]
        send_ref[all_in + all_grad :] = stacked_lines(lines, send_ref.shape[0] - all_in - all_grad).astype(BF16)


def second_weights(weight_ref, chan, local_ch):
    first = pl.multiple_of(chan * local_ch, local_ch)
    result = []
    for a in range(3):
        parts = []
        for b in range(3):
            w = weight_ref[2 - a, 2 - b, pl.ds(first, local_ch), :].astype(F32)
            half = w.shape[1] // 2
            parts.append(jnp.where(chan == 0, w, jnp.concatenate([w[:, half:], w[:, :half]], axis=1)))
        result.append(jnp.concatenate(parts, axis=0).T.astype(BF16))
    return result


def edge_columns(edge, local_ch, n):
    at = (2, 3) if n == 0 else (0, 1)
    return tuple(edge[k * local_ch : (k + 1) * local_ch] for k in at)


def inner_kernel(wide_ref, edge_ref, hidden_ref, weight_ref, slab_ref, mine_ref, other_ref, second_ref, grad_ref):
    images, local_ch, tile_w, block_rows = grad_ref.shape
    grad_ref[...] = wide_ref[...].reshape(grad_ref.shape).astype(BF16)
    edge = edge_ref[...].T
    for x in range(tile_w):
        for n in range(images):
            rows = wide_ref[pl.ds(n * local_ch * tile_w + x, local_ch, stride=tile_w), :]
            before, after = edge_columns(edge, local_ch, n)
            for b in range(3):
                slab_ref[x, b * local_ch : (b + 1) * local_ch, n * block_rows : (n + 1) * block_rows] = tap(
                    rows, b, before[:, x : x + 1], after[:, x : x + 1]
                ).astype(BF16)
    weights = [weight_ref[a] for a in range(3)]
    sums = [None] * 3
    for x in range(1, tile_w - 1):
        total = None
        for a in range(3):
            slab = slab_ref[x + a - 1]
            total = added(total, jnp.dot(weights[a], slab, preferred_element_type=F32))
            sums[a] = added(sums[a], nt(slab, hidden_ref[x]))
        mine_ref[x - 1] = total[:local_ch]
        other_ref[x - 1] = total[local_ch:].astype(BF16)
    for a in range(3):
        second_ref[a] = sums[a]


def added(total, product):
    return product if total is None else total + product


def inner_first_kernel(mine_ref, arrived_ref, hidden_ref, layer_slab, out_ref):
    rows, local_ch, _ = mine_ref.shape
    first = pl.multiple_of(lax.axis_index("chan") * local_ch, local_ch)
    sums = [None] * 3
    for x in range(1, rows + 1):
        grad = masked(mine_ref[x - 1], arrived_ref[x - 1], hidden_ref[x, pl.ds(first, local_ch), :])
        for a in range(3):
            sums[a] = added(sums[a], nt(grad, layer_slab[x + a - 1]))
    for a in range(3):
        out_ref[a] = sums[a]


def masked(mine, arrived, hidden):
    return jnp.where(hidden.astype(F32) > 0, mine + arrived.astype(F32), 0.0).astype(BF16)


def halo_at(own, halo, p):
    return halo[0] if p < 0 else halo[1] if p >= own.shape[0] else own[p]


def outer_kernel(before_ref, after_ref, layer_slab, grad_slab, w_first_ref, w_second_ref,
                 layer_edge, grad_edge, hidden_edge, mine_ref, other_ref):
    tile_w, triple, lanes = layer_slab.shape
    channels = triple // 3
    local_ch = grad_slab.shape[1] // 3
    images = 2
    block_rows = lanes // images
    all_in, all_grad = (images * channels, images * local_ch)
    col = lax.axis_index("col")
    present = (col > 0, col < lax.axis_size("col") - 1)
    for side, (ref, ok) in enumerate(zip((before_ref, after_ref), present)):
        block = jnp.where(ok, ref[...].astype(F32), 0.0)
        corners = block[all_in + all_grad : all_in + all_grad + 8].T
        edge = corners[:, 2:3]
        for n in range(images):
            lanes_here = slice(n * block_rows, (n + 1) * block_rows)
            part = slice(n * channels, (n + 1) * channels)
            rows = block[all_in + n * local_ch : all_in + (n + 1) * local_ch]
            before, after = edge_columns(edge, local_ch, n)
            for b in range(3):
                layer_edge[side, b * channels : (b + 1) * channels, lanes_here] = tap(
                    block[part], b, corners[part, 0:1], corners[part, 1:2]
                ).astype(BF16)
                grad_edge[side, b * local_ch : (b + 1) * local_ch, lanes_here] = tap(
                    rows, b, before, after
                ).astype(BF16)
    first = [w_first_ref[a] for a in range(3)]
    second = [w_second_ref[a] for a in range(3)]
    for side, x in enumerate((0, tile_w - 1)):
        hidden_edge[side] = hidden_row(first, [halo_at(layer_slab, layer_edge, x + a - 1) for a in range(3)])
        total = None
        for a in range(3):
            slab = halo_at(grad_slab, grad_edge, x + a - 1)
            total = added(total, jnp.dot(second[a], slab, preferred_element_type=F32))
        mine_ref[side] = total[:local_ch]
        other_ref[side] = total[local_ch:].astype(BF16)


def second_kernel(inner_ref, grad_slab, grad_edge, hidden_edge, out_ref):
    tile_w = grad_slab.shape[0]
    for a in range(3):
        total = inner_ref[a]
        for side, x in enumerate((0, tile_w - 1)):
            total = total + nt(halo_at(grad_slab, grad_edge, x + a - 1), hidden_edge[side])
        out_ref[a] = total


def last_kernel(mine_ref, arrived_ref, hidden_edge, layer_slab, layer_edge, inner_ref, second_ref, out_ref):
    tile_w = layer_slab.shape[0]
    local_ch = mine_ref.shape[1]
    channels = layer_slab.shape[1] // 3
    first = pl.multiple_of(lax.axis_index("chan") * local_ch, local_ch)
    sums = [inner_ref[a] for a in range(3)]
    for side, x in enumerate((0, tile_w - 1)):
        grad = masked(mine_ref[side], arrived_ref[side], hidden_edge[side, pl.ds(first, local_ch), :])
        for a in range(3):
            sums[a] = sums[a] + nt(grad, halo_at(layer_slab, layer_edge, x + a - 1))
    for a in range(3):
        for b in range(3):
            one = sums[a][:, b * channels : (b + 1) * channels]
            two = second_ref[2 - a, (2 - b) * local_ch : (3 - b) * local_ch, :]
            out_ref[3 * a + b] = jnp.concatenate([one, two], axis=1)


def finish_kernel(factor, own_ref, arrived_ref, first_ref, second_ref):
    local_ch = own_ref.shape[1]
    channels = first_ref.shape[3]
    chan = lax.axis_index("chan")
    for ref, at in ((own_ref, chan), (arrived_ref, 1 - chan)):
        here = pl.ds(pl.multiple_of(at * local_ch, local_ch), local_ch)
        for a in range(3):
            for b in range(3):
                block = ref[3 * a + b] * factor
                first_ref[a, b, here, :] = block[:, :channels]
                second_ref[a, b, here, :] = block[:, channels:]


def swapped(block, axis, step=1):
    return lax.ppermute(block, axis, [(i, i ^ step) for i in range(lax.axis_size(axis))])


def exchanged(partial, axis, *steps):
    rounded = lax.reduce_precision(partial, 8, 7)
    sent = rounded.astype(BF16)
    terms = [rounded] + [swapped(sent, axis, step).astype(F32) for step in steps]
    while len(terms) > 1:
        terms = [sum(terms[i : i + 2]) for i in range(0, len(terms), 2)]
    return terms[0]


def summed(partial):
    peers = lax.axis_size("row")
    step = 1
    while step < peers:
        if step * 2 < peers:
            partial = exchanged(partial, "row", step, 2 * step, 3 * step)
            step *= 4
        else:
            partial = exchanged(partial, "row", step)
            step *= 2
    peers = lax.axis_size("col")
    step = 1
    while step < peers:
        partial = exchanged(partial, "col", step)
        step *= 2
    return partial


def whole(layer_input, features, vol_target, offsets, w_first, w_second):
    images, channels, tile_w, block_rows = layer_input.shape
    local_ch = features.shape[1]
    groups = vol_target.shape[0]
    lanes = images * block_rows
    tile = (tile_w, block_rows)
    plain, framed = ((local_ch + k, *tile) for k in (0, 1))
    swap = lax.axis_size("col") == 2
    routing = routes()
    w_first = w_first.transpose(2, 3, 0, 1)
    w_second = w_second.transpose(2, 3, 0, 1)

    packed = call(
        functools.partial(pack_kernel, routing), [(framed, BF16)] * len(routing), layer_input, features, far=True,
        scratch=[pltpu.VMEM(layer_input.shape, BF16), pltpu.VMEM(plain, BF16),
                 pltpu.SemaphoreType.DMA((images + 1,))],
    )
    blocks = []
    for block, route in zip(packed, routing):
        blocks.append(delivered(block, route, 1))

    arrays = (vol_target, features, layer_input, w_first, w_second)
    vol_target, features, layer_input, w_first, w_second = call(
        fetch_kernel, [(array.shape, array.dtype) for array in arrays], *arrays, far=True,
        scratch=[pltpu.SemaphoreType.DMA((len(arrays),))],
    )

    size = local_ch // groups
    left_grad, own, *outgoing = call(
        functools.partial(correlation_kernel, routing),
        [(plain, BF16), (framed, F32)] + [(framed, BF16)] * len(routing),
        offsets, features, vol_target, *blocks, smem=1, flops=1 << 26,
        scratch=[pltpu.VMEM((DISP, size, *tile), F32), pltpu.VMEM((DISP, *tile), F32)],
    )
    arrivals = []
    for block, route in zip(outgoing, routing):
        arrivals.append(delivered(block, route, -1))

    messages = 1 if swap else 2
    slab_shape, hidden_shape = ((3 * channels, lanes), (channels, lanes))
    lines = (images * channels, block_rows)
    layer_slab, hidden, w_first, w_second, *border = call(
        functools.partial(hidden_kernel, routing),
        [((tile_w, *slab_shape), BF16), ((tile_w, *hidden_shape), BF16),
         ((3, channels, 3 * channels), BF16), ((3, channels, 3 * local_ch), BF16)]
        + [(lines, BF16)] * messages + [(tile, F32)] * messages,
        layer_input, w_first, w_second, *blocks, flops=1 << 28,
        scratch=[pltpu.VMEM((images * channels * tile_w, block_rows), F32), pltpu.VMEM((2, *tile), F32)],
    )
    message = ((images * (channels + local_ch) + 16, block_rows), BF16)
    wide, edge, *sends = call(
        functools.partial(combine_kernel, len(routing)),
        [((images * local_ch * tile_w, block_rows), F32), (tile, F32)] + [message] * messages,
        left_grad, own, *arrivals, *border,
        scratch=[pltpu.VMEM(tile, F32)],
    )
    if swap:
        before = after = swapped(sends[0], "col")
    else:
        before, after = (moved(sends[0], "col", 1), moved(sends[1], "col", -1))
    middle, rim = (tile_w - 2, local_ch, lanes), (2, local_ch, lanes)
    sums = (3, 3 * local_ch, channels)
    grad_slab, mine, other, second, grad_features = call(
        inner_kernel,
        [((tile_w, 3 * local_ch, lanes), BF16), (middle, F32), (middle, BF16), (sums, F32),
         ((images, *plain), BF16)],
        wide, edge, hidden, w_second, flops=1 << 28,
    )
    arrived = swapped(other, "chan")
    inner_first, = call(
        inner_first_kernel, [((3, local_ch, 3 * channels), F32)],
        mine, arrived, hidden, layer_slab, flops=1 << 28,
    )
    layer_edge, grad_edge, hidden_edge, mine, other = call(
        outer_kernel,
        [((2, *slab_shape), BF16), ((2, 3 * local_ch, lanes), BF16), ((2, *hidden_shape), BF16),
         (rim, F32), (rim, BF16)],
        before, after, layer_slab, grad_slab, w_first, w_second, flops=1 << 27,
    )
    arrived = swapped(other, "chan")
    second, = call(second_kernel, [(sums, F32)], second, grad_slab, grad_edge, hidden_edge, flops=1 << 27)
    partial, = call(
        last_kernel, [((9, local_ch, 2 * channels), F32)],
        mine, arrived, hidden_edge, layer_slab, layer_edge, inner_first, second, flops=1 << 27,
    )
    total = summed(partial)
    factor = 1.0 / math.sqrt(
        2.0 * tile_w * lax.axis_size("col") * block_rows * lax.axis_size("row")
    )
    first, second = call(
        functools.partial(finish_kernel, factor), [((3, 3, channels, channels), F32)] * 2,
        total, swapped(total, "chan"),
    )
    return (grad_features, first.transpose(2, 3, 0, 1), second.transpose(2, 3, 0, 1))


def solution(mesh):
    return jax.shard_map(
        whole,
        mesh=mesh,
        in_specs=(
            P(None, None, ("groups", "col"), "row"),
            P(None, "chan", ("groups", "col"), "row"),
            P("chan", None, ("groups", "col"), "row"),
            P("row", ("groups", "col")),
            P(),
            P(),
        ),
        out_specs=(
            P(None, "chan", ("groups", "col"), "row"),
            P("groups", None, None, None),
            P("groups", None, None, None),
        ),
        check_vma=False,
    )
```

time: 56 us -> 51.6 us (0.921)
  waiting for transfers between devices: 22.1 us -> 17.6 us
  blocking collectives: 2.02 us -> 0 us
  local copies, waits for them, and re-layouts: 2.96 us -> 4.64 us
  Pallas kernels: 8.43 us -> 9.77 us
  starting transfers between devices: 18.6 us -> 17.8 us
    ppermute x6 -> x0, starting transfers between devices: 15.4 us -> none  [moved(): return lax.ppermute(block, axis, route)]
    ppermute x5 -> x14, starting transfers between devices: 3.26 us -> 17.8 us  [swapped(): lax.ppermute(block, axis, [(i, i ^ step) for i in range(lax.axis_size(axi...]
    ppermute x6 -> x0, waiting for transfers between devices: 7.19 us -> none  [moved(): return lax.ppermute(block, axis, route)]
    ppermute x5 -> x14, waiting for transfers between devices: 14.9 us -> 17.6 us  [swapped(): lax.ppermute(block, axis, [(i, i ^ step) for i in range(lax.axis_size(axi...]
    unnamed x16 -> x14, local copies, waits for them, and re-layouts: 2.06 us -> 4.64 us
    all_gather x1 -> x0, blocking collectives: 2.02 us -> none  [body(): both = lax.all_gather(partial * factor, 'chan', axis=1, tiled=True)]
    pallas_call x7 -> x11, Pallas kernels: 8.43 us -> 9.77 us  [call(): pl.pallas_call(kernel, in_specs=[pl.BlockSpec(memory_space=pltpu.SMEM)] *...]
    slice x1 -> x0, local copies, waits for them, and re-layouts: 0.9 us -> none  [body(): return (grad_features, both[:, :channels], both[:, channels:])]
  transfers between devices with their start and end apart: 11 -> 14, of which waited for: 9 -> 10; matrix products, arithmetic and copies ran while one was open for 0% -> 0% of each run, Pallas kernels for 3% -> 6%
where the time goes in v3:
time: 51.6 us; the launch traced here: 51.4 us
  starting transfers between devices  17.8 us (34%)
  waiting for transfers between devices  17.6 us (34%)
  Pallas kernels  9.77 us (19%)
  local copies, waits for them, and re-layouts  4.64 us (9%)
  between operations  1.44 us (3%)
    ppermute x14, starting transfers between devices, swapped(): lax.ppermute(block, axis, [(i, i ^ step) for i in range(lax.axis_size(axi...  17.8 us
    ppermute x14, waiting for transfers between devices, swapped(): lax.ppermute(block, axis, [(i, i ^ step) for i in range(lax.axis_size(axi...  17.6 us
    pallas_call x11, Pallas kernels, call(): pl.pallas_call(kernel, in_specs=[pl.BlockSpec(memory_space=pltpu.SMEM)] *...  9.77 us
    unnamed x14, local copies, waits for them, and re-layouts  4.64 us
  transfers between devices with their start and end apart: 14, of which 10 were waited for; matrix products, arithmetic and copies ran while one was open for 0% of the time, Pallas kernels for 6%

profile of v3, /device:TPU:0, one launch (start us, length us, event | category | flops | bytes accessed | tf_op | source)
XLA Modules:
  0.0 51.4 jit_solution(3235685426691146247)
XLA Ops:
  0.6 0.9 %copy-done = bf16[2,64,8,128]{3,2,1,0:T(8,128)(2,1)S(1)} copy-done((bf16[2,64,8,128]{3,2,1,0:T(8,128)(2,1)S(1)}, bf16[2,64,8,128]{3,2,1,0:T(8,128)(2,1)}, u32[]{:S(2)}) %copy-start) | copy-done | bytes 262168
  1.6 0.9 %copy-done.2 = bf16[2,32,8,128]{3,2,1,0:T(8,128)(2,1)S(1)} copy-done((bf16[2,32,8,128]{3,2,1,0:T(8,128)(2,1)S(1)}, bf16[2,32,8,128]{3,2,1,0:T(8,128)(2,1)}, u32[]{:S(2)}) %copy-start.2) | copy-done | bytes 131096
  3.2 3.1 %collective-permute-start = (bf16[33,8,128]{2,1,0:T(8,128)(2,1)S(1)}, bf16[33,8,128]{2,1,0:T(8,128)(2,1)S(1)}, u32[]{:S(2)}, u32[]{:S(2)}) collective-permute-start(bf16[33,8,128]{2,1,0:T(8,128)(2,1)S(1)} %get-tuple-element.39), channel_id=1, source_target_pairs={{0,4},{4,0},{8,12},{12,8},{1,5},{5,1},{9,13},{13,9},{2,6},{6,2},{1... | collective-permute-start | bytes 202760 | tf_op jit(solution)/shard_map/ppermute | solution.py:443
  6.3 2.6 %collective-permute-start.1 = (bf16[33,8,128]{2,1,0:T(8,128)(2,1)S(1)}, bf16[33,8,128]{2,1,0:T(8,128)(2,1)S(1)}, u32[]{:S(2)}, u32[]{:S(2)}) collective-permute-start(bf16[33,8,128]{2,1,0:T(8,128)(2,1)S(1)} %get-tuple-element.40), channel_id=1, source_target_pairs={{0,8},{4,12},{8,0},{12,4},{1,9},{5,13},{9,1},{13,5},{2,10},{6,14},... | collective-permute-start | bytes 202760 | tf_op jit(solution)/shard_map/ppermute | solution.py:443
  9.6 1.0 %copy-done.4 = bf16[4,40,8,128]{3,2,1,0:T(8,128)(2,1)S(1)} copy-done((bf16[4,40,8,128]{3,2,1,0:T(8,128)(2,1)S(1)}, bf16[4,40,8,128]{3,2,1,0:T(8,128)(2,1)}, u32[]{:S(2)}) %copy-start.4) | copy-done | bytes 327704
  10.5 0.9 %copy-done.5 = bf16[64,64,3,3]{1,0,3,2:T(8,128)(2,1)S(1)} copy-done((bf16[64,64,3,3]{1,0,3,2:T(8,128)(2,1)S(1)}, bf16[64,64,3,3]{1,0,3,2:T(8,128)(2,1)}, u32[]{:S(2)}) %copy-start.5) | copy-done | bytes 73752
  11.4 0.9 %copy-done.6 = bf16[64,64,3,3]{1,0,3,2:T(8,128)(2,1)S(1)} copy-done((bf16[64,64,3,3]{1,0,3,2:T(8,128)(2,1)S(1)}, bf16[64,64,3,3]{1,0,3,2:T(8,128)(2,1)}, u32[]{:S(2)}) %copy-start.6) | copy-done | bytes 73752
  13.7 1.4 %collective-permute-done.2.rest_2_ = bf16[33,8,128]{2,1,0:T(8,128)(2,1)S(1)} collective-permute-done((bf16[33,8,128]{2,1,0:T(8,128)(2,1)S(1)}, bf16[33,8,128]{2,1,0:T(8,128)(2,1)S(1)}, u32[]{:S(2)}, u32[]{:S(2)}) %collective-permute-start.2) | collective-permute-done | bytes 67616 | tf_op jit(solution)/shard_map/ppermute | solution.py:443
  15.0 3.6 %shard_map.87 = (bf16[32,8,128]{2,1,0:T(8,128)(2,1)S(1)}, f32[33,8,128]{2,1,0:T(8,128)S(1)}, bf16[33,8,128]{2,1,0:T(8,128)(2,1)S(1)}, bf16[33,8,128]{2,1,0:T(8,128)(2,1)S(1)}, bf16[33,8,128]{2,1,0:T(8,128)(2,1)S(1)}) custom-call(s32[1,1]{1,0:T(1,128)S(6)} %copy.9.offset_ref, bf16[2,32,8,128]{3,2,1,0:T(8,128)(2,1)S(1)} %get-tuple-element.37.features_ref, ...), custom_call_target="tpu_custom_call" | custom-call | flops 67108864 | bytes 1048576 | tf_op jit(solution)/shard_map/pallas_call | solution.py:22
  19.4 1.8 %collective-permute-start.4 = (bf16[33,8,128]{2,1,0:T(8,128)(2,1)S(1)}, bf16[33,8,128]{2,1,0:T(8,128)(2,1)S(1)}, u32[]{:S(2)}, u32[]{:S(2)}) collective-permute-start(bf16[33,8,128]{2,1,0:T(8,128)(2,1)S(1)} %get-tuple-element.45), channel_id=1, source_target_pairs={{0,8},{4,12},{8,0},{12,4},{1,9},{5,13},{9,1},{13,5},{2,10},{6,14},... | collective-permute-start | bytes 202760 | tf_op jit(solution)/shard_map/ppermute | solution.py:443
  21.2 1.9 %collective-permute-start.5 = (bf16[33,8,128]{2,1,0:T(8,128)(2,1)S(1)}, bf16[33,8,128]{2,1,0:T(8,128)(2,1)S(1)}, u32[]{:S(2)}, u32[]{:S(2)}) collective-permute-start(bf16[33,8,128]{2,1,0:T(8,128)(2,1)S(1)} %get-tuple-element.46), channel_id=1, source_target_pairs={{0,12},{4,8},{8,4},{12,0},{1,13},{5,9},{9,5},{13,1},{2,14},{6,10},... | collective-permute-start | bytes 202760 | tf_op jit(solution)/shard_map/ppermute | solution.py:443
  24.0 2.0 %collective-permute-done.4.rest_1_ = bf16[33,8,128]{2,1,0:T(8,128)(2,1)S(1)} collective-permute-done((bf16[33,8,128]{2,1,0:T(8,128)(2,1)S(1)}, bf16[33,8,128]{2,1,0:T(8,128)(2,1)S(1)}, u32[]{:S(2)}, u32[]{:S(2)}) %collective-permute-start.4) | collective-permute-done | bytes 67616 | tf_op jit(solution)/shard_map/ppermute | solution.py:443
  26.0 1.4 %collective-permute-done.5.rest_2_ = bf16[33,8,128]{2,1,0:T(8,128)(2,1)S(1)} collective-permute-done((bf16[33,8,128]{2,1,0:T(8,128)(2,1)S(1)}, bf16[33,8,128]{2,1,0:T(8,128)(2,1)S(1)}, u32[]{:S(2)}, u32[]{:S(2)}) %collective-permute-start.5) | collective-permute-done | bytes 67616 | tf_op jit(solution)/shard_map/ppermute | solution.py:443
  27.4 1.3 %shard_map.90 = (bf16[8,96,256]{2,1,0:T(8,128)(2,1)S(1)}, f32[6,32,256]{2,1,0:T(8,128)S(1)}, bf16[6,32,256]{2,1,0:T(8,128)(2,1)S(1)}, f32[3,96,64]{2,1,0:T(8,128)S(1)}, bf16[2,32,8,128]{3,2,1,0:T(8,128)(2,1)}) custom-call(f32[512,128]{1,0:T(8,128)S(1)} %get-tuple-element.52.wide_ref, f32[8,128]{1,0:T(8,128)S(1)} %get-tuple-element.53.edge_ref, ...), custom_call_target="tpu_custom_call" | custom-call | flops 268435456 | bytes 1048576 | tf_op jit(solution)/shard_map/pallas_call | solution.py:22
  28.7 1.5 %collective-permute-start.6 = (bf16[208,128]{1,0:T(8,128)(2,1)S(1)}, bf16[208,128]{1,0:T(8,128)(2,1)S(1)}, u32[]{:S(2)}, u32[]{:S(2)}) collective-permute-start(bf16[208,128]{1,0:T(8,128)(2,1)S(1)} %get-tuple-element.57), channel_id=1, source_target_pairs={{0,2},{2,0},{1,3},{3,1},{4,6},{6,4},{5,7},{7,5},{8,10},{10,8},{9,1... | collective-permute-start | bytes 159752 | tf_op jit(solution)/shard_map/ppermute | solution.py:443
  30.2 2.8 %collective-permute-done.6.before_ref.after_ref = bf16[208,128]{1,0:T(8,128)(2,1)S(1)} collective-permute-done((bf16[208,128]{1,0:T(8,128)(2,1)S(1)}, bf16[208,128]{1,0:T(8,128)(2,1)S(1)}, u32[]{:S(2)}, u32[]{:S(2)}) %collective-permute-start.6) | collective-permute-done | bytes 53280 | tf_op jit(solution)/shard_map/ppermute | solution.py:443
  35.1 2.0 %collective-permute-start.11 = (bf16[9,32,128]{2,1,0:T(8,128)(2,1)S(1)}, bf16[9,32,128]{2,1,0:T(8,128)(2,1)S(1)}, u32[]{:S(2)}, u32[]{:S(2)}) collective-permute-start(bf16[9,32,128]{2,1,0:T(8,128)(2,1)S(1)} %reduce-precision_convert_fusion), channel_id=1, source_target_pairs={{0,12},{4,8},{8,4},{12,0},{1,13},{5,9},{9,5},{13,1},{2,14},{6,10},... | collective-permute-start | bytes 221192 | tf_op jit(solution)/shard_map/ppermute | solution.py:443
  37.3 2.3 %collective-permute-start.9 = (bf16[9,32,128]{2,1,0:T(8,128)(2,1)S(1)}, bf16[9,32,128]{2,1,0:T(8,128)(2,1)S(1)}, u32[]{:S(2)}, u32[]{:S(2)}) collective-permute-start(bf16[9,32,128]{2,1,0:T(8,128)(2,1)S(1)} %reduce-precision_convert_fusion), channel_id=1, source_target_pairs={{0,4},{4,0},{8,12},{12,8},{1,5},{5,1},{9,13},{13,9},{2,6},{6,2},{1... | collective-permute-start | bytes 221192 | tf_op jit(solution)/shard_map/ppermute | solution.py:443
  39.6 2.7 %collective-permute-done.11 = bf16[9,32,128]{2,1,0:T(8,128)(2,1)S(1)} collective-permute-done((bf16[9,32,128]{2,1,0:T(8,128)(2,1)S(1)}, bf16[9,32,128]{2,1,0:T(8,128)(2,1)S(1)}, u32[]{:S(2)}, u32[]{:S(2)}) %collective-permute-start.11) | collective-permute-done | bytes 73760 | tf_op jit(solution)/shard_map/ppermute | solution.py:443
  42.2 2.3 %collective-permute-done.10 = bf16[9,32,128]{2,1,0:T(8,128)(2,1)S(1)} collective-permute-done((bf16[9,32,128]{2,1,0:T(8,128)(2,1)S(1)}, bf16[9,32,128]{2,1,0:T(8,128)(2,1)S(1)}, u32[]{:S(2)}, u32[]{:S(2)}) %collective-permute-start.10) | collective-permute-done | bytes 73760 | tf_op jit(solution)/shard_map/ppermute | solution.py:443
  44.6 1.6 %collective-permute-start.12 = (bf16[9,32,128]{2,1,0:T(8,128)(2,1)S(1)}, bf16[9,32,128]{2,1,0:T(8,128)(2,1)S(1)}, u32[]{:S(2)}, u32[]{:S(2)}) collective-permute-start(bf16[9,32,128]{2,1,0:T(8,128)(2,1)S(1)} %fusion), channel_id=1, source_target_pairs={{0,2},{2,0},{1,3},{3,1},{4,6},{6,4},{5,7},{7,5},{8,10},{10,8},{9,1... | collective-permute-start | bytes 221192 | tf_op jit(solution)/shard_map/ppermute | solution.py:443
  46.1 2.9 %collective-permute-done.12 = bf16[9,32,128]{2,1,0:T(8,128)(2,1)S(1)} collective-permute-done((bf16[9,32,128]{2,1,0:T(8,128)(2,1)S(1)}, bf16[9,32,128]{2,1,0:T(8,128)(2,1)S(1)}, u32[]{:S(2)}, u32[]{:S(2)}) %collective-permute-start.12) | collective-permute-done | bytes 73760 | tf_op jit(solution)/shard_map/ppermute | solution.py:443
  49.1 1.4 %collective-permute-done.13.arrived_ref = f32[9,32,128]{2,1,0:T(8,128)S(1)} collective-permute-done((f32[9,32,128]{2,1,0:T(8,128)S(1)}, f32[9,32,128]{2,1,0:T(8,128)S(1)}, u32[]{:S(2)}, u32[]{:S(2)}) %collective-permute-start.13) | collective-permute-done | bytes 147488 | tf_op jit(solution)/shard_map/ppermute | solution.py:443
  50.5 0.9 %shard_map.95 = (f32[3,3,64,64]{3,2,1,0:T(8,128)}, f32[3,3,64,64]{3,2,1,0:T(8,128)}) custom-call(f32[9,32,128]{2,1,0:T(8,128)S(1)} %convert_add_fusion.own_ref, f32[9,32,128]{2,1,0:T(8,128)S(1)} %collective-permute-done.13.arrived_ref), custom_call_target="tpu_custom_call" | custom-call | flops 1048576 | bytes 1048576 | tf_op jit(solution)/shard_map/pallas_call | solution.py:22
  (32 shorter events, 6.1 us)
Async XLA Ops:
  0.6 1.0 %copy-start = (bf16[2,64,8,128]{3,2,1,0:T(8,128)(2,1)S(1)}, bf16[2,64,8,128]{3,2,1,0:T(8,128)(2,1)}, u32[]{:S(2)}) copy-start(bf16[2,64,8,128]{3,2,1,0:T(8,128)(2,1)} %layer_hbm.1) | copy-start | bytes 786436
  1.6 0.9 %copy-start.2 = (bf16[2,32,8,128]{3,2,1,0:T(8,128)(2,1)S(1)}, bf16[2,32,8,128]{3,2,1,0:T(8,128)(2,1)}, u32[]{:S(2)}) copy-start(bf16[2,32,8,128]{3,2,1,0:T(8,128)(2,1)} %features_hbm.1) | copy-start | bytes 393220
  2.5 7.0 %copy-start.1 = (bf16[2,64,8,128]{3,2,1,0:T(8,128)(2,1)S(1)}, bf16[2,64,8,128]{3,2,1,0:T(8,128)(2,1)}, u32[]{:S(2)}) copy-start(bf16[2,64,8,128]{3,2,1,0:T(8,128)(2,1)} %layer_hbm.1) | copy-start | bytes 786436
  2.5 7.0 %copy-start.3 = (bf16[2,32,8,128]{3,2,1,0:T(8,128)(2,1)S(1)}, bf16[2,32,8,128]{3,2,1,0:T(8,128)(2,1)}, u32[]{:S(2)}) copy-start(bf16[2,32,8,128]{3,2,1,0:T(8,128)(2,1)} %features_hbm.1) | copy-start | bytes 393220
  3.2 9.9 %collective-permute-start = (bf16[33,8,128]{2,1,0:T(8,128)(2,1)S(1)}, bf16[33,8,128]{2,1,0:T(8,128)(2,1)S(1)}, u32[]{:S(2)}, u32[]{:S(2)}) collective-permute-start(bf16[33,8,128]{2,1,0:T(8,128)(2,1)S(1)} %get-tuple-element.39), channel_id=1, source_target_pairs={{0,4},{4,0},{8,12},{12,8},{1,5},{5,1},{9,13},{13,9},{2,6},{6,2},{1... | collective-permute-start | bytes 202760 | tf_op jit(solution)/shard_map/ppermute | solution.py:443
  6.3 7.4 %collective-permute-start.1 = (bf16[33,8,128]{2,1,0:T(8,128)(2,1)S(1)}, bf16[33,8,128]{2,1,0:T(8,128)(2,1)S(1)}, u32[]{:S(2)}, u32[]{:S(2)}) collective-permute-start(bf16[33,8,128]{2,1,0:T(8,128)(2,1)S(1)} %get-tuple-element.40), channel_id=1, source_target_pairs={{0,8},{4,12},{8,0},{12,4},{1,9},{5,13},{9,1},{13,5},{2,10},{6,14},... | collective-permute-start | bytes 202760 | tf_op jit(solution)/shard_map/ppermute | solution.py:443
  8.9 6.2 %collective-permute-start.2 = (bf16[33,8,128]{2,1,0:T(8,128)(2,1)S(1)}, bf16[33,8,128]{2,1,0:T(8,128)(2,1)S(1)}, u32[]{:S(2)}, u32[]{:S(2)}) collective-permute-start(bf16[33,8,128]{2,1,0:T(8,128)(2,1)S(1)} %get-tuple-element.41), channel_id=1, source_target_pairs={{0,12},{4,8},{8,4},{12,0},{1,13},{5,9},{9,5},{13,1},{2,14},{6,10},... | collective-permute-start | bytes 202760 | tf_op jit(solution)/shard_map/ppermute | solution.py:443
  9.5 1.0 %copy-start.4 = (bf16[4,40,8,128]{3,2,1,0:T(8,128)(2,1)S(1)}, bf16[4,40,8,128]{3,2,1,0:T(8,128)(2,1)}, u32[]{:S(2)}) copy-start(bf16[4,40,8,128]{3,2,1,0:T(8,128)(2,1)} %refs_0_.1) | copy-start | bytes 983044
  10.5 0.9 %copy-start.5 = (bf16[64,64,3,3]{1,0,3,2:T(8,128)(2,1)S(1)}, bf16[64,64,3,3]{1,0,3,2:T(8,128)(2,1)}, u32[]{:S(2)}) copy-start(bf16[64,64,3,3]{1,0,3,2:T(8,128)(2,1)} %param.10) | copy-start | bytes 221188
  11.4 0.9 %copy-start.6 = (bf16[64,64,3,3]{1,0,3,2:T(8,128)(2,1)S(1)}, bf16[64,64,3,3]{1,0,3,2:T(8,128)(2,1)}, u32[]{:S(2)}) copy-start(bf16[64,64,3,3]{1,0,3,2:T(8,128)(2,1)} %param.11) | copy-start | bytes 221188
  18.7 5.3 %collective-permute-start.3 = (bf16[33,8,128]{2,1,0:T(8,128)(2,1)S(1)}, bf16[33,8,128]{2,1,0:T(8,128)(2,1)S(1)}, u32[]{:S(2)}, u32[]{:S(2)}) collective-permute-start(bf16[33,8,128]{2,1,0:T(8,128)(2,1)S(1)} %get-tuple-element.44), channel_id=1, source_target_pairs={{0,4},{4,0},{8,12},{12,8},{1,5},{5,1},{9,13},{13,9},{2,6},{6,2},{1... | collective-permute-start | bytes 202760 | tf_op jit(solution)/shard_map/ppermute | solution.py:443
  19.4 6.6 %collective-permute-start.4 = (bf16[33,8,128]{2,1,0:T(8,128)(2,1)S(1)}, bf16[33,8,128]{2,1,0:T(8,128)(2,1)S(1)}, u32[]{:S(2)}, u32[]{:S(2)}) collective-permute-start(bf16[33,8,128]{2,1,0:T(8,128)(2,1)S(1)} %get-tuple-element.45), channel_id=1, source_target_pairs={{0,8},{4,12},{8,0},{12,4},{1,9},{5,13},{9,1},{13,5},{2,10},{6,14},... | collective-permute-start | bytes 202760 | tf_op jit(solution)/shard_map/ppermute | solution.py:443
  21.2 6.2 %collective-permute-start.5 = (bf16[33,8,128]{2,1,0:T(8,128)(2,1)S(1)}, bf16[33,8,128]{2,1,0:T(8,128)(2,1)S(1)}, u32[]{:S(2)}, u32[]{:S(2)}) collective-permute-start(bf16[33,8,128]{2,1,0:T(8,128)(2,1)S(1)} %get-tuple-element.46), channel_id=1, source_target_pairs={{0,12},{4,8},{8,4},{12,0},{1,13},{5,9},{9,5},{13,1},{2,14},{6,10},... | collective-permute-start | bytes 202760 | tf_op jit(solution)/shard_map/ppermute | solution.py:443
  28.7 5.0 %collective-permute-start.8 = (bf16[6,32,256]{2,1,0:T(8,128)(2,1)S(1)}, bf16[6,32,256]{2,1,0:T(8,128)(2,1)S(1)}, u32[]{:S(2)}, u32[]{:S(2)}) collective-permute-start(bf16[6,32,256]{2,1,0:T(8,128)(2,1)S(1)} %get-tuple-element.66), channel_id=1, source_target_pairs={{0,1},{1,0},{2,3},{3,2},{4,5},{5,4},{6,7},{7,6},{8,9},{9,8},{10,11... | collective-permute-start | bytes 294920 | tf_op jit(solution)/shard_map/ppermute | solution.py:443
  28.7 4.2 %collective-permute-start.6 = (bf16[208,128]{1,0:T(8,128)(2,1)S(1)}, bf16[208,128]{1,0:T(8,128)(2,1)S(1)}, u32[]{:S(2)}, u32[]{:S(2)}) collective-permute-start(bf16[208,128]{1,0:T(8,128)(2,1)S(1)} %get-tuple-element.57), channel_id=1, source_target_pairs={{0,2},{2,0},{1,3},{3,1},{4,6},{6,4},{5,7},{7,5},{8,10},{10,8},{9,1... | collective-permute-start | bytes 159752 | tf_op jit(solution)/shard_map/ppermute | solution.py:443
  33.5 1.3 %collective-permute-start.7 = (bf16[2,32,256]{2,1,0:T(8,128)(2,1)S(1)}, bf16[2,32,256]{2,1,0:T(8,128)(2,1)S(1)}, u32[]{:S(2)}, u32[]{:S(2)}) collective-permute-start(bf16[2,32,256]{2,1,0:T(8,128)(2,1)S(1)} %get-tuple-element.62), channel_id=1, source_target_pairs={{0,1},{1,0},{2,3},{3,2},{4,5},{5,4},{6,7},{7,6},{8,9},{9,8},{10,11... | collective-permute-start | bytes 98312 | tf_op jit(solution)/shard_map/ppermute | solution.py:443
  35.1 7.1 %collective-permute-start.11 = (bf16[9,32,128]{2,1,0:T(8,128)(2,1)S(1)}, bf16[9,32,128]{2,1,0:T(8,128)(2,1)S(1)}, u32[]{:S(2)}, u32[]{:S(2)}) collective-permute-start(bf16[9,32,128]{2,1,0:T(8,128)(2,1)S(1)} %reduce-precision_convert_fusion), channel_id=1, source_target_pairs={{0,12},{4,8},{8,4},{12,0},{1,13},{5,9},{9,5},{13,1},{2,14},{6,10},... | collective-permute-start | bytes 221192 | tf_op jit(solution)/shard_map/ppermute | solution.py:443
  37.1 7.4 %collective-permute-start.10 = (bf16[9,32,128]{2,1,0:T(8,128)(2,1)S(1)}, bf16[9,32,128]{2,1,0:T(8,128)(2,1)S(1)}, u32[]{:S(2)}, u32[]{:S(2)}) collective-permute-start(bf16[9,32,128]{2,1,0:T(8,128)(2,1)S(1)} %reduce-precision_convert_fusion), channel_id=1, source_target_pairs={{0,8},{4,12},{8,0},{12,4},{1,9},{5,13},{9,1},{13,5},{2,10},{6,14},... | collective-permute-start | bytes 221192 | tf_op jit(solution)/shard_map/ppermute | solution.py:443
  37.3 7.2 %collective-permute-start.9 = (bf16[9,32,128]{2,1,0:T(8,128)(2,1)S(1)}, bf16[9,32,128]{2,1,0:T(8,128)(2,1)S(1)}, u32[]{:S(2)}, u32[]{:S(2)}) collective-permute-start(bf16[9,32,128]{2,1,0:T(8,128)(2,1)S(1)} %reduce-precision_convert_fusion), channel_id=1, source_target_pairs={{0,4},{4,0},{8,12},{12,8},{1,5},{5,1},{9,13},{13,9},{2,6},{6,2},{1... | collective-permute-start | bytes 221192 | tf_op jit(solution)/shard_map/ppermute | solution.py:443
  44.6 4.4 %collective-permute-start.12 = (bf16[9,32,128]{2,1,0:T(8,128)(2,1)S(1)}, bf16[9,32,128]{2,1,0:T(8,128)(2,1)S(1)}, u32[]{:S(2)}, u32[]{:S(2)}) collective-permute-start(bf16[9,32,128]{2,1,0:T(8,128)(2,1)S(1)} %fusion), channel_id=1, source_target_pairs={{0,2},{2,0},{1,3},{3,1},{4,6},{6,4},{5,7},{7,5},{8,10},{10,8},{9,1... | collective-permute-start | bytes 221192 | tf_op jit(solution)/shard_map/ppermute | solution.py:443
  49.1 1.4 %collective-permute-start.13 = (f32[9,32,128]{2,1,0:T(8,128)S(1)}, f32[9,32,128]{2,1,0:T(8,128)S(1)}, u32[]{:S(2)}, u32[]{:S(2)}) collective-permute-start(f32[9,32,128]{2,1,0:T(8,128)S(1)} %convert_add_fusion.own_ref), channel_id=1, source_target_pairs={{0,1},{1,0},{2,3},{3,2},{4,5},{5,4},{6,7},{7,6},{8,9},{9,8},{10,11... | collective-permute-start | bytes 442376 | tf_op jit(solution)/shard_map/ppermute | solution.py:443

commit v4 on v3

--- a/solution.py
+++ b/solution.py
@@ -81,17 +81,9 @@
         copy.wait()
 
 
-def pack_kernel(routing, layer_hbm, features_hbm, *rest):
-    out_refs, (layer_ref, features_ref, sems) = rest[:-3], rest[-3:]
+def pack_kernel(routing, layer_ref, features_ref, *out_refs):
     images, channels, tile_w, block_rows = layer_ref.shape
-    local_ch = features_ref.shape[0]
-    copies = [pltpu.make_async_copy(features_hbm.at[1], features_ref, sems.at[images])]
-    for n in range(images):
-        copies.append(pltpu.make_async_copy(layer_hbm.at[n], layer_ref.at[n], sems.at[n]))
-    for copy in copies:
-        copy.start()
-    for copy in copies:
-        copy.wait()
+    local_ch = features_ref.shape[1]
     shape = (tile_w, block_rows)
     lane = lax.broadcasted_iota(jnp.int32, shape, 1)
     first = jnp.zeros(shape, F32)
@@ -104,7 +96,7 @@
             last = jnp.where(here, jnp.broadcast_to(tile[:, block_rows - 1 :], shape), last)
     for route, out_ref in zip(routing, out_refs):
         ahead = distance(route) if route[0] == "line" else -distance(route)
-        out_ref[:local_ch] = features_ref[...]
+        out_ref[:local_ch] = features_ref[1]
         out_ref[local_ch] = jnp.where(ahead == 1, last, jnp.where(ahead == -1, first, 0.0)).astype(BF16)
 
 
@@ -312,9 +304,11 @@
     return tuple(edge[k * local_ch : (k + 1) * local_ch] for k in at)
 
 
-def inner_kernel(wide_ref, edge_ref, hidden_ref, weight_ref, slab_ref, mine_ref, other_ref, second_ref, grad_ref):
-    images, local_ch, tile_w, block_rows = grad_ref.shape
-    grad_ref[...] = wide_ref[...].reshape(grad_ref.shape).astype(BF16)
+def inner_kernel(wide_ref, edge_ref, hidden_ref, weight_ref, slab_ref, mine_ref, other_ref, second_ref):
+    tile_w, local_ch, lanes = slab_ref.shape
+    local_ch //= 3
+    block_rows = wide_ref.shape[1]
+    images = lanes // block_rows
     edge = edge_ref[...].T
     for x in range(tile_w):
         for n in range(images):
@@ -400,8 +394,9 @@
         other_ref[side] = total[local_ch:].astype(BF16)
 
 
-def second_kernel(inner_ref, grad_slab, grad_edge, hidden_edge, out_ref):
+def second_kernel(wide_ref, inner_ref, grad_slab, grad_edge, hidden_edge, grad_ref, out_ref):
     tile_w = grad_slab.shape[0]
+    grad_ref[...] = wide_ref[...].reshape(grad_ref.shape).astype(BF16)
     for a in range(3):
         total = inner_ref[a]
         for side, x in enumerate((0, tile_w - 1)):
@@ -482,19 +477,14 @@
     w_first = w_first.transpose(2, 3, 0, 1)
     w_second = w_second.transpose(2, 3, 0, 1)
 
-    packed = call(
-        functools.partial(pack_kernel, routing), [(framed, BF16)] * len(routing), layer_input, features, far=True,
-        scratch=[pltpu.VMEM(layer_input.shape, BF16), pltpu.VMEM(plain, BF16),
-                 pltpu.SemaphoreType.DMA((images + 1,))],
-    )
+    packed = call(functools.partial(pack_kernel, routing), [(framed, BF16)] * len(routing), layer_input, features)
     blocks = []
     for block, route in zip(packed, routing):
         blocks.append(delivered(block, route, 1))
 
-    arrays = (vol_target, features, layer_input, w_first, w_second)
-    vol_target, features, layer_input, w_first, w_second = call(
-        fetch_kernel, [(array.shape, array.dtype) for array in arrays], *arrays, far=True,
-        scratch=[pltpu.SemaphoreType.DMA((len(arrays),))],
+    vol_target, = call(
+        fetch_kernel, [(vol_target.shape, BF16)], vol_target, far=True,
+        scratch=[pltpu.SemaphoreType.DMA((1,))],
     )
 
     size = local_ch // groups
@@ -532,10 +522,9 @@
         before, after = (moved(sends[0], "col", 1), moved(sends[1], "col", -1))
     middle, rim = (tile_w - 2, local_ch, lanes), (2, local_ch, lanes)
     sums = (3, 3 * local_ch, channels)
-    grad_slab, mine, other, second, grad_features = call(
+    grad_slab, mine, other, second = call(
         inner_kernel,
-        [((tile_w, 3 * local_ch, lanes), BF16), (middle, F32), (middle, BF16), (sums, F32),
-         ((images, *plain), BF16)],
+        [((tile_w, 3 * local_ch, lanes), BF16), (middle, F32), (middle, BF16), (sums, F32)],
         wide, edge, hidden, w_second, flops=1 << 28,
     )
     arrived = swapped(other, "chan")
@@ -550,7 +539,10 @@
         before, after, layer_slab, grad_slab, w_first, w_second, flops=1 << 27,
     )
     arrived = swapped(other, "chan")
-    second, = call(second_kernel, [(sums, F32)], second, grad_slab, grad_edge, hidden_edge, flops=1 << 27)
+    grad_features, second = call(
+        second_kernel, [((images, *plain), BF16), (sums, F32)],
+        wide, second, grad_slab, grad_edge, hidden_edge, flops=1 << 27,
+    )
     partial, = call(
         last_kernel, [((9, local_ch, 2 * channels), F32)],
         mine, arrived, hidden_edge, layer_slab, layer_edge, inner_first, second, flops=1 << 27,

time: 51.6 us -> 51 us (0.988)
  waiting for transfers between devices: 17.6 us -> 20.7 us
  local copies, waits for them, and re-layouts: 4.64 us -> 1.87 us
  Pallas kernels: 9.77 us -> 8.72 us
    ppermute x14, waiting for transfers between devices: 17.6 us -> 20.7 us  [swapped(): lax.ppermute(block, axis, [(i, i ^ step) for i in range(lax.axis_size(axi...]
    unnamed x14 -> x12, local copies, waits for them, and re-layouts: 4.64 us -> 1.87 us
    pallas_call x11, Pallas kernels: 9.77 us -> 8.72 us  [call(): pl.pallas_call(kernel, in_specs=[pl.BlockSpec(memory_space=pltpu.SMEM)] *...]
  transfers between devices with their start and end apart: 14 -> 14, of which waited for: 10 -> 9; matrix products, arithmetic and copies ran while one was open for 0% -> 0% of each run, Pallas kernels for 6% -> 6%
where the time goes in v4:
time: 51 us; the launch traced here: 50.8 us
  waiting for transfers between devices  20.7 us (41%)
  starting transfers between devices  17.9 us (35%)
  Pallas kernels  8.72 us (17%)
  local copies, waits for them, and re-layouts  1.87 us (4%)
  between operations  1.45 us (3%)
    ppermute x14, waiting for transfers between devices, swapped(): lax.ppermute(block, axis, [(i, i ^ step) for i in range(lax.axis_size(axi...  20.7 us
    ppermute x14, starting transfers between devices, swapped(): lax.ppermute(block, axis, [(i, i ^ step) for i in range(lax.axis_size(axi...  17.9 us
    pallas_call x11, Pallas kernels, call(): pl.pallas_call(kernel, in_specs=[pl.BlockSpec(memory_space=pltpu.SMEM)] *...  8.72 us
    unnamed x12, local copies, waits for them, and re-layouts  1.87 us
  transfers between devices with their start and end apart: 14, of which 9 were waited for; matrix products, arithmetic and copies ran while one was open for 0% of the time, Pallas kernels for 6%

profile of v4, /device:TPU:0, one launch (start us, length us, event | category | flops | bytes accessed | tf_op | source)
XLA Modules:
  0.0 50.8 jit_solution(11259236283462534306)
XLA Ops:
  0.6 0.9 %copy-done = bf16[2,32,8,128]{3,2,1,0:T(8,128)(2,1)S(1)} copy-done((bf16[2,32,8,128]{3,2,1,0:T(8,128)(2,1)S(1)}, bf16[2,32,8,128]{3,2,1,0:T(8,128)(2,1)}, u32[]{:S(2)}) %copy-start) | copy-done | bytes 131096
  1.5 0.9 %copy-done.3 = bf16[2,64,8,128]{3,2,1,0:T(8,128)(2,1)S(1)} copy-done((bf16[2,64,8,128]{3,2,1,0:T(8,128)(2,1)S(1)}, bf16[2,64,8,128]{3,2,1,0:T(8,128)(2,1)}, u32[]{:S(2)}) %copy-start.3) | copy-done | bytes 262168
  2.7 3.1 %collective-permute-start = (bf16[33,8,128]{2,1,0:T(8,128)(2,1)S(1)}, bf16[33,8,128]{2,1,0:T(8,128)(2,1)S(1)}, u32[]{:S(2)}, u32[]{:S(2)}) collective-permute-start(bf16[33,8,128]{2,1,0:T(8,128)(2,1)S(1)} %get-tuple-element.33), channel_id=1, source_target_pairs={{0,4},{4,0},{8,12},{12,8},{1,5},{5,1},{9,13},{13,9},{2,6},{6,2},{1... | collective-permute-start | bytes 202760 | tf_op jit(solution)/shard_map/ppermute | solution.py:438
  5.8 2.6 %collective-permute-start.1 = (bf16[33,8,128]{2,1,0:T(8,128)(2,1)S(1)}, bf16[33,8,128]{2,1,0:T(8,128)(2,1)S(1)}, u32[]{:S(2)}, u32[]{:S(2)}) collective-permute-start(bf16[33,8,128]{2,1,0:T(8,128)(2,1)S(1)} %get-tuple-element.34), channel_id=1, source_target_pairs={{0,8},{4,12},{8,0},{12,4},{1,9},{5,13},{9,1},{13,5},{2,10},{6,14},... | collective-permute-start | bytes 202760 | tf_op jit(solution)/shard_map/ppermute | solution.py:438
  9.2 4.0 %collective-permute-done.1.rest_1_ = bf16[33,8,128]{2,1,0:T(8,128)(2,1)S(1)} collective-permute-done((bf16[33,8,128]{2,1,0:T(8,128)(2,1)S(1)}, bf16[33,8,128]{2,1,0:T(8,128)(2,1)S(1)}, u32[]{:S(2)}, u32[]{:S(2)}) %collective-permute-start.1) | collective-permute-done | bytes 67616 | tf_op jit(solution)/shard_map/ppermute | solution.py:438
  13.2 1.4 %collective-permute-done.2.rest_2_ = bf16[33,8,128]{2,1,0:T(8,128)(2,1)S(1)} collective-permute-done((bf16[33,8,128]{2,1,0:T(8,128)(2,1)S(1)}, bf16[33,8,128]{2,1,0:T(8,128)(2,1)S(1)}, u32[]{:S(2)}, u32[]{:S(2)}) %collective-permute-start.2) | collective-permute-done | bytes 67616 | tf_op jit(solution)/shard_map/ppermute | solution.py:438
  14.6 3.6 %shard_map.87 = (bf16[32,8,128]{2,1,0:T(8,128)(2,1)S(1)}, f32[33,8,128]{2,1,0:T(8,128)S(1)}, bf16[33,8,128]{2,1,0:T(8,128)(2,1)S(1)}, bf16[33,8,128]{2,1,0:T(8,128)(2,1)S(1)}, bf16[33,8,128]{2,1,0:T(8,128)(2,1)S(1)}) custom-call(s32[1,1]{1,0:T(1,128)S(6)} %copy.9.offset_ref, bf16[2,32,8,128]{3,2,1,0:T(8,128)(2,1)S(1)} %copy-done.1, ...), custom_call_target="tpu_custom_call" | custom-call | flops 67108864 | bytes 1048576 | tf_op jit(solution)/shard_map/pallas_call | solution.py:22
  18.9 1.8 %collective-permute-start.4 = (bf16[33,8,128]{2,1,0:T(8,128)(2,1)S(1)}, bf16[33,8,128]{2,1,0:T(8,128)(2,1)S(1)}, u32[]{:S(2)}, u32[]{:S(2)}) collective-permute-start(bf16[33,8,128]{2,1,0:T(8,128)(2,1)S(1)} %get-tuple-element.39), channel_id=1, source_target_pairs={{0,8},{4,12},{8,0},{12,4},{1,9},{5,13},{9,1},{13,5},{2,10},{6,14},... | collective-permute-start | bytes 202760 | tf_op jit(solution)/shard_map/ppermute | solution.py:438
  20.7 2.0 %collective-permute-start.5 = (bf16[33,8,128]{2,1,0:T(8,128)(2,1)S(1)}, bf16[33,8,128]{2,1,0:T(8,128)(2,1)S(1)}, u32[]{:S(2)}, u32[]{:S(2)}) collective-permute-start(bf16[33,8,128]{2,1,0:T(8,128)(2,1)S(1)} %get-tuple-element.40), channel_id=1, source_target_pairs={{0,12},{4,8},{8,4},{12,0},{1,13},{5,9},{9,5},{13,1},{2,14},{6,10},... | collective-permute-start | bytes 202760 | tf_op jit(solution)/shard_map/ppermute | solution.py:438
  22.7 0.9 %shard_map.88 = (bf16[8,192,256]{2,1,0:T(8,128)(2,1)S(1)}, bf16[8,64,256]{2,1,0:T(8,128)(2,1)S(1)}, bf16[3,64,192]{2,1,0:T(8,128)(2,1)S(1)}, bf16[3,64,96]{2,1,0...) custom-call(bf16[2,64,8,128]{3,2,1,0:T(8,128)(2,1)S(1)} %copy-done.3, ...), custom_call_target="tpu_custom_call" | custom-call | flops 268435456 | bytes 1048576 | tf_op jit(solution)/shard_map/pallas_call | solution.py:22
  23.5 1.7 %collective-permute-done.4.rest_1_ = bf16[33,8,128]{2,1,0:T(8,128)(2,1)S(1)} collective-permute-done((bf16[33,8,128]{2,1,0:T(8,128)(2,1)S(1)}, bf16[33,8,128]{2,1,0:T(8,128)(2,1)S(1)}, u32[]{:S(2)}, u32[]{:S(2)}) %collective-permute-start.4) | collective-permute-done | bytes 67616 | tf_op jit(solution)/shard_map/ppermute | solution.py:438
  25.2 1.5 %collective-permute-done.5.rest_2_ = bf16[33,8,128]{2,1,0:T(8,128)(2,1)S(1)} collective-permute-done((bf16[33,8,128]{2,1,0:T(8,128)(2,1)S(1)}, bf16[33,8,128]{2,1,0:T(8,128)(2,1)S(1)}, u32[]{:S(2)}, u32[]{:S(2)}) %collective-permute-start.5) | collective-permute-done | bytes 67616 | tf_op jit(solution)/shard_map/ppermute | solution.py:438
  26.8 0.7 %shard_map.90 = (bf16[8,96,256]{2,1,0:T(8,128)(2,1)S(1)}, f32[6,32,256]{2,1,0:T(8,128)S(1)}, bf16[6,32,256]{2,1,0:T(8,128)(2,1)S(1)}, f32[3,96,64]{2,1,0:T(8,128)S(1)}) custom-call(f32[512,128]{1,0:T(8,128)S(1)} %get-tuple-element.43.wide_ref, f32[8,128]{1,0:T(8,128)S(1)} %get-tuple-element.44.edge_ref, ...), custom_call_target="tpu_custom_call" | custom-call | flops 268435456 | bytes 1048576 | tf_op jit(solution)/shard_map/pallas_call | solution.py:22
  27.6 1.6 %collective-permute-start.6 = (bf16[208,128]{1,0:T(8,128)(2,1)S(1)}, bf16[208,128]{1,0:T(8,128)(2,1)S(1)}, u32[]{:S(2)}, u32[]{:S(2)}) collective-permute-start(bf16[208,128]{1,0:T(8,128)(2,1)S(1)} %get-tuple-element.49), channel_id=1, source_target_pairs={{0,2},{2,0},{1,3},{3,1},{4,6},{6,4},{5,7},{7,5},{8,10},{10,8},{9,1... | collective-permute-start | bytes 159752 | tf_op jit(solution)/shard_map/ppermute | solution.py:438
  29.2 2.7 %collective-permute-done.6.before_ref.after_ref = bf16[208,128]{1,0:T(8,128)(2,1)S(1)} collective-permute-done((bf16[208,128]{1,0:T(8,128)(2,1)S(1)}, bf16[208,128]{1,0:T(8,128)(2,1)S(1)}, u32[]{:S(2)}, u32[]{:S(2)}) %collective-permute-start.6) | collective-permute-done | bytes 53280 | tf_op jit(solution)/shard_map/ppermute | solution.py:438
  32.4 0.8 %shard_map.92 = (bf16[2,32,8,128]{3,2,1,0:T(8,128)(2,1)}, f32[3,96,64]{2,1,0:T(8,128)S(1)}) custom-call(f32[512,128]{1,0:T(8,128)S(1)} %get-tuple-element.43.wide_ref, f32[3,96,64]{2,1,0:T(8,128)S(1)} %get-tuple-element.47.inner_ref, bf16[8,96,256]{2,1,0:T(8,128)(2,1)S(1)} %get-tuple-element.48.grad_slab, ...), custom_call_target="tpu_custom_call" | custom-call | flops 134217728 | bytes 1048576 | tf_op jit(solution)/shard_map/pallas_call | solution.py:22
  34.3 2.2 %collective-permute-start.11 = (bf16[9,32,128]{2,1,0:T(8,128)(2,1)S(1)}, bf16[9,32,128]{2,1,0:T(8,128)(2,1)S(1)}, u32[]{:S(2)}, u32[]{:S(2)}) collective-permute-start(bf16[9,32,128]{2,1,0:T(8,128)(2,1)S(1)} %reduce-precision_convert_fusion), channel_id=1, source_target_pairs={{0,12},{4,8},{8,4},{12,0},{1,13},{5,9},{9,5},{13,1},{2,14},{6,10},... | collective-permute-start | bytes 221192 | tf_op jit(solution)/shard_map/ppermute | solution.py:438
  36.4 2.3 %collective-permute-start.9 = (bf16[9,32,128]{2,1,0:T(8,128)(2,1)S(1)}, bf16[9,32,128]{2,1,0:T(8,128)(2,1)S(1)}, u32[]{:S(2)}, u32[]{:S(2)}) collective-permute-start(bf16[9,32,128]{2,1,0:T(8,128)(2,1)S(1)} %reduce-precision_convert_fusion), channel_id=1, source_target_pairs={{0,4},{4,0},{8,12},{12,8},{1,5},{5,1},{9,13},{13,9},{2,6},{6,2},{1... | collective-permute-start | bytes 221192 | tf_op jit(solution)/shard_map/ppermute | solution.py:438
  38.7 2.6 %collective-permute-done.11 = bf16[9,32,128]{2,1,0:T(8,128)(2,1)S(1)} collective-permute-done((bf16[9,32,128]{2,1,0:T(8,128)(2,1)S(1)}, bf16[9,32,128]{2,1,0:T(8,128)(2,1)S(1)}, u32[]{:S(2)}, u32[]{:S(2)}) %collective-permute-start.11) | collective-permute-done | bytes 73760 | tf_op jit(solution)/shard_map/ppermute | solution.py:438
  41.4 2.6 %collective-permute-done.10 = bf16[9,32,128]{2,1,0:T(8,128)(2,1)S(1)} collective-permute-done((bf16[9,32,128]{2,1,0:T(8,128)(2,1)S(1)}, bf16[9,32,128]{2,1,0:T(8,128)(2,1)S(1)}, u32[]{:S(2)}, u32[]{:S(2)}) %collective-permute-start.10) | collective-permute-done | bytes 73760 | tf_op jit(solution)/shard_map/ppermute | solution.py:438
  44.0 1.6 %collective-permute-start.12 = (bf16[9,32,128]{2,1,0:T(8,128)(2,1)S(1)}, bf16[9,32,128]{2,1,0:T(8,128)(2,1)S(1)}, u32[]{:S(2)}, u32[]{:S(2)}) collective-permute-start(bf16[9,32,128]{2,1,0:T(8,128)(2,1)S(1)} %fusion), channel_id=1, source_target_pairs={{0,2},{2,0},{1,3},{3,1},{4,6},{6,4},{5,7},{7,5},{8,10},{10,8},{9,1... | collective-permute-start | bytes 221192 | tf_op jit(solution)/shard_map/ppermute | solution.py:438
  45.6 2.9 %collective-permute-done.12 = bf16[9,32,128]{2,1,0:T(8,128)(2,1)S(1)} collective-permute-done((bf16[9,32,128]{2,1,0:T(8,128)(2,1)S(1)}, bf16[9,32,128]{2,1,0:T(8,128)(2,1)S(1)}, u32[]{:S(2)}, u32[]{:S(2)}) %collective-permute-start.12) | collective-permute-done | bytes 73760 | tf_op jit(solution)/shard_map/ppermute | solution.py:438
  48.6 1.4 %collective-permute-done.13.arrived_ref = f32[9,32,128]{2,1,0:T(8,128)S(1)} collective-permute-done((f32[9,32,128]{2,1,0:T(8,128)S(1)}, f32[9,32,128]{2,1,0:T(8,128)S(1)}, u32[]{:S(2)}, u32[]{:S(2)}) %collective-permute-start.13) | collective-permute-done | bytes 147488 | tf_op jit(solution)/shard_map/ppermute | solution.py:438
  49.9 0.9 %shard_map.95 = (f32[3,3,64,64]{3,2,1,0:T(8,128)}, f32[3,3,64,64]{3,2,1,0:T(8,128)}) custom-call(f32[9,32,128]{2,1,0:T(8,128)S(1)} %convert_add_fusion.own_ref, f32[9,32,128]{2,1,0:T(8,128)S(1)} %collective-permute-done.13.arrived_ref), custom_call_target="tpu_custom_call" | custom-call | flops 1048576 | bytes 1048576 | tf_op jit(solution)/shard_map/pallas_call | solution.py:22
  (30 shorter events, 3.0 us)
Async XLA Ops:
  0.6 0.9 %copy-start = (bf16[2,32,8,128]{3,2,1,0:T(8,128)(2,1)S(1)}, bf16[2,32,8,128]{3,2,1,0:T(8,128)(2,1)}, u32[]{:S(2)}) copy-start(bf16[2,32,8,128]{3,2,1,0:T(8,128)(2,1)} %features_ref.3) | copy-start | bytes 393220
  1.5 0.9 %copy-start.3 = (bf16[2,64,8,128]{3,2,1,0:T(8,128)(2,1)S(1)}, bf16[2,64,8,128]{3,2,1,0:T(8,128)(2,1)}, u32[]{:S(2)}) copy-start(bf16[2,64,8,128]{3,2,1,0:T(8,128)(2,1)} %layer_ref.3) | copy-start | bytes 786436
  2.5 6.6 %copy-start.2 = (bf16[4,40,8,128]{3,2,1,0:T(8,128)(2,1)S(1)}, bf16[4,40,8,128]{3,2,1,0:T(8,128)(2,1)}, u32[]{:S(2)}) copy-start(bf16[4,40,8,128]{3,2,1,0:T(8,128)(2,1)} %refs_0_.1) | copy-start | bytes 983044
  2.7 6.5 %collective-permute-start = (bf16[33,8,128]{2,1,0:T(8,128)(2,1)S(1)}, bf16[33,8,128]{2,1,0:T(8,128)(2,1)S(1)}, u32[]{:S(2)}, u32[]{:S(2)}) collective-permute-start(bf16[33,8,128]{2,1,0:T(8,128)(2,1)S(1)} %get-tuple-element.33), channel_id=1, source_target_pairs={{0,4},{4,0},{8,12},{12,8},{1,5},{5,1},{9,13},{13,9},{2,6},{6,2},{1... | collective-permute-start | bytes 202760 | tf_op jit(solution)/shard_map/ppermute | solution.py:438
  5.8 7.4 %collective-permute-start.1 = (bf16[33,8,128]{2,1,0:T(8,128)(2,1)S(1)}, bf16[33,8,128]{2,1,0:T(8,128)(2,1)S(1)}, u32[]{:S(2)}, u32[]{:S(2)}) collective-permute-start(bf16[33,8,128]{2,1,0:T(8,128)(2,1)S(1)} %get-tuple-element.34), channel_id=1, source_target_pairs={{0,8},{4,12},{8,0},{12,4},{1,9},{5,13},{9,1},{13,5},{2,10},{6,14},... | collective-permute-start | bytes 202760 | tf_op jit(solution)/shard_map/ppermute | solution.py:438
  8.4 6.2 %collective-permute-start.2 = (bf16[33,8,128]{2,1,0:T(8,128)(2,1)S(1)}, bf16[33,8,128]{2,1,0:T(8,128)(2,1)S(1)}, u32[]{:S(2)}, u32[]{:S(2)}) collective-permute-start(bf16[33,8,128]{2,1,0:T(8,128)(2,1)S(1)} %get-tuple-element.35), channel_id=1, source_target_pairs={{0,12},{4,8},{8,4},{12,0},{1,13},{5,9},{9,5},{13,1},{2,14},{6,10},... | collective-permute-start | bytes 202760 | tf_op jit(solution)/shard_map/ppermute | solution.py:438
  9.1 5.5 %copy-start.1 = (bf16[2,32,8,128]{3,2,1,0:T(8,128)(2,1)S(1)}, bf16[2,32,8,128]{3,2,1,0:T(8,128)(2,1)}, u32[]{:S(2)}) copy-start(bf16[2,32,8,128]{3,2,1,0:T(8,128)(2,1)} %features_ref.3) | copy-start | bytes 393220
  9.2 13.5 %copy-start.4 = (bf16[64,64,3,3]{1,0,3,2:T(8,128)(2,1)S(1)}, bf16[64,64,3,3]{1,0,3,2:T(8,128)(2,1)}, u32[]{:S(2)}) copy-start(bf16[64,64,3,3]{1,0,3,2:T(8,128)(2,1)} %param.10) | copy-start | bytes 221188
  9.2 13.4 %copy-start.5 = (bf16[64,64,3,3]{1,0,3,2:T(8,128)(2,1)S(1)}, bf16[64,64,3,3]{1,0,3,2:T(8,128)(2,1)}, u32[]{:S(2)}) copy-start(bf16[64,64,3,3]{1,0,3,2:T(8,128)(2,1)} %param.11) | copy-start | bytes 221188
  18.2 5.3 %collective-permute-start.3 = (bf16[33,8,128]{2,1,0:T(8,128)(2,1)S(1)}, bf16[33,8,128]{2,1,0:T(8,128)(2,1)S(1)}, u32[]{:S(2)}, u32[]{:S(2)}) collective-permute-start(bf16[33,8,128]{2,1,0:T(8,128)(2,1)S(1)} %get-tuple-element.38), channel_id=1, source_target_pairs={{0,4},{4,0},{8,12},{12,8},{1,5},{5,1},{9,13},{13,9},{2,6},{6,2},{1... | collective-permute-start | bytes 202760 | tf_op jit(solution)/shard_map/ppermute | solution.py:438
  18.9 6.3 %collective-permute-start.4 = (bf16[33,8,128]{2,1,0:T(8,128)(2,1)S(1)}, bf16[33,8,128]{2,1,0:T(8,128)(2,1)S(1)}, u32[]{:S(2)}, u32[]{:S(2)}) collective-permute-start(bf16[33,8,128]{2,1,0:T(8,128)(2,1)S(1)} %get-tuple-element.39), channel_id=1, source_target_pairs={{0,8},{4,12},{8,0},{12,4},{1,9},{5,13},{9,1},{13,5},{2,10},{6,14},... | collective-permute-start | bytes 202760 | tf_op jit(solution)/shard_map/ppermute | solution.py:438
  20.7 6.1 %collective-permute-start.5 = (bf16[33,8,128]{2,1,0:T(8,128)(2,1)S(1)}, bf16[33,8,128]{2,1,0:T(8,128)(2,1)S(1)}, u32[]{:S(2)}, u32[]{:S(2)}) collective-permute-start(bf16[33,8,128]{2,1,0:T(8,128)(2,1)S(1)} %get-tuple-element.40), channel_id=1, source_target_pairs={{0,12},{4,8},{8,4},{12,0},{1,13},{5,9},{9,5},{13,1},{2,14},{6,10},... | collective-permute-start | bytes 202760 | tf_op jit(solution)/shard_map/ppermute | solution.py:438
  27.5 5.7 %collective-permute-start.8 = (bf16[6,32,256]{2,1,0:T(8,128)(2,1)S(1)}, bf16[6,32,256]{2,1,0:T(8,128)(2,1)S(1)}, u32[]{:S(2)}, u32[]{:S(2)}) collective-permute-start(bf16[6,32,256]{2,1,0:T(8,128)(2,1)S(1)} %get-tuple-element.59), channel_id=1, source_target_pairs={{0,1},{1,0},{2,3},{3,2},{4,5},{5,4},{6,7},{7,6},{8,9},{9,8},{10,11... | collective-permute-start | bytes 294920 | tf_op jit(solution)/shard_map/ppermute | solution.py:438
  27.6 4.2 %collective-permute-start.6 = (bf16[208,128]{1,0:T(8,128)(2,1)S(1)}, bf16[208,128]{1,0:T(8,128)(2,1)S(1)}, u32[]{:S(2)}, u32[]{:S(2)}) collective-permute-start(bf16[208,128]{1,0:T(8,128)(2,1)S(1)} %get-tuple-element.49), channel_id=1, source_target_pairs={{0,2},{2,0},{1,3},{3,1},{4,6},{6,4},{5,7},{7,5},{8,10},{10,8},{9,1... | collective-permute-start | bytes 159752 | tf_op jit(solution)/shard_map/ppermute | solution.py:438
  32.3 1.6 %collective-permute-start.7 = (bf16[2,32,256]{2,1,0:T(8,128)(2,1)S(1)}, bf16[2,32,256]{2,1,0:T(8,128)(2,1)S(1)}, u32[]{:S(2)}, u32[]{:S(2)}) collective-permute-start(bf16[2,32,256]{2,1,0:T(8,128)(2,1)S(1)} %get-tuple-element.56), channel_id=1, source_target_pairs={{0,1},{1,0},{2,3},{3,2},{4,5},{5,4},{6,7},{7,6},{8,9},{9,8},{10,11... | collective-permute-start | bytes 98312 | tf_op jit(solution)/shard_map/ppermute | solution.py:438
  34.3 7.1 %collective-permute-start.11 = (bf16[9,32,128]{2,1,0:T(8,128)(2,1)S(1)}, bf16[9,32,128]{2,1,0:T(8,128)(2,1)S(1)}, u32[]{:S(2)}, u32[]{:S(2)}) collective-permute-start(bf16[9,32,128]{2,1,0:T(8,128)(2,1)S(1)} %reduce-precision_convert_fusion), channel_id=1, source_target_pairs={{0,12},{4,8},{8,4},{12,0},{1,13},{5,9},{9,5},{13,1},{2,14},{6,10},... | collective-permute-start | bytes 221192 | tf_op jit(solution)/shard_map/ppermute | solution.py:438
  36.4 7.5 %collective-permute-start.10 = (bf16[9,32,128]{2,1,0:T(8,128)(2,1)S(1)}, bf16[9,32,128]{2,1,0:T(8,128)(2,1)S(1)}, u32[]{:S(2)}, u32[]{:S(2)}) collective-permute-start(bf16[9,32,128]{2,1,0:T(8,128)(2,1)S(1)} %reduce-precision_convert_fusion), channel_id=1, source_target_pairs={{0,8},{4,12},{8,0},{12,4},{1,9},{5,13},{9,1},{13,5},{2,10},{6,14},... | collective-permute-start | bytes 221192 | tf_op jit(solution)/shard_map/ppermute | solution.py:438
  36.4 7.5 %collective-permute-start.9 = (bf16[9,32,128]{2,1,0:T(8,128)(2,1)S(1)}, bf16[9,32,128]{2,1,0:T(8,128)(2,1)S(1)}, u32[]{:S(2)}, u32[]{:S(2)}) collective-permute-start(bf16[9,32,128]{2,1,0:T(8,128)(2,1)S(1)} %reduce-precision_convert_fusion), channel_id=1, source_target_pairs={{0,4},{4,0},{8,12},{12,8},{1,5},{5,1},{9,13},{13,9},{2,6},{6,2},{1... | collective-permute-start | bytes 221192 | tf_op jit(solution)/shard_map/ppermute | solution.py:438
  44.0 4.4 %collective-permute-start.12 = (bf16[9,32,128]{2,1,0:T(8,128)(2,1)S(1)}, bf16[9,32,128]{2,1,0:T(8,128)(2,1)S(1)}, u32[]{:S(2)}, u32[]{:S(2)}) collective-permute-start(bf16[9,32,128]{2,1,0:T(8,128)(2,1)S(1)} %fusion), channel_id=1, source_target_pairs={{0,2},{2,0},{1,3},{3,1},{4,6},{6,4},{5,7},{7,5},{8,10},{10,8},{9,1... | collective-permute-start | bytes 221192 | tf_op jit(solution)/shard_map/ppermute | solution.py:438
  48.5 1.4 %collective-permute-start.13 = (f32[9,32,128]{2,1,0:T(8,128)S(1)}, f32[9,32,128]{2,1,0:T(8,128)S(1)}, u32[]{:S(2)}, u32[]{:S(2)}) collective-permute-start(f32[9,32,128]{2,1,0:T(8,128)S(1)} %convert_add_fusion.own_ref), channel_id=1, source_target_pairs={{0,1},{1,0},{2,3},{3,2},{4,5},{5,4},{6,7},{7,6},{8,9},{9,8},{10,11... | collective-permute-start | bytes 442376 | tf_op jit(solution)/shard_map/ppermute | solution.py:438

commit v5 on v4

--- a/solution.py
+++ b/solution.py
@@ -16,9 +16,21 @@
 SPACE = 12 << 20
 
 
-def call(kernel, outs, *args, smem=0, far=False, scratch=(), flops=1 << 20):
+def call(kernel, outs, *args, smem=0, far=False, last=0, scratch=(), flops=1 << 20):
     whole = pl.BlockSpec(memory_space=pltpu.VMEM)
     given = pl.BlockSpec(memory_space=pltpu.HBM) if far else whole
+    if last:
+        away = pl.BlockSpec(memory_space=pltpu.HBM)
+        count = len(args) - len(outs) if last > 1 else len(args)
+        return pl.pallas_call(
+            kernel,
+            in_specs=[whole] * count + [away] * (len(args) - count),
+            out_specs=[away] * len(outs),
+            out_shape=[jax.ShapeDtypeStruct(s, t) for s, t in outs],
+            input_output_aliases={count + i: i for i in range(len(args) - count)},
+            scratch_shapes=list(scratch),
+            compiler_params=pltpu.CompilerParams(vmem_limit_bytes=SPACE),
+        )(*args)
     return pl.pallas_call(
         kernel,
         in_specs=[pl.BlockSpec(memory_space=pltpu.SMEM)] * smem + [given] * (len(args) - smem),
@@ -45,6 +57,13 @@
     return row - (row ^ value)
 
 
+def has_edges(route):
+    kind, value = route
+    if kind == "line":
+        return abs(value) == 1
+    return any(abs(i - (i ^ value)) == 1 for i in range(lax.axis_size("row")))
+
+
 def delivered(block, route, sign):
     kind, value = route
     if kind == "swap":
@@ -81,9 +100,9 @@
         copy.wait()
 
 
-def pack_kernel(routing, layer_ref, features_ref, *out_refs):
+def pack_kernel(routing, layer_ref, right_ref, *out_refs):
     images, channels, tile_w, block_rows = layer_ref.shape
-    local_ch = features_ref.shape[1]
+    local_ch = right_ref.shape[0]
     shape = (tile_w, block_rows)
     lane = lax.broadcasted_iota(jnp.int32, shape, 1)
     first = jnp.zeros(shape, F32)
@@ -96,7 +115,7 @@
             last = jnp.where(here, jnp.broadcast_to(tile[:, block_rows - 1 :], shape), last)
     for route, out_ref in zip(routing, out_refs):
         ahead = distance(route) if route[0] == "line" else -distance(route)
-        out_ref[:local_ch] = features_ref[1]
+        out_ref[:local_ch] = right_ref[...]
         out_ref[local_ch] = jnp.where(ahead == 1, last, jnp.where(ahead == -1, first, 0.0)).astype(BF16)
 
 
@@ -147,8 +166,8 @@
             while len(products) > 1:
                 products = [sum(products[i : i + 2]) for i in range(0, len(products), 2)]
             residual_ref[d] = products[0] - target_ref[g, d].astype(F32)
-        for first in range(0, size, 2):
-            channels = range(first, min(first + 2, size))
+        for first in range(0, size, 8):
+            channels = range(first, min(first + 8, size))
             left_grad = {c: zero for c in channels}
             whole_grad = {c: zero for c in channels}
             spill_grad = {c: zero for c in channels}
@@ -421,17 +440,24 @@
             out_ref[3 * a + b] = jnp.concatenate([one, two], axis=1)
 
 
-def finish_kernel(factor, own_ref, arrived_ref, first_ref, second_ref):
-    local_ch = own_ref.shape[1]
+def finish_kernel(factor, mine, sum_ref, *rest):
+    first_out, second_out, first_ref, second_ref, sems = rest[-5:]
+    local_ch = sum_ref.shape[1]
     channels = first_ref.shape[3]
     chan = lax.axis_index("chan")
-    for ref, at in ((own_ref, chan), (arrived_ref, 1 - chan)):
-        here = pl.ds(pl.multiple_of(at * local_ch, local_ch), local_ch)
-        for a in range(3):
-            for b in range(3):
-                block = ref[3 * a + b] * factor
-                first_ref[a, b, here, :] = block[:, :channels]
-                second_ref[a, b, here, :] = block[:, channels:]
+    here = pl.ds(pl.multiple_of((chan if mine else 1 - chan) * local_ch, local_ch), local_ch)
+    copies = []
+    for a in range(3):
+        for b in range(3):
+            block = sum_ref[3 * a + b] * factor
+            first_ref[a, b] = block[:, :channels]
+            second_ref[a, b] = block[:, channels:]
+        copies.append(pltpu.make_async_copy(first_ref.at[a], first_out.at[a, :, here, :], sems.at[0, a]))
+        copies.append(pltpu.make_async_copy(second_ref.at[a], second_out.at[a, :, here, :], sems.at[1, a]))
+        copies[-2].start()
+        copies[-1].start()
+    for copy in copies:
+        copy.wait()
 
 
 def swapped(block, axis, step=1):
@@ -441,13 +467,20 @@
 def exchanged(partial, axis, *steps):
     rounded = lax.reduce_precision(partial, 8, 7)
     sent = rounded.astype(BF16)
-    terms = [rounded] + [swapped(sent, axis, step).astype(F32) for step in steps]
+    terms = [rounded]
+    for step in steps:
+        terms.append(swapped(sent, axis, step).astype(F32))
     while len(terms) > 1:
         terms = [sum(terms[i : i + 2]) for i in range(0, len(terms), 2)]
     return terms[0]
 
 
 def summed(partial):
+    peers = lax.axis_size("col")
+    step = 1
+    while step < peers:
+        partial = exchanged(partial, "col", step)
+        step *= 2
     peers = lax.axis_size("row")
     step = 1
     while step < peers:
@@ -457,11 +490,6 @@
         else:
             partial = exchanged(partial, "row", step)
             step *= 2
-    peers = lax.axis_size("col")
-    step = 1
-    while step < peers:
-        partial = exchanged(partial, "col", step)
-        step *= 2
     return partial
 
 
@@ -477,10 +505,12 @@
     w_first = w_first.transpose(2, 3, 0, 1)
     w_second = w_second.transpose(2, 3, 0, 1)
 
-    packed = call(functools.partial(pack_kernel, routing), [(framed, BF16)] * len(routing), layer_input, features)
+    edged = [route for route in routing if has_edges(route)]
+    right = features[1]
+    packed = call(functools.partial(pack_kernel, edged), [(framed, BF16)] * len(edged), layer_input, right)
     blocks = []
-    for block, route in zip(packed, routing):
-        blocks.append(delivered(block, route, 1))
+    for route in routing:
+        blocks.append(delivered(packed[edged.index(route)] if route in edged else right, route, 1))
 
     vol_target, = call(
         fetch_kernel, [(vol_target.shape, BF16)], vol_target, far=True,
@@ -551,9 +581,12 @@
     factor = 1.0 / math.sqrt(
         2.0 * tile_w * lax.axis_size("col") * block_rows * lax.axis_size("row")
     )
+    others = swapped(total, "chan")
+    kernels = [((3, 3, channels, channels), F32)] * 2
+    room = [pltpu.VMEM((3, 3, local_ch, channels), F32)] * 2 + [pltpu.SemaphoreType.DMA((2, 3))]
+    halves = call(functools.partial(finish_kernel, factor, True), kernels, total, last=1, scratch=room)
     first, second = call(
-        functools.partial(finish_kernel, factor), [((3, 3, channels, channels), F32)] * 2,
-        total, swapped(total, "chan"),
+        functools.partial(finish_kernel, factor, False), kernels, others, *halves, last=2, scratch=room
     )
     return (grad_features, first.transpose(2, 3, 0, 1), second.transpose(2, 3, 0, 1))
 

time: 51 us -> 51.1 us (level)
    pallas_call x0 -> x2, Pallas kernels: none -> 1.63 us  [call(): pl.pallas_call(kernel, in_specs=[whole] * count + [away] * (len(args) - c...]
    pallas_call x11 -> x10, Pallas kernels: 8.72 us -> 7.26 us  [call(): pl.pallas_call(kernel, in_specs=[pl.BlockSpec(memory_space=pltpu.SMEM)] *...]
    squeeze x0 -> x1, local copies, waits for them, and re-layouts: none -> 0.89 us  [whole(): right = features[1]]
    unnamed x12, local copies, waits for them, and re-layouts: 1.87 us -> 0.98 us
  transfers between devices with their start and end apart: 14 -> 14, of which waited for: 9 -> 8; matrix products, arithmetic and copies ran while one was open for 0% -> 0% of each run, Pallas kernels for 6% -> 7%
where the time goes in v5:
time: 51.1 us; the launch traced here: 51 us
  waiting for transfers between devices  20.7 us (41%)
  starting transfers between devices  17.9 us (35%)
  Pallas kernels  8.89 us (17%)
  local copies, waits for them, and re-layouts  1.87 us (4%)
  between operations  1.46 us (3%)
    ppermute x14, waiting for transfers between devices, swapped(): lax.ppermute(block, axis, [(i, i ^ step) for i in range(lax.axis_size(axi...  20.7 us
    ppermute x14, starting transfers between devices, swapped(): lax.ppermute(block, axis, [(i, i ^ step) for i in range(lax.axis_size(axi...  17.9 us
    pallas_call x10, Pallas kernels, call(): pl.pallas_call(kernel, in_specs=[pl.BlockSpec(memory_space=pltpu.SMEM)] *...  7.26 us
    pallas_call x2, Pallas kernels, call(): pl.pallas_call(kernel, in_specs=[whole] * count + [away] * (len(args) - c...  1.63 us
  transfers between devices with their start and end apart: 14, of which 8 were waited for; matrix products, arithmetic and copies ran while one was open for 0% of the time, Pallas kernels for 7%

profile of v5, /device:TPU:0, one launch (start us, length us, event | category | flops | bytes accessed | tf_op | source)
XLA Modules:
  0.0 51.0 jit_solution(7755935905424234767)
XLA Ops:
  0.6 0.9 %slice_bitcast_fusion.right_ref = bf16[32,8,128]{2,1,0:T(8,128)(2,1)S(1)} fusion(bf16[2,32,8,128]{3,2,1,0:T(8,128)(2,1)} %features_ref.1), kind=kLoop, calls=%fused_computation.4 | loop fusion | bytes 131072 | tf_op jit(solution)/shard_map/squeeze | solution.py:509
  1.5 0.9 %copy-done.2 = bf16[2,64,8,128]{3,2,1,0:T(8,128)(2,1)S(1)} copy-done((bf16[2,64,8,128]{3,2,1,0:T(8,128)(2,1)S(1)}, bf16[2,64,8,128]{3,2,1,0:T(8,128)(2,1)}, u32[]{:S(2)}) %copy-start.2) | copy-done | bytes 262168
  2.7 3.1 %collective-permute-start = (bf16[33,8,128]{2,1,0:T(8,128)(2,1)S(1)}, bf16[33,8,128]{2,1,0:T(8,128)(2,1)S(1)}, u32[]{:S(2)}, u32[]{:S(2)}) collective-permute-start(bf16[33,8,128]{2,1,0:T(8,128)(2,1)S(1)} %get-tuple-element.34), channel_id=1, source_target_pairs={{0,4},{4,0},{8,12},{12,8},{1,5},{5,1},{9,13},{13,9},{2,6},{6,2},{1... | collective-permute-start | bytes 202760 | tf_op jit(solution)/shard_map/ppermute | solution.py:464
  5.8 2.5 %collective-permute-start.2 = (bf16[33,8,128]{2,1,0:T(8,128)(2,1)S(1)}, bf16[33,8,128]{2,1,0:T(8,128)(2,1)S(1)}, u32[]{:S(2)}, u32[]{:S(2)}) collective-permute-start(bf16[33,8,128]{2,1,0:T(8,128)(2,1)S(1)} %get-tuple-element.35), channel_id=1, source_target_pairs={{0,12},{4,8},{8,4},{12,0},{1,13},{5,9},{9,5},{13,1},{2,14},{6,10},... | collective-permute-start | bytes 202760 | tf_op jit(solution)/shard_map/ppermute | solution.py:464
  9.2 5.6 %collective-permute-done.1.rest_1_ = bf16[32,8,128]{2,1,0:T(8,128)(2,1)S(1)} collective-permute-done((bf16[32,8,128]{2,1,0:T(8,128)(2,1)S(1)}, bf16[32,8,128]{2,1,0:T(8,128)(2,1)S(1)}, u32[]{:S(2)}, u32[]{:S(2)}) %collective-permute-start.1) | collective-permute-done | bytes 65568 | tf_op jit(solution)/shard_map/ppermute | solution.py:464
  14.8 3.0 %shard_map.87 = (bf16[32,8,128]{2,1,0:T(8,128)(2,1)S(1)}, f32[33,8,128]{2,1,0:T(8,128)S(1)}, bf16[33,8,128]{2,1,0:T(8,128)(2,1)S(1)}, bf16[33,8,128]{2,1,0:T(8,128)(2,1)S(1)}, bf16[33,8,128]{2,1,0:T(8,128)(2,1)S(1)}) custom-call(s32[1,1]{1,0:T(1,128)S(6)} %copy.13.offset_ref, bf16[2,32,8,128]{3,2,1,0:T(8,128)(2,1)S(1)} %copy-done.1, ...), custom_call_target="tpu_custom_call" | custom-call | flops 67108864 | bytes 1048576 | tf_op jit(solution)/shard_map/pallas_call | solution.py:34
  17.9 3.0 %collective-permute-start.4 = (bf16[33,8,128]{2,1,0:T(8,128)(2,1)S(1)}, bf16[33,8,128]{2,1,0:T(8,128)(2,1)S(1)}, u32[]{:S(2)}, u32[]{:S(2)}) collective-permute-start(bf16[33,8,128]{2,1,0:T(8,128)(2,1)S(1)} %get-tuple-element.39), channel_id=1, source_target_pairs={{0,8},{4,12},{8,0},{12,4},{1,9},{5,13},{9,1},{13,5},{2,10},{6,14},... | collective-permute-start | bytes 202760 | tf_op jit(solution)/shard_map/ppermute | solution.py:464
  20.9 1.4 %collective-permute-start.5 = (bf16[33,8,128]{2,1,0:T(8,128)(2,1)S(1)}, bf16[33,8,128]{2,1,0:T(8,128)(2,1)S(1)}, u32[]{:S(2)}, u32[]{:S(2)}) collective-permute-start(bf16[33,8,128]{2,1,0:T(8,128)(2,1)S(1)} %get-tuple-element.40), channel_id=1, source_target_pairs={{0,12},{4,8},{8,4},{12,0},{1,13},{5,9},{9,5},{13,1},{2,14},{6,10},... | collective-permute-start | bytes 202760 | tf_op jit(solution)/shard_map/ppermute | solution.py:464
  22.3 0.9 %shard_map.88 = (bf16[8,192,256]{2,1,0:T(8,128)(2,1)S(1)}, bf16[8,64,256]{2,1,0:T(8,128)(2,1)S(1)}, bf16[3,64,192]{2,1,0:T(8,128)(2,1)S(1)}, bf16[3,64,96]{2,1,0...) custom-call(bf16[2,64,8,128]{3,2,1,0:T(8,128)(2,1)S(1)} %copy-done.3, ...), custom_call_target="tpu_custom_call" | custom-call | flops 268435456 | bytes 1048576 | tf_op jit(solution)/shard_map/pallas_call | solution.py:34
  23.2 2.6 %collective-permute-done.4.rest_1_ = bf16[33,8,128]{2,1,0:T(8,128)(2,1)S(1)} collective-permute-done((bf16[33,8,128]{2,1,0:T(8,128)(2,1)S(1)}, bf16[33,8,128]{2,1,0:T(8,128)(2,1)S(1)}, u32[]{:S(2)}, u32[]{:S(2)}) %collective-permute-start.4) | collective-permute-done | bytes 67616 | tf_op jit(solution)/shard_map/ppermute | solution.py:464
  25.7 1.3 %collective-permute-done.5.rest_2_ = bf16[33,8,128]{2,1,0:T(8,128)(2,1)S(1)} collective-permute-done((bf16[33,8,128]{2,1,0:T(8,128)(2,1)S(1)}, bf16[33,8,128]{2,1,0:T(8,128)(2,1)S(1)}, u32[]{:S(2)}, u32[]{:S(2)}) %collective-permute-start.5) | collective-permute-done | bytes 67616 | tf_op jit(solution)/shard_map/ppermute | solution.py:464
  27.1 0.7 %shard_map.90 = (bf16[8,96,256]{2,1,0:T(8,128)(2,1)S(1)}, f32[6,32,256]{2,1,0:T(8,128)S(1)}, bf16[6,32,256]{2,1,0:T(8,128)(2,1)S(1)}, f32[3,96,64]{2,1,0:T(8,128)S(1)}) custom-call(f32[512,128]{1,0:T(8,128)S(1)} %get-tuple-element.43.wide_ref, f32[8,128]{1,0:T(8,128)S(1)} %get-tuple-element.44.edge_ref, ...), custom_call_target="tpu_custom_call" | custom-call | flops 268435456 | bytes 1048576 | tf_op jit(solution)/shard_map/pallas_call | solution.py:34
  27.9 1.6 %collective-permute-start.6 = (bf16[208,128]{1,0:T(8,128)(2,1)S(1)}, bf16[208,128]{1,0:T(8,128)(2,1)S(1)}, u32[]{:S(2)}, u32[]{:S(2)}) collective-permute-start(bf16[208,128]{1,0:T(8,128)(2,1)S(1)} %get-tuple-element.49), channel_id=1, source_target_pairs={{0,2},{2,0},{1,3},{3,1},{4,6},{6,4},{5,7},{7,5},{8,10},{10,8},{9,1... | collective-permute-start | bytes 159752 | tf_op jit(solution)/shard_map/ppermute | solution.py:464
  29.5 2.7 %collective-permute-done.6.before_ref.after_ref = bf16[208,128]{1,0:T(8,128)(2,1)S(1)} collective-permute-done((bf16[208,128]{1,0:T(8,128)(2,1)S(1)}, bf16[208,128]{1,0:T(8,128)(2,1)S(1)}, u32[]{:S(2)}, u32[]{:S(2)}) %collective-permute-start.6) | collective-permute-done | bytes 53280 | tf_op jit(solution)/shard_map/ppermute | solution.py:464
  32.7 0.8 %shard_map.92 = (bf16[2,32,8,128]{3,2,1,0:T(8,128)(2,1)}, f32[3,96,64]{2,1,0:T(8,128)S(1)}) custom-call(f32[512,128]{1,0:T(8,128)S(1)} %get-tuple-element.43.wide_ref, f32[3,96,64]{2,1,0:T(8,128)S(1)} %get-tuple-element.47.inner_ref, bf16[8,96,256]{2,1,0:T(8,128)(2,1)S(1)} %get-tuple-element.48.grad_slab, ...), custom_call_target="tpu_custom_call" | custom-call | flops 134217728 | bytes 1048576 | tf_op jit(solution)/shard_map/pallas_call | solution.py:34
  34.6 1.6 %collective-permute-start.9 = (bf16[9,32,128]{2,1,0:T(8,128)(2,1)S(1)}, bf16[9,32,128]{2,1,0:T(8,128)(2,1)S(1)}, u32[]{:S(2)}, u32[]{:S(2)}) collective-permute-start(bf16[9,32,128]{2,1,0:T(8,128)(2,1)S(1)} %reduce-precision_convert_fusion), channel_id=1, source_target_pairs={{0,2},{2,0},{1,3},{3,1},{4,6},{6,4},{5,7},{7,5},{8,10},{10,8},{9,1... | collective-permute-start | bytes 221192 | tf_op jit(solution)/shard_map/ppermute | solution.py:464
  36.1 3.2 %collective-permute-done.9 = bf16[9,32,128]{2,1,0:T(8,128)(2,1)S(1)} collective-permute-done((bf16[9,32,128]{2,1,0:T(8,128)(2,1)S(1)}, bf16[9,32,128]{2,1,0:T(8,128)(2,1)S(1)}, u32[]{:S(2)}, u32[]{:S(2)}) %collective-permute-start.9) | collective-permute-done | bytes 73760 | tf_op jit(solution)/shard_map/ppermute | solution.py:464
  39.3 1.4 %collective-permute-start.12 = (bf16[9,32,128]{2,1,0:T(8,128)(2,1)S(1)}, bf16[9,32,128]{2,1,0:T(8,128)(2,1)S(1)}, u32[]{:S(2)}, u32[]{:S(2)}) collective-permute-start(bf16[9,32,128]{2,1,0:T(8,128)(2,1)S(1)} %fusion), channel_id=1, source_target_pairs={{0,12},{4,8},{8,4},{12,0},{1,13},{5,9},{9,5},{13,1},{2,14},{6,10},... | collective-permute-start | bytes 221192 | tf_op jit(solution)/shard_map/ppermute | solution.py:464
  40.7 0.8 %collective-permute-start.11 = (bf16[9,32,128]{2,1,0:T(8,128)(2,1)S(1)}, bf16[9,32,128]{2,1,0:T(8,128)(2,1)S(1)}, u32[]{:S(2)}, u32[]{:S(2)}) collective-permute-start(bf16[9,32,128]{2,1,0:T(8,128)(2,1)S(1)} %fusion), channel_id=1, source_target_pairs={{0,8},{4,12},{8,0},{12,4},{1,9},{5,13},{9,1},{13,5},{2,10},{6,14},... | collective-permute-start | bytes 221192 | tf_op jit(solution)/shard_map/ppermute | solution.py:464
  41.6 2.2 %collective-permute-start.10 = (bf16[9,32,128]{2,1,0:T(8,128)(2,1)S(1)}, bf16[9,32,128]{2,1,0:T(8,128)(2,1)S(1)}, u32[]{:S(2)}, u32[]{:S(2)}) collective-permute-start(bf16[9,32,128]{2,1,0:T(8,128)(2,1)S(1)} %fusion), channel_id=1, source_target_pairs={{0,4},{4,0},{8,12},{12,8},{1,5},{5,1},{9,13},{13,9},{2,6},{6,2},{1... | collective-permute-start | bytes 221192 | tf_op jit(solution)/shard_map/ppermute | solution.py:464
  43.8 2.6 %collective-permute-done.12 = bf16[9,32,128]{2,1,0:T(8,128)(2,1)S(1)} collective-permute-done((bf16[9,32,128]{2,1,0:T(8,128)(2,1)S(1)}, bf16[9,32,128]{2,1,0:T(8,128)(2,1)S(1)}, u32[]{:S(2)}, u32[]{:S(2)}) %collective-permute-start.12) | collective-permute-done | bytes 73760 | tf_op jit(solution)/shard_map/ppermute | solution.py:464
  46.3 2.3 %collective-permute-done.11 = bf16[9,32,128]{2,1,0:T(8,128)(2,1)S(1)} collective-permute-done((bf16[9,32,128]{2,1,0:T(8,128)(2,1)S(1)}, bf16[9,32,128]{2,1,0:T(8,128)(2,1)S(1)}, u32[]{:S(2)}, u32[]{:S(2)}) %collective-permute-start.11) | collective-permute-done | bytes 73760 | tf_op jit(solution)/shard_map/ppermute | solution.py:464
  48.8 0.8 %shard_map.95 = (f32[3,3,64,64]{3,2,1,0:T(8,128)}, f32[3,3,64,64]{3,2,1,0:T(8,128)}) custom-call(f32[9,32,128]{2,1,0:T(8,128)S(1)} %add_add_fusion.sum_ref), custom_call_target="tpu_custom_call" | custom-call | tf_op jit(solution)/shard_map/pallas_call | solution.py:25
  50.1 0.8 %shard_map.96 = (f32[3,3,64,64]{3,2,1,0:T(8,128)}, f32[3,3,64,64]{3,2,1,0:T(8,128)}) custom-call(f32[9,32,128]{2,1,0:T(8,128)S(1)} %collective-permute-done.13.sum_ref, f32[3,3,64,64]{3,2,1,0:T(8,128)} %get-tuple-element.61.rest_0_, f32[3,3,64,64]{3,2,1,0:T(8,128)} %get-tuple-element.62.rest_1_), custom_call_target="tpu_custom_call", output_to_operand_aliasing={{0}: (1, {}), {1}: (2, {})} | custom-call | tf_op jit(solution)/shard_map/pallas_call | solution.py:25
  (32 shorter events, 3.0 us)
Async XLA Ops:
  0.6 8.4 %copy-start = (bf16[4,40,8,128]{3,2,1,0:T(8,128)(2,1)S(1)}, bf16[4,40,8,128]{3,2,1,0:T(8,128)(2,1)}, u32[]{:S(2)}) copy-start(bf16[4,40,8,128]{3,2,1,0:T(8,128)(2,1)} %refs_0_.1) | copy-start | bytes 983044
  1.5 0.9 %copy-start.2 = (bf16[2,64,8,128]{3,2,1,0:T(8,128)(2,1)S(1)}, bf16[2,64,8,128]{3,2,1,0:T(8,128)(2,1)}, u32[]{:S(2)}) copy-start(bf16[2,64,8,128]{3,2,1,0:T(8,128)(2,1)} %layer_ref.3) | copy-start | bytes 786436
  2.7 12.1 %collective-permute-start = (bf16[33,8,128]{2,1,0:T(8,128)(2,1)S(1)}, bf16[33,8,128]{2,1,0:T(8,128)(2,1)S(1)}, u32[]{:S(2)}, u32[]{:S(2)}) collective-permute-start(bf16[33,8,128]{2,1,0:T(8,128)(2,1)S(1)} %get-tuple-element.34), channel_id=1, source_target_pairs={{0,4},{4,0},{8,12},{12,8},{1,5},{5,1},{9,13},{13,9},{2,6},{6,2},{1... | collective-permute-start | bytes 202760 | tf_op jit(solution)/shard_map/ppermute | solution.py:464
  5.8 9.0 %collective-permute-start.2 = (bf16[33,8,128]{2,1,0:T(8,128)(2,1)S(1)}, bf16[33,8,128]{2,1,0:T(8,128)(2,1)S(1)}, u32[]{:S(2)}, u32[]{:S(2)}) collective-permute-start(bf16[33,8,128]{2,1,0:T(8,128)(2,1)S(1)} %get-tuple-element.35), channel_id=1, source_target_pairs={{0,12},{4,8},{8,4},{12,0},{1,13},{5,9},{9,5},{13,1},{2,14},{6,10},... | collective-permute-start | bytes 202760 | tf_op jit(solution)/shard_map/ppermute | solution.py:464
  8.3 6.5 %collective-permute-start.1 = (bf16[32,8,128]{2,1,0:T(8,128)(2,1)S(1)}, bf16[32,8,128]{2,1,0:T(8,128)(2,1)S(1)}, u32[]{:S(2)}, u32[]{:S(2)}) collective-permute-start(bf16[32,8,128]{2,1,0:T(8,128)(2,1)S(1)} %slice_bitcast_fusion.right_ref), channel_id=1, source_target_pairs={{0,8},{4,12},{8,0},{12,4},{1,9},{5,13},{9,1},{13,5},{2,10},{6,14},... | collective-permute-start | bytes 196616 | tf_op jit(solution)/shard_map/ppermute | solution.py:464
  9.1 5.7 %copy-start.1 = (bf16[2,32,8,128]{3,2,1,0:T(8,128)(2,1)S(1)}, bf16[2,32,8,128]{3,2,1,0:T(8,128)(2,1)}, u32[]{:S(2)}) copy-start(bf16[2,32,8,128]{3,2,1,0:T(8,128)(2,1)} %features_ref.1) | copy-start | bytes 393220
  9.2 13.1 %copy-start.3 = (bf16[2,64,8,128]{3,2,1,0:T(8,128)(2,1)S(1)}, bf16[2,64,8,128]{3,2,1,0:T(8,128)(2,1)}, u32[]{:S(2)}) copy-start(bf16[2,64,8,128]{3,2,1,0:T(8,128)(2,1)} %layer_ref.3) | copy-start | bytes 786436
  9.2 13.1 %copy-start.4 = (bf16[64,64,3,3]{1,0,3,2:T(8,128)(2,1)S(1)}, bf16[64,64,3,3]{1,0,3,2:T(8,128)(2,1)}, u32[]{:S(2)}) copy-start(bf16[64,64,3,3]{1,0,3,2:T(8,128)(2,1)} %param.10) | copy-start | bytes 221188
  9.2 13.1 %copy-start.5 = (bf16[64,64,3,3]{1,0,3,2:T(8,128)(2,1)S(1)}, bf16[64,64,3,3]{1,0,3,2:T(8,128)(2,1)}, u32[]{:S(2)}) copy-start(bf16[64,64,3,3]{1,0,3,2:T(8,128)(2,1)} %param.11) | copy-start | bytes 221188
  17.8 5.3 %collective-permute-start.3 = (bf16[33,8,128]{2,1,0:T(8,128)(2,1)S(1)}, bf16[33,8,128]{2,1,0:T(8,128)(2,1)S(1)}, u32[]{:S(2)}, u32[]{:S(2)}) collective-permute-start(bf16[33,8,128]{2,1,0:T(8,128)(2,1)S(1)} %get-tuple-element.38), channel_id=1, source_target_pairs={{0,4},{4,0},{8,12},{12,8},{1,5},{5,1},{9,13},{13,9},{2,6},{6,2},{1... | collective-permute-start | bytes 202760 | tf_op jit(solution)/shard_map/ppermute | solution.py:464
  17.9 7.8 %collective-permute-start.4 = (bf16[33,8,128]{2,1,0:T(8,128)(2,1)S(1)}, bf16[33,8,128]{2,1,0:T(8,128)(2,1)S(1)}, u32[]{:S(2)}, u32[]{:S(2)}) collective-permute-start(bf16[33,8,128]{2,1,0:T(8,128)(2,1)S(1)} %get-tuple-element.39), channel_id=1, source_target_pairs={{0,8},{4,12},{8,0},{12,4},{1,9},{5,13},{9,1},{13,5},{2,10},{6,14},... | collective-permute-start | bytes 202760 | tf_op jit(solution)/shard_map/ppermute | solution.py:464
  20.9 6.2 %collective-permute-start.5 = (bf16[33,8,128]{2,1,0:T(8,128)(2,1)S(1)}, bf16[33,8,128]{2,1,0:T(8,128)(2,1)S(1)}, u32[]{:S(2)}, u32[]{:S(2)}) collective-permute-start(bf16[33,8,128]{2,1,0:T(8,128)(2,1)S(1)} %get-tuple-element.40), channel_id=1, source_target_pairs={{0,12},{4,8},{8,4},{12,0},{1,13},{5,9},{9,5},{13,1},{2,14},{6,10},... | collective-permute-start | bytes 202760 | tf_op jit(solution)/shard_map/ppermute | solution.py:464
  27.8 5.7 %collective-permute-start.8 = (bf16[6,32,256]{2,1,0:T(8,128)(2,1)S(1)}, bf16[6,32,256]{2,1,0:T(8,128)(2,1)S(1)}, u32[]{:S(2)}, u32[]{:S(2)}) collective-permute-start(bf16[6,32,256]{2,1,0:T(8,128)(2,1)S(1)} %get-tuple-element.59), channel_id=1, source_target_pairs={{0,1},{1,0},{2,3},{3,2},{4,5},{5,4},{6,7},{7,6},{8,9},{9,8},{10,11... | collective-permute-start | bytes 294920 | tf_op jit(solution)/shard_map/ppermute | solution.py:464
  27.9 4.2 %collective-permute-start.6 = (bf16[208,128]{1,0:T(8,128)(2,1)S(1)}, bf16[208,128]{1,0:T(8,128)(2,1)S(1)}, u32[]{:S(2)}, u32[]{:S(2)}) collective-permute-start(bf16[208,128]{1,0:T(8,128)(2,1)S(1)} %get-tuple-element.49), channel_id=1, source_target_pairs={{0,2},{2,0},{1,3},{3,1},{4,6},{6,4},{5,7},{7,5},{8,10},{10,8},{9,1... | collective-permute-start | bytes 159752 | tf_op jit(solution)/shard_map/ppermute | solution.py:464
  32.6 1.6 %collective-permute-start.7 = (bf16[2,32,256]{2,1,0:T(8,128)(2,1)S(1)}, bf16[2,32,256]{2,1,0:T(8,128)(2,1)S(1)}, u32[]{:S(2)}, u32[]{:S(2)}) collective-permute-start(bf16[2,32,256]{2,1,0:T(8,128)(2,1)S(1)} %get-tuple-element.56), channel_id=1, source_target_pairs={{0,1},{1,0},{2,3},{3,2},{4,5},{5,4},{6,7},{7,6},{8,9},{9,8},{10,11... | collective-permute-start | bytes 98312 | tf_op jit(solution)/shard_map/ppermute | solution.py:464
  34.6 4.7 %collective-permute-start.9 = (bf16[9,32,128]{2,1,0:T(8,128)(2,1)S(1)}, bf16[9,32,128]{2,1,0:T(8,128)(2,1)S(1)}, u32[]{:S(2)}, u32[]{:S(2)}) collective-permute-start(bf16[9,32,128]{2,1,0:T(8,128)(2,1)S(1)} %reduce-precision_convert_fusion), channel_id=1, source_target_pairs={{0,2},{2,0},{1,3},{3,1},{4,6},{6,4},{5,7},{7,5},{8,10},{10,8},{9,1... | collective-permute-start | bytes 221192 | tf_op jit(solution)/shard_map/ppermute | solution.py:464
  39.3 7.0 %collective-permute-start.12 = (bf16[9,32,128]{2,1,0:T(8,128)(2,1)S(1)}, bf16[9,32,128]{2,1,0:T(8,128)(2,1)S(1)}, u32[]{:S(2)}, u32[]{:S(2)}) collective-permute-start(bf16[9,32,128]{2,1,0:T(8,128)(2,1)S(1)} %fusion), channel_id=1, source_target_pairs={{0,12},{4,8},{8,4},{12,0},{1,13},{5,9},{9,5},{13,1},{2,14},{6,10},... | collective-permute-start | bytes 221192 | tf_op jit(solution)/shard_map/ppermute | solution.py:464
  40.7 7.9 %collective-permute-start.11 = (bf16[9,32,128]{2,1,0:T(8,128)(2,1)S(1)}, bf16[9,32,128]{2,1,0:T(8,128)(2,1)S(1)}, u32[]{:S(2)}, u32[]{:S(2)}) collective-permute-start(bf16[9,32,128]{2,1,0:T(8,128)(2,1)S(1)} %fusion), channel_id=1, source_target_pairs={{0,8},{4,12},{8,0},{12,4},{1,9},{5,13},{9,1},{13,5},{2,10},{6,14},... | collective-permute-start | bytes 221192 | tf_op jit(solution)/shard_map/ppermute | solution.py:464
  41.6 7.1 %collective-permute-start.10 = (bf16[9,32,128]{2,1,0:T(8,128)(2,1)S(1)}, bf16[9,32,128]{2,1,0:T(8,128)(2,1)S(1)}, u32[]{:S(2)}, u32[]{:S(2)}) collective-permute-start(bf16[9,32,128]{2,1,0:T(8,128)(2,1)S(1)} %fusion), channel_id=1, source_target_pairs={{0,4},{4,0},{8,12},{12,8},{1,5},{5,1},{9,13},{13,9},{2,6},{6,2},{1... | collective-permute-start | bytes 221192 | tf_op jit(solution)/shard_map/ppermute | solution.py:464
  48.7 1.4 %collective-permute-start.13 = (f32[9,32,128]{2,1,0:T(8,128)S(1)}, f32[9,32,128]{2,1,0:T(8,128)S(1)}, u32[]{:S(2)}, u32[]{:S(2)}) collective-permute-start(f32[9,32,128]{2,1,0:T(8,128)S(1)} %add_add_fusion.sum_ref), channel_id=1, source_target_pairs={{0,1},{1,0},{2,3},{3,2},{4,5},{5,4},{6,7},{7,6},{8,9},{9,8},{10,11... | collective-permute-start | bytes 442376 | tf_op jit(solution)/shard_map/ppermute | solution.py:464
